TPU v7x, 32 devices: a whole 2x2x4 slice. The times are simulated.
32 devices in a mesh: groups: 2 (over y), energy: 4 (over z), tile: 2 (over x), mode: 2 (over core).
Axes of the slice: x: 2, y: 2, z: 4, core: 2. Of those that a mesh axis runs over, the one named last changes fastest.
Arguments:
- object_field: float32 [2, 16, 256, 192], P(None, ('groups', 'energy', 'mode'), 'tile'), parts along dimension 1, may hold values from -6 to 6
- probe_field: float32 [2, 3, 16, 128, 128], P(None, None, ('groups', 'energy', 'mode')), parts along dimension 2, may hold values from -6 to 6
- modulus: bfloat16 [16, 16, 128, 128], P(('groups', 'energy', 'mode'), 'tile'), parts along dimension 0, may hold values from 0 to 2
- offsets: int32 [32, 2], P(('groups', 'tile')), parts along dimension 0, may hold values from 0 to 31
- spectra_basis: float32 [8, 8], replicated, may hold values from -2 to 2
- analysis: float32 [8, 8], replicated, may hold values from -2 to 2
- threshold: float32 [8], replicated, may hold values from 0.05 to 0.5
Outputs:
- object_out: float32 [2, 16, 256, 192], P(None, ('groups', 'energy', 'mode'), 'tile'), parts along dimension 1
- probe_out: float32 [2, 3, 16, 128, 128], P(None, None, ('groups', 'energy', 'mode')), parts along dimension 2
There are 2 independent parts, one for each index of `groups`. A program takes and returns all parts, laid end to end along the dimension named above; an argument that names none is the same for every part. Nothing has to cross between parts.
All inputs are finite; a program needn't handle non-finite values.
Results may differ from a plain program's by a relative error of at most 0.0033.
Values may be sent and summed in bfloat16 or wider, within the bound.
No kernel may reach another device: no remote copies, remote signals or barrier semaphores. Data moves between devices by JAX's collectives and lax.ppermute only.
A program may use at most 128 MiB of HBM per device.

v0:
```python
import functools
import math

import jax
import jax.numpy as jnp
import ml_dtypes
import numpy as np
from jax import lax
from jax.experimental import pallas as pl
from jax.experimental.pallas import tpu as pltpu
from jax.sharding import PartitionSpec as P

PCOLS = 2
STEP = 32
LANES = 128
PAD_ROWS = 16

VMEM = pl.BlockSpec(memory_space=pltpu.VMEM)
SMEM = pl.BlockSpec(memory_space=pltpu.SMEM)


def swap_pairs(size, distance):
    return [(i, i ^ distance) for i in range(size)]


def power_of_two(size):
    return size & (size - 1) == 0


def dft_tables(extent):
    counter = np.arange(extent)
    phases = -2.0 * math.pi / extent * (counter[:, None] * counter[None, :] % extent)
    cosine = np.cos(phases) / math.sqrt(extent)
    sine = np.sin(phases) / math.sqrt(extent)
    forward = np.block([[cosine, -sine], [sine, cosine]])
    backward = np.block([[cosine, sine], [-sine, cosine]])
    return (
        jnp.asarray(forward.astype(np.float32).astype(ml_dtypes.bfloat16)),
        jnp.asarray(backward.astype(np.float32).astype(ml_dtypes.bfloat16)),
    )


def corner(offsets_ref, q):
    row = STEP * (q // PCOLS) + offsets_ref[q, 0]
    col = STEP * (q % PCOLS) + offsets_ref[q, 1]
    return row, col


def spread(block, col):
    lane = lax.broadcasted_iota(jnp.int32, block.shape, 1)
    turned = pltpu.roll(block, col, 1)
    left = jnp.where(lane >= col, turned, 0.0)
    right = jnp.where(lane < col, turned, 0.0)
    return left, right


def round_kernel(offsets_ref, object_ref, message_ref):
    rows, cols = object_ref.shape[2:]
    positions = offsets_ref.shape[0]
    for part in range(2):
        message_ref[part, :rows] = object_ref[part, 0].astype(jnp.bfloat16)
    lane = lax.broadcasted_iota(jnp.int32, (PAD_ROWS, cols), 1)
    line = jnp.zeros((PAD_ROWS, cols), jnp.float32)
    for q in range(positions):
        for k in range(2):
            value = offsets_ref[q, k].astype(jnp.float32)
            line = jnp.where(lane == 2 * q + k, value, line)
    for part in range(2):
        message_ref[part, rows:] = line.astype(jnp.bfloat16)


def wave_kernel(
    offsets_ref,
    own_ref,
    below_ref,
    probe_ref,
    moduli_ref,
    forward_ref,
    backward_ref,
    upper_ref,
    lower_ref,
    share_ref,
    extended,
    total,
    window,
    stacked,
    batch,
    columns,
    probe_num,
    probe_den,
    *,
    tiles,
    group,
):
    extent = probe_ref.shape[-1]
    modes = probe_ref.shape[1]
    rows = own_ref.shape[1] - PAD_ROWS
    cols = own_ref.shape[2]
    positions = offsets_ref.shape[0]
    has_below = lax.axis_index("tile") < tiles - 1
    for part in range(2):
        own = own_ref[part, :rows].astype(jnp.float32)
        below = jnp.where(has_below, below_ref[part, :rows].astype(jnp.float32), 0.0)
        for side, first in enumerate(range(0, cols, LANES)):
            last = min(first + LANES, cols)
            extended[part, side, :rows, : last - first] = own[:, first:last]
            extended[part, side, rows:, : last - first] = below[:, first:last]
    total[...] = jnp.zeros_like(total)
    probe_num[...] = jnp.zeros_like(probe_num)
    probe_den[...] = jnp.zeros_like(probe_den)
    lane = lax.broadcasted_iota(jnp.int32, (extent, extent), 1)

    def step(block, carry):
        for member in range(group):
            q = block * group + member
            row, col = corner(offsets_ref, q)
            here = pl.ds(row, extent)
            for part in range(2):
                left = pltpu.roll(extended[part, 0, here], extent - col, 1)
                right = pltpu.roll(extended[part, 1, here], extent - col, 1)
                window[member, part] = jnp.where(lane < extent - col, left, right)
            object_real = window[member, 0]
            object_imag = window[member, 1]
            probe_den[...] += object_real * object_real + object_imag * object_imag
            for m in range(modes):
                w = member * modes + m
                probe_real = probe_ref[0, m, 0]
                probe_imag = probe_ref[1, m, 0]
                wave_real = probe_real * object_real - probe_imag * object_imag
                wave_imag = probe_real * object_imag + probe_imag * object_real
                stacked[w, :extent] = wave_real
                stacked[w, extent:] = wave_imag
                place = slice(w * extent, (w + 1) * extent)
                batch[:extent, place] = wave_real.astype(jnp.bfloat16)
                batch[extent:, place] = wave_imag.astype(jnp.bfloat16)
        halfway = jnp.dot(forward_ref[...], batch[...], preferred_element_type=jnp.float32)
        for w in range(group * modes):
            place = slice(w * extent, (w + 1) * extent)
            columns[place, :extent] = halfway[:extent, place].astype(jnp.bfloat16)
            columns[place, extent:] = halfway[extent:, place].astype(jnp.bfloat16)
        spectrum = jnp.dot(columns[...], backward_ref[...], preferred_element_type=jnp.float32)
        for member in range(group):
            q = block * group + member
            magnitude = jnp.full((extent, extent), 0.01, jnp.float32)
            for m in range(modes):
                w = member * modes + m
                place = slice(w * extent, (w + 1) * extent)
                real = spectrum[place, :extent]
                imag = spectrum[place, extent:]
                magnitude += real * real + imag * imag
            factor = moduli_ref[0, q].astype(jnp.float32) * lax.rsqrt(magnitude)
            for m in range(modes):
                w = member * modes + m
                place = slice(w * extent, (w + 1) * extent)
                real = spectrum[place, :extent]
                imag = spectrum[place, extent:]
                columns[place, :extent] = (real * factor).astype(jnp.bfloat16)
                columns[place, extent:] = (imag * factor).astype(jnp.bfloat16)
        returned = jnp.dot(columns[...], forward_ref[...], preferred_element_type=jnp.float32)
        for w in range(group * modes):
            place = slice(w * extent, (w + 1) * extent)
            batch[:extent, place] = returned[place, :extent].astype(jnp.bfloat16)
            batch[extent:, place] = returned[place, extent:].astype(jnp.bfloat16)
        new_wave = jnp.dot(backward_ref[...], batch[...], preferred_element_type=jnp.float32)
        for member in range(group):
            q = block * group + member
            row, col = corner(offsets_ref, q)
            here = pl.ds(row, extent)
            object_real = window[member, 0]
            object_imag = window[member, 1]
            sum_real = jnp.zeros((extent, extent), jnp.float32)
            sum_imag = jnp.zeros((extent, extent), jnp.float32)
            for m in range(modes):
                w = member * modes + m
                place = slice(w * extent, (w + 1) * extent)
                change_real = new_wave[:extent, place] - stacked[w, :extent]
                change_imag = new_wave[extent:, place] - stacked[w, extent:]
                probe_real = probe_ref[0, m, 0]
                probe_imag = probe_ref[1, m, 0]
                sum_real += probe_real * change_real + probe_imag * change_imag
                sum_imag += probe_real * change_imag - probe_imag * change_real
                probe_num[0, m] += object_real * change_real + object_imag * change_imag
                probe_num[1, m] += object_real * change_imag - object_imag * change_real
            for part, value in enumerate((sum_real, sum_imag)):
                for side, moved in enumerate(spread(value, col)):
                    total[part, side, here] += moved
        return carry

    lax.fori_loop(0, positions // group, step, 0)
    for part in range(2):
        for side, first in enumerate(range(0, cols, LANES)):
            last = min(first + LANES, cols)
            upper_ref[part, :, first:last] = total[part, side, :rows, : last - first]
            lower_ref[part, :, first:last] = total[part, side, rows:, : last - first].astype(
                jnp.bfloat16
            )
        for m in range(modes):
            share_ref[part * modes + m] = probe_num[part, m].astype(jnp.bfloat16)
    share_ref[2 * modes] = probe_den[...].astype(jnp.bfloat16)


def weight_kernel(offsets_ref, above_ref, probe_ref, inverse_ref, own, other):
    extent = probe_ref.shape[-1]
    modes = probe_ref.shape[1]
    rows, cols = inverse_ref.shape
    positions = offsets_ref.shape[0]
    power = jnp.zeros((extent, extent), jnp.float32)
    for part in range(2):
        for m in range(modes):
            value = probe_ref[part, m, 0]
            power += value * value
    largest = jnp.max(power)
    own[...] = jnp.zeros_like(own)
    other[...] = jnp.zeros_like(other)
    for table, place in ((offsets_ref, own), (above_ref, other)):
        for q in range(positions):
            row, col = corner(table, q)
            here = pl.ds(row, extent)
            for side, moved in enumerate(spread(power, col)):
                place[side, here] += moved
    has_above = lax.axis_index("tile") > 0
    for side, first in enumerate(range(0, cols, LANES)):
        last = min(first + LANES, cols)
        extra = jnp.where(has_above, other[side, rows:], 0.0)
        inverse = 1.0 / (own[side, :rows] + extra + 0.1 * largest + 1e-06)
        inverse_ref[:, first:last] = inverse[:, : last - first]


def object_kernel(object_ref, upper_ref, received_ref, inverse_ref, new_ref, sent_ref):
    has_above = lax.axis_index("tile") > 0
    for part in range(2):
        received = received_ref[part].astype(jnp.float32)
        wave = upper_ref[part] + jnp.where(has_above, received, 0.0)
        value = object_ref[part, 0] + wave * inverse_ref[...]
        new_ref[part] = value
        sent_ref[part] = value.astype(jnp.bfloat16)


def spectral_kernel(basis_ref, analysis_ref, threshold_ref, own_ref, *refs, sources, sizes):
    others, out_ref = refs[:-1], refs[-1]
    parts, rows, cols = own_ref.shape
    components = threshold_ref.shape[0]
    zs, ms = sizes
    z = lax.axis_index("energy")
    m = lax.axis_index("mode")
    mine = z * ms + m
    labels = [(z ^ dz) * ms + (m ^ dm) for dz, dm in sources]
    chunk = 16
    per_part = rows // chunk

    def step(index, carry):
        part = index // per_part
        here = pl.ds(pl.multiple_of((index % per_part) * chunk, chunk), chunk)
        own = own_ref[part, here]
        values = [own] + [ref[part, here].astype(jnp.float32) for ref in others]
        projected = 0.5 * own
        for k in range(components):
            c = analysis_ref[k, mine] * values[0]
            for label, value in zip(labels, values[1:]):
                c += analysis_ref[k, label] * value
            t = threshold_ref[k]
            c = c - jnp.minimum(jnp.maximum(c, -t), t)
            projected += (0.5 * basis_ref[mine, k]) * c
        out_ref[part, 0, here] = projected
        return carry

    lax.fori_loop(0, parts * per_part, step, 0)


def probe_kernel(probe_ref, own_ref, received_ref, out_ref):
    modes = probe_ref.shape[1]
    density = own_ref[2 * modes].astype(jnp.float32) + received_ref[2 * modes].astype(jnp.float32)
    inverse = 1.0 / (density + 0.1 * jnp.max(density) + 1e-06)
    for part in range(2):
        for m in range(modes):
            k = part * modes + m
            numerator = own_ref[k].astype(jnp.float32) + received_ref[k].astype(jnp.float32)
            out_ref[part, m, 0] = probe_ref[part, m, 0] + numerator * inverse


def call(kernel, inputs, scalars, outputs, scratch=(), cost=0, name=None):
    return pl.pallas_call(
        kernel,
        out_shape=outputs,
        in_specs=[SMEM] * scalars + [VMEM] * (len(inputs) - scalars),
        out_specs=jax.tree.map(lambda _: VMEM, outputs),
        scratch_shapes=list(scratch),
        name=name,
    )(*inputs)


def body(object_field, probe_field, modulus, offsets, spectra_basis, analysis, threshold):
    extent = probe_field.shape[-1]
    modes = probe_field.shape[1]
    rows, cols = object_field.shape[2:]
    positions = offsets.shape[0]
    tiles = lax.axis_size("tile")
    zs = lax.axis_size("energy")
    ms = lax.axis_size("mode")
    forward, backward = dft_tables(extent)
    shape = jax.ShapeDtypeStruct
    f32, bf16 = jnp.float32, jnp.bfloat16
    sides = pl.cdiv(cols, LANES)

    message = call(
        round_kernel, (offsets, object_field), 1, shape((2, rows + PAD_ROWS, cols), bf16), name="round"
    )
    if tiles == 2:
        below = above = lax.ppermute(message, "tile", swap_pairs(2, 1))
    else:
        below = lax.ppermute(message, "tile", [(i + 1, i) for i in range(tiles - 1)])
        above = lax.ppermute(message, "tile", [(i, i + 1) for i in range(tiles - 1)])
    above_offsets = above[0, rows, : 2 * positions].astype(jnp.int32).reshape(positions, 2)

    group = 2
    waves = group * modes
    upper, lower, share = call(
        functools.partial(wave_kernel, tiles=tiles, group=group),
        (offsets, message, below, probe_field, modulus, forward, backward),
        1,
        (
            shape((2, rows, cols), f32),
            shape((2, rows, cols), bf16),
            shape((2 * modes + 1, extent, extent), bf16),
        ),
        (
            pltpu.VMEM((2, sides, rows + extent, LANES), f32),
            pltpu.VMEM((2, sides, rows + extent, LANES), f32),
            pltpu.VMEM((group, 2, extent, extent), f32),
            pltpu.VMEM((waves, 2 * extent, extent), f32),
            pltpu.VMEM((2 * extent, waves * extent), bf16),
            pltpu.VMEM((waves * extent, 2 * extent), bf16),
            pltpu.VMEM((2, modes, extent, extent), f32),
            pltpu.VMEM((extent, extent), f32),
        ),
        name="wave",
    )
    if tiles == 2:
        received = lax.ppermute(lower, "tile", swap_pairs(2, 1))
    else:
        received = lax.ppermute(lower, "tile", [(i, i + 1) for i in range(tiles - 1)])
    inverse = call(
        weight_kernel,
        (offsets, above_offsets, probe_field),
        2,
        shape((rows, cols), f32),
        (
            pltpu.VMEM((sides, rows + extent, LANES), f32),
            pltpu.VMEM((sides, rows + extent, LANES), f32),
        ),
        name="weight",
    )
    object_new, sent = call(
        object_kernel,
        (object_field, upper, received, inverse),
        0,
        (shape((2, rows, cols), f32), shape((2, rows, cols), bf16)),
        name="object",
    )
    sources = []
    arrived = []
    for dz in range(zs):
        piece = sent if dz == 0 else lax.ppermute(sent, "energy", swap_pairs(zs, dz))
        for dm in range(ms):
            if dz == 0 and dm == 0:
                continue
            sources.append((dz, dm))
            arrived.append(piece if dm == 0 else lax.ppermute(piece, "mode", swap_pairs(ms, dm)))
    object_out = call(
        functools.partial(spectral_kernel, sources=tuple(sources), sizes=(zs, ms)),
        (spectra_basis, analysis, threshold, object_new, *arrived),
        3,
        shape(object_field.shape, f32),
        name="spectral",
    )
    for distance in [1 << k for k in range(1, tiles.bit_length() - 1)]:
        other = lax.ppermute(share, "tile", swap_pairs(tiles, distance))
        share = (share.astype(f32) + other.astype(f32)).astype(bf16)
    other = lax.ppermute(share, "tile", swap_pairs(tiles, 1))
    probe_out = call(
        probe_kernel, (probe_field, share, other), 0, shape(probe_field.shape, f32), name="probes"
    )
    return (object_out, probe_out)


def solution(mesh):
    placed = (
        P(None, ("groups", "energy", "mode"), "tile", None),
        P(None, None, ("groups", "energy", "mode"), None, None),
        P(("groups", "energy", "mode"), "tile", None, None),
        P(("groups", "tile"), None),
        P(),
        P(),
        P(),
    )
    return jax.shard_map(
        body,
        mesh=mesh,
        in_specs=placed,
        out_specs=(
            P(None, ("groups", "energy", "mode"), "tile", None),
            P(None, None, ("groups", "energy", "mode"), None, None),
        ),
        check_vma=False,
    )
```

profile of v0, /device:TPU:0, one launch (start us, length us, event | category | flops | bytes accessed | tf_op | source)
XLA Modules:
  0.0 52.6 jit_solution(1696138885642653334)
XLA Ops:
  0.6 1.3 %copy.19.offsets_ref = s32[8,2]{1,0:T(8,128)} copy(s32[8,2]{0,1:T(2,128)} %param.12) | data formatting | bytes 128 | tf_op args[3]
  2.0 1.8 %copy.21.object_ref = f32[2,1,128,192]{3,2,1,0:T(8,128)} copy(f32[2,1,128,192]{2,3,1,0:T(8,128)} %param.9) | data formatting | bytes 393216 | tf_op args[0]
  3.7 1.6 %round.1.own_ref = bf16[2,144,192]{2,1,0:T(8,128)(2,1)} custom-call(s32[8,2]{1,0:T(8,128)} %copy.19.offsets_ref, f32[2,1,128,192]{3,2,1,0:T(8,128)} %copy.21.object_ref), custom_call_target="tpu_custom_call" | custom-call | tf_op jit(solution)/shard_map/round/pallas_call | solution.py:282
  5.4 3.0 %collective-permute-start = (bf16[2,144,192]{2,1,0:T(8,128)(2,1)}, bf16[2,144,192]{2,1,0:T(8,128)(2,1)S(1)}, u32[]{:S(2)}, u32[]{:S(2)}) collective-permute-start(bf16[2,144,192]{2,1,0:T(8,128)(2,1)} %round.1.own_ref), channel_id=1, source_target_pairs={{0,2},{2,0},{1,3},{3,1},{4,6},{6,4},{5,7},{7,5},{8,10},{10,8},{9,1... | collective-permute-start | bytes 331784 | tf_op jit(solution)/shard_map/ppermute | solution.py:309
  8.3 4.1 %collective-permute-done.below_ref = bf16[2,144,192]{2,1,0:T(8,128)(2,1)S(1)} collective-permute-done((bf16[2,144,192]{2,1,0:T(8,128)(2,1)}, bf16[2,144,192]{2,1,0:T(8,128)(2,1)S(1)}, u32[]{:S(2)}, u32[]{:S(2)}) %collective-permute-start) | collective-permute-done | bytes 110624 | tf_op jit(solution)/shard_map/ppermute | solution.py:309
  12.4 0.7 %copy-done.1 = bf16[2,144,192]{2,1,0:T(8,128)(2,1)} copy-done((bf16[2,144,192]{2,1,0:T(8,128)(2,1)}, bf16[2,144,192]{2,1,0:T(8,128)(2,1)S(1)}, u32[]{:S(2)}) %copy-start.1) | copy-done | bytes 110616
  13.0 8.0 %wave.1 = (f32[2,128,192]{2,1,0:T(8,128)}, bf16[2,128,192]{2,1,0:T(8,128)(2,1)}, bf16[7,128,128]{2,1,0:T(8,128)(2,1)}) custom-call(s32[8,2]{1,0:T(8,128)} %copy.19.offsets_ref, bf16[2,144,192]{2,1,0:T(8,128)(2,1)} %round.1.own_ref, bf16[2,144,192]{2,1,0:T(8,128)(2,1)} %copy-done.1, f32[2,3,1,128,128]{4,3,2,1,0:T(8,128)} %probe_ref.5, ...), custom_call_target="tpu_custom_call" | custom-call | tf_op jit(solution)/shard_map/wave/pallas_call | solution.py:282
  21.0 1.7 %collective-permute-start.1 = (bf16[2,128,192]{2,1,0:T(8,128)(2,1)}, bf16[2,128,192]{2,1,0:T(8,128)(2,1)S(1)}, u32[]{:S(2)}, u32[]{:S(2)}) collective-permute-start(bf16[2,128,192]{2,1,0:T(8,128)(2,1)} %get-tuple-element.8), channel_id=1, source_target_pairs={{0,2},{2,0},{1,3},{3,1},{4,6},{6,4},{5,7},{7,5},{8,10},{10,8},{9,1... | collective-permute-start | bytes 294920 | tf_op jit(solution)/shard_map/ppermute | solution.py:339
  23.1 0.7 %fusion = s32[16]{0:T(128)S(1)} fusion(bf16[2,144,192]{2,1,0:T(8,128)(2,1)} %copy-done.1), kind=kLoop, calls=%fused_computation.1 | loop fusion | flops 16 | bytes 96 | tf_op jit(solution)/shard_map/convert_element_type | solution.py:313
  23.7 0.7 %reshape.8.above_ref = s32[8,2]{1,0:T(8,128)} reshape(s32[16]{0:T(128)S(1)} %fusion) | data formatting | bytes 128 | tf_op jit(solution)/shard_map/convert_element_type | solution.py:313
  24.4 2.1 %weight.1.inverse_ref = f32[128,192]{1,0:T(8,128)} custom-call(s32[8,2]{1,0:T(8,128)} %copy.19.offsets_ref, s32[8,2]{1,0:T(8,128)} %reshape.8.above_ref, f32[2,3,1,128,128]{4,3,2,1,0:T(8,128)} %probe_ref.5), custom_call_target="tpu_custom_call" | custom-call | tf_op jit(solution)/shard_map/weight/pallas_call | solution.py:282
  26.5 1.1 %collective-permute-done.1.received_ref = bf16[2,128,192]{2,1,0:T(8,128)(2,1)S(1)} collective-permute-done((bf16[2,128,192]{2,1,0:T(8,128)(2,1)}, bf16[2,128,192]{2,1,0:T(8,128)(2,1)S(1)}, u32[]{:S(2)}, u32[]{:S(2)}) %collective-permute-start.1) | collective-permute-done | bytes 98336 | tf_op jit(solution)/shard_map/ppermute | solution.py:339
  27.6 0.7 %copy-done.2 = bf16[2,128,192]{2,1,0:T(8,128)(2,1)} copy-done((bf16[2,128,192]{2,1,0:T(8,128)(2,1)}, bf16[2,128,192]{2,1,0:T(8,128)(2,1)S(1)}, u32[]{:S(2)}) %copy-start.2) | copy-done | bytes 98328
  28.3 1.9 %object.1 = (f32[2,128,192]{2,1,0:T(8,128)}, bf16[2,128,192]{2,1,0:T(8,128)(2,1)}) custom-call(f32[2,1,128,192]{3,2,1,0:T(8,128)} %copy.21.object_ref, f32[2,128,192]{2,1,0:T(8,128)} %get-tuple-element.7.upper_ref, bf16[2,128,192]{2,1,0:T(8,128)(2,1)} %copy-done.2, f32[128,192]{1,0:T(8,128)} %weight.1.inverse_ref), custom_call_target="tpu_custom_call" | custom-call | tf_op jit(solution)/shard_map/object/pallas_call | solution.py:282
  30.2 3.9 %collective-permute-start.7 = (bf16[2,128,192]{2,1,0:T(8,128)(2,1)}, bf16[2,128,192]{2,1,0:T(8,128)(2,1)S(1)}, u32[]{:S(2)}, u32[]{:S(2)}) collective-permute-start(bf16[2,128,192]{2,1,0:T(8,128)(2,1)} %get-tuple-element.10), channel_id=1, source_target_pairs={{0,12},{4,8},{8,4},{12,0},{1,13},{5,9},{9,5},{13,1},{2,14},{6,10},... | collective-permute-start | bytes 294920 | tf_op jit(solution)/shard_map/ppermute | solution.py:363
  34.0 0.6 %collective-permute-start.3 = (bf16[2,128,192]{2,1,0:T(8,128)(2,1)}, bf16[2,128,192]{2,1,0:T(8,128)(2,1)S(1)}, u32[]{:S(2)}, u32[]{:S(2)}) collective-permute-start(bf16[2,128,192]{2,1,0:T(8,128)(2,1)} %get-tuple-element.10), channel_id=1, source_target_pairs={{0,4},{4,0},{8,12},{12,8},{1,5},{5,1},{9,13},{13,9},{2,6},{6,2},{1... | collective-permute-start | bytes 294920 | tf_op jit(solution)/shard_map/ppermute | solution.py:363
  34.6 3.8 %collective-permute-done.7.refs_5_ = bf16[2,128,192]{2,1,0:T(8,128)(2,1)S(1)} collective-permute-done((bf16[2,128,192]{2,1,0:T(8,128)(2,1)}, bf16[2,128,192]{2,1,0:T(8,128)(2,1)S(1)}, u32[]{:S(2)}, u32[]{:S(2)}) %collective-permute-start.7) | collective-permute-done | bytes 98336 | tf_op jit(solution)/shard_map/ppermute | solution.py:363
  38.4 4.3 %collective-permute-done.5.refs_3_ = bf16[2,128,192]{2,1,0:T(8,128)(2,1)S(1)} collective-permute-done((bf16[2,128,192]{2,1,0:T(8,128)(2,1)}, bf16[2,128,192]{2,1,0:T(8,128)(2,1)S(1)}, u32[]{:S(2)}, u32[]{:S(2)}) %collective-permute-start.5) | collective-permute-done | bytes 98336 | tf_op jit(solution)/shard_map/ppermute | solution.py:363
  42.8 0.5 collective-permute-start.4
  43.3 0.7 %copy-done = bf16[7,128,128]{2,1,0:T(8,128)(2,1)} copy-done((bf16[7,128,128]{2,1,0:T(8,128)(2,1)}, bf16[7,128,128]{2,1,0:T(8,128)(2,1)S(1)}, u32[]{:S(2)}) %copy-start) | copy-done | bytes 229400
  44.0 2.1 %probes.1 = f32[2,3,1,128,128]{4,3,2,1,0:T(8,128)} custom-call(f32[2,3,1,128,128]{4,3,2,1,0:T(8,128)} %probe_ref.5, bf16[7,128,128]{2,1,0:T(8,128)(2,1)} %get-tuple-element.11.own_ref, bf16[7,128,128]{2,1,0:T(8,128)(2,1)} %copy-done), custom_call_target="tpu_custom_call" | custom-call | tf_op jit(solution)/shard_map/probes/pallas_call | solution.py:282
  46.2 0.6 %copy-done.6 = bf16[2,128,192]{2,1,0:T(8,128)(2,1)} copy-done((bf16[2,128,192]{2,1,0:T(8,128)(2,1)}, bf16[2,128,192]{2,1,0:T(8,128)(2,1)S(1)}, u32[]{:S(2)}) %copy-start.6) | copy-done | bytes 98328
  46.9 3.9 %spectral.1 = f32[2,1,128,192]{3,2,1,0:T(8,128)} custom-call(f32[8,8]{1,0:T(8,128)} %basis_ref.1, f32[8,8]{1,0:T(8,128)} %analysis_ref.1, f32[8]{0:T(128)} %threshold_ref.1, f32[2,128,192]{2,1,0:T(8,128)} %get-tuple-element.9.own_ref, bf16[2,128,192]{2,1,0:T(8,128)(2,1)} %copy-done.6, bf16[2,128,192]{2,1,0:T(8,128)(2,1)} %copy-done.5, ...), custom_call_target="tpu_custom_call" | custom-call | tf_op jit(solution)/shard_map/spectral/pallas_call | solution.py:282
  50.8 1.8 %copy.22 = f32[2,1,128,192]{2,3,1,0:T(8,128)} copy(f32[2,1,128,192]{3,2,1,0:T(8,128)} %spectral.1) | data formatting | bytes 393216
  (27 shorter events, 0.5 us)
Async XLA Ops:
  5.4 7.0 %collective-permute-start = (bf16[2,144,192]{2,1,0:T(8,128)(2,1)}, bf16[2,144,192]{2,1,0:T(8,128)(2,1)S(1)}, u32[]{:S(2)}, u32[]{:S(2)}) collective-permute-start(bf16[2,144,192]{2,1,0:T(8,128)(2,1)} %round.1.own_ref), channel_id=1, source_target_pairs={{0,2},{2,0},{1,3},{3,1},{4,6},{6,4},{5,7},{7,5},{8,10},{10,8},{9,1... | collective-permute-start | bytes 331784 | tf_op jit(solution)/shard_map/ppermute | solution.py:309
  12.4 0.7 %copy-start.1 = (bf16[2,144,192]{2,1,0:T(8,128)(2,1)}, bf16[2,144,192]{2,1,0:T(8,128)(2,1)S(1)}, u32[]{:S(2)}) copy-start(bf16[2,144,192]{2,1,0:T(8,128)(2,1)S(1)} %collective-permute-done.below_ref) | copy-start | bytes 331780
  21.0 6.6 %collective-permute-start.1 = (bf16[2,128,192]{2,1,0:T(8,128)(2,1)}, bf16[2,128,192]{2,1,0:T(8,128)(2,1)S(1)}, u32[]{:S(2)}, u32[]{:S(2)}) collective-permute-start(bf16[2,128,192]{2,1,0:T(8,128)(2,1)} %get-tuple-element.8), channel_id=1, source_target_pairs={{0,2},{2,0},{1,3},{3,1},{4,6},{6,4},{5,7},{7,5},{8,10},{10,8},{9,1... | collective-permute-start | bytes 294920 | tf_op jit(solution)/shard_map/ppermute | solution.py:339
  22.8 20.5 %collective-permute-start.9 = (bf16[7,128,128]{2,1,0:T(8,128)(2,1)}, bf16[7,128,128]{2,1,0:T(8,128)(2,1)S(1)}, u32[]{:S(2)}, u32[]{:S(2)}) collective-permute-start(bf16[7,128,128]{2,1,0:T(8,128)(2,1)} %get-tuple-element.11.own_ref), channel_id=1, source_target_pairs={{0,2},{2,0},{1,3},{3,1},{4,6},{6,4},{5,7},{7,5},{8,10},{10,8},{9,1... | collective-permute-start | bytes 688136 | tf_op jit(solution)/shard_map/ppermute | solution.py:379
  27.6 0.7 %copy-start.2 = (bf16[2,128,192]{2,1,0:T(8,128)(2,1)}, bf16[2,128,192]{2,1,0:T(8,128)(2,1)S(1)}, u32[]{:S(2)}) copy-start(bf16[2,128,192]{2,1,0:T(8,128)(2,1)S(1)} %collective-permute-done.1.received_ref) | copy-start | bytes 294916
  30.2 8.3 %collective-permute-start.7 = (bf16[2,128,192]{2,1,0:T(8,128)(2,1)}, bf16[2,128,192]{2,1,0:T(8,128)(2,1)S(1)}, u32[]{:S(2)}, u32[]{:S(2)}) collective-permute-start(bf16[2,128,192]{2,1,0:T(8,128)(2,1)} %get-tuple-element.10), channel_id=1, source_target_pairs={{0,12},{4,8},{8,4},{12,0},{1,13},{5,9},{9,5},{13,1},{2,14},{6,10},... | collective-permute-start | bytes 294920 | tf_op jit(solution)/shard_map/ppermute | solution.py:363
  34.0 8.8 %collective-permute-start.5 = (bf16[2,128,192]{2,1,0:T(8,128)(2,1)}, bf16[2,128,192]{2,1,0:T(8,128)(2,1)S(1)}, u32[]{:S(2)}, u32[]{:S(2)}) collective-permute-start(bf16[2,128,192]{2,1,0:T(8,128)(2,1)} %get-tuple-element.10), channel_id=1, source_target_pairs={{0,8},{4,12},{8,0},{12,4},{1,9},{5,13},{9,1},{13,5},{2,10},{6,14},... | collective-permute-start | bytes 294920 | tf_op jit(solution)/shard_map/ppermute | solution.py:363
  34.0 8.8 %collective-permute-start.3 = (bf16[2,128,192]{2,1,0:T(8,128)(2,1)}, bf16[2,128,192]{2,1,0:T(8,128)(2,1)S(1)}, u32[]{:S(2)}, u32[]{:S(2)}) collective-permute-start(bf16[2,128,192]{2,1,0:T(8,128)(2,1)} %get-tuple-element.10), channel_id=1, source_target_pairs={{0,4},{4,0},{8,12},{12,8},{1,5},{5,1},{9,13},{13,9},{2,6},{6,2},{1... | collective-permute-start | bytes 294920 | tf_op jit(solution)/shard_map/ppermute | solution.py:363
  34.6 11.5 %collective-permute-start.2 = (bf16[2,128,192]{2,1,0:T(8,128)(2,1)}, bf16[2,128,192]{2,1,0:T(8,128)(2,1)S(1)}, u32[]{:S(2)}, u32[]{:S(2)}) collective-permute-start(bf16[2,128,192]{2,1,0:T(8,128)(2,1)} %get-tuple-element.10), channel_id=1, source_target_pairs={{0,1},{1,0},{2,3},{3,2},{4,5},{5,4},{6,7},{7,6},{8,9},{9,8},{10,11... | collective-permute-start | bytes 294920 | tf_op jit(solution)/shard_map/ppermute | solution.py:368
  38.4 7.6 %copy-start.3 = (bf16[2,128,192]{2,1,0:T(8,128)(2,1)}, bf16[2,128,192]{2,1,0:T(8,128)(2,1)S(1)}, u32[]{:S(2)}) copy-start(bf16[2,128,192]{2,1,0:T(8,128)(2,1)S(1)} %collective-permute-done.7.refs_5_) | copy-start | bytes 294916
  38.4 7.7 %collective-permute-start.8 = (bf16[2,128,192]{2,1,0:T(8,128)(2,1)S(1)}, bf16[2,128,192]{2,1,0:T(8,128)(2,1)S(1)}, u32[]{:S(2)}, u32[]{:S(2)}) collective-permute-start(bf16[2,128,192]{2,1,0:T(8,128)(2,1)S(1)} %collective-permute-done.7.refs_5_), channel_id=1, source_target_pairs={{0,1},{1,0},{2,3},{3,2},{4,5},{5,4},{6,7},{7,6},{8,9},{9,8},{10,11... | collective-permute-start | bytes 294920 | tf_op jit(solution)/shard_map/ppermute | solution.py:368
  42.8 3.3 %copy-start.4 = (bf16[2,128,192]{2,1,0:T(8,128)(2,1)}, bf16[2,128,192]{2,1,0:T(8,128)(2,1)S(1)}, u32[]{:S(2)}) copy-start(bf16[2,128,192]{2,1,0:T(8,128)(2,1)S(1)} %collective-permute-done.5.refs_3_) | copy-start | bytes 294916
  42.8 3.3 %collective-permute-start.6 = (bf16[2,128,192]{2,1,0:T(8,128)(2,1)S(1)}, bf16[2,128,192]{2,1,0:T(8,128)(2,1)S(1)}, u32[]{:S(2)}, u32[]{:S(2)}) collective-permute-start(bf16[2,128,192]{2,1,0:T(8,128)(2,1)S(1)} %collective-permute-done.5.refs_3_), channel_id=1, source_target_pairs={{0,1},{1,0},{2,3},{3,2},{4,5},{5,4},{6,7},{7,6},{8,9},{9,8},{10,11... | collective-permute-start | bytes 294920 | tf_op jit(solution)/shard_map/ppermute | solution.py:368
  42.8 3.3 %copy-start.5 = (bf16[2,128,192]{2,1,0:T(8,128)(2,1)}, bf16[2,128,192]{2,1,0:T(8,128)(2,1)S(1)}, u32[]{:S(2)}) copy-start(bf16[2,128,192]{2,1,0:T(8,128)(2,1)S(1)} %collective-permute-done.3.refs_1_) | copy-start | bytes 294916
  42.8 3.3 %collective-permute-start.4 = (bf16[2,128,192]{2,1,0:T(8,128)(2,1)S(1)}, bf16[2,128,192]{2,1,0:T(8,128)(2,1)S(1)}, u32[]{:S(2)}, u32[]{:S(2)}) collective-permute-start(bf16[2,128,192]{2,1,0:T(8,128)(2,1)S(1)} %collective-permute-done.3.refs_1_), channel_id=1, source_target_pairs={{0,1},{1,0},{2,3},{3,2},{4,5},{5,4},{6,7},{7,6},{8,9},{9,8},{10,11... | collective-permute-start | bytes 294920 | tf_op jit(solution)/shard_map/ppermute | solution.py:368
  43.3 0.7 %copy-start = (bf16[7,128,128]{2,1,0:T(8,128)(2,1)}, bf16[7,128,128]{2,1,0:T(8,128)(2,1)S(1)}, u32[]{:S(2)}) copy-start(bf16[7,128,128]{2,1,0:T(8,128)(2,1)S(1)} %collective-permute-done.9.received_ref) | copy-start | bytes 688132
  46.1 0.7 %copy-start.6 = (bf16[2,128,192]{2,1,0:T(8,128)(2,1)}, bf16[2,128,192]{2,1,0:T(8,128)(2,1)S(1)}, u32[]{:S(2)}) copy-start(bf16[2,128,192]{2,1,0:T(8,128)(2,1)S(1)} %collective-permute-done.2.refs_0_) | copy-start | bytes 294916
  46.1 0.7 %copy-start.7 = (bf16[2,128,192]{2,1,0:T(8,128)(2,1)}, bf16[2,128,192]{2,1,0:T(8,128)(2,1)S(1)}, u32[]{:S(2)}) copy-start(bf16[2,128,192]{2,1,0:T(8,128)(2,1)S(1)} %collective-permute-done.8.refs_6_) | copy-start | bytes 294916
  46.1 0.7 %copy-start.8 = (bf16[2,128,192]{2,1,0:T(8,128)(2,1)}, bf16[2,128,192]{2,1,0:T(8,128)(2,1)S(1)}, u32[]{:S(2)}) copy-start(bf16[2,128,192]{2,1,0:T(8,128)(2,1)S(1)} %collective-permute-done.6.refs_4_) | copy-start | bytes 294916
  46.2 0.7 %copy-start.9 = (bf16[2,128,192]{2,1,0:T(8,128)(2,1)}, bf16[2,128,192]{2,1,0:T(8,128)(2,1)S(1)}, u32[]{:S(2)}) copy-start(bf16[2,128,192]{2,1,0:T(8,128)(2,1)S(1)} %collective-permute-done.4.refs_2_) | copy-start | bytes 294916
where the time goes:
time: 52.9 us; the launch traced here: 52.6 us
  Pallas kernels  19.6 us (37%)
  waiting for transfers between devices  13.4 us (25%)
  starting transfers between devices  9.92 us (19%)
  local copies, waits for them, and re-layouts  8.24 us (16%)
  between operations  0.73 us (1%)
  other arithmetic  0.68 us (1%)
    pallas_call x6, Pallas kernels, call(): pl.pallas_call(kernel, out_shape=outputs, in_specs=[SMEM] * scalars + [VM...  19.6 us
    ppermute x3, waiting for transfers between devices, body(): lax.ppermute(sent, 'energy', swap_pairs(zs, dz))  8.18 us
    unnamed x23, local copies, waits for them, and re-layouts  7.57 us
    ppermute x3, starting transfers between devices, body(): lax.ppermute(sent, 'energy', swap_pairs(zs, dz))  4.42 us
    ppermute x1, waiting for transfers between devices, body(): below = above = lax.ppermute(message, 'tile', swap_pairs(2, 1))  4.05 us
    ppermute x1, starting transfers between devices, body(): below = above = lax.ppermute(message, 'tile', swap_pairs(2, 1))  2.97 us
    ppermute x1, starting transfers between devices, body(): received = lax.ppermute(lower, 'tile', swap_pairs(2, 1))  1.74 us
    ppermute x1, waiting for transfers between devices, body(): received = lax.ppermute(lower, 'tile', swap_pairs(2, 1))  1.12 us
  transfers between devices with their start and end apart: 10, of which 4 were waited for; matrix products, arithmetic and copies ran while one was open for 3% of the time, Pallas kernels for 12%

commit v1 on v0

v1 whole, which is shorter than its diff:
```python
import functools
import math

import jax
import jax.numpy as jnp
import ml_dtypes
import numpy as np
from jax import lax
from jax.experimental import pallas as pl
from jax.experimental.pallas import tpu as pltpu
from jax.sharding import PartitionSpec as P

PCOLS = 2
STEP = 32
LANES = 128
PAD_ROWS = 16

VMEM = pl.BlockSpec(memory_space=pltpu.VMEM)
SMEM = pl.BlockSpec(memory_space=pltpu.SMEM)


def swap_pairs(size, distance):
    return [(i, i ^ distance) for i in range(size)]


def dft_tables(extent):
    counter = np.arange(extent)
    phases = -2.0 * math.pi / extent * (counter[:, None] * counter[None, :] % extent)
    cosine = np.cos(phases) / math.sqrt(extent)
    sine = np.sin(phases) / math.sqrt(extent)
    forward = np.block([[cosine, -sine], [sine, cosine]])
    backward = np.block([[cosine, sine], [-sine, cosine]])
    return (
        jnp.asarray(forward.astype(np.float32).astype(ml_dtypes.bfloat16)),
        jnp.asarray(backward.astype(np.float32).astype(ml_dtypes.bfloat16)),
    )


def corner(offsets, q):
    row = STEP * (q // PCOLS) + offsets[0, q]
    col = STEP * (q % PCOLS) + offsets[1, q]
    return row, col


def spread(block, row):
    lane = lax.broadcasted_iota(jnp.int32, block.shape, 1)
    turned = pltpu.roll(block, row, 1)
    left = jnp.where(lane >= row, turned, 0.0)
    right = jnp.where(lane < row, turned, 0.0)
    return left, right


def round_kernel(offsets_ref, object_ref, message_ref):
    cols, rows = object_ref.shape[2:]
    positions = offsets_ref.shape[1]
    for part in range(2):
        message_ref[part, :cols] = object_ref[part, 0].astype(jnp.bfloat16)
    lane = lax.broadcasted_iota(jnp.int32, (PAD_ROWS, rows), 1)
    line = jnp.zeros((PAD_ROWS, rows), jnp.float32)
    for k in range(2):
        for q in range(positions):
            value = offsets_ref[k, q].astype(jnp.float32)
            line = jnp.where(lane == k * positions + q, value, line)
    for part in range(2):
        message_ref[part, cols:] = line.astype(jnp.bfloat16)


def turn_kernel(probe_ref, moduli_ref, turned_ref, moduli_out_ref):
    modes = probe_ref.shape[1]
    for part in range(2):
        for m in range(modes):
            turned_ref[part, m] = probe_ref[part, m, 0].T
    for q in range(moduli_ref.shape[1]):
        moduli_out_ref[q] = moduli_ref[0, q].astype(jnp.float32).T


def wave_kernel(
    offsets_ref,
    own_ref,
    below_ref,
    probe_ref,
    moduli_ref,
    forward_ref,
    backward_ref,
    upper_ref,
    lower_ref,
    share_ref,
    extended,
    total,
    window,
    stacked,
    tall,
    long,
    probe_num,
    probe_den,
    *,
    tiles,
    group,
):
    extent = probe_ref.shape[-1]
    modes = probe_ref.shape[1]
    cols = own_ref.shape[1] - PAD_ROWS
    positions = offsets_ref.shape[1]
    has_below = lax.axis_index("tile") < tiles - 1
    for part in range(2):
        extended[part, 0] = own_ref[part, :cols].astype(jnp.float32)
        below = below_ref[part, :cols].astype(jnp.float32)
        extended[part, 1] = jnp.where(has_below, below, 0.0)
    total[...] = jnp.zeros_like(total)
    probe_num[...] = jnp.zeros_like(probe_num)
    probe_den[...] = jnp.zeros_like(probe_den)
    lane = lax.broadcasted_iota(jnp.int32, (extent, extent), 1)

    def places(member, m):
        w = member * modes + m
        return slice(w * extent, (w + 1) * extent)

    def step(block, carry):
        for member in range(group):
            q = block * group + member
            row, col = corner(offsets_ref, q)
            here = pl.ds(col, extent)
            for part in range(2):
                left = pltpu.roll(extended[part, 0, here], extent - row, 1)
                right = pltpu.roll(extended[part, 1, here], extent - row, 1)
                window[member, part] = jnp.where(lane < extent - row, left, right)
            object_real = window[member, 0]
            object_imag = window[member, 1]
            probe_den[...] += object_real * object_real + object_imag * object_imag
            for m in range(modes):
                place = places(member, m)
                probe_real = probe_ref[0, m]
                probe_imag = probe_ref[1, m]
                wave_real = probe_real * object_real - probe_imag * object_imag
                wave_imag = probe_real * object_imag + probe_imag * object_real
                stacked[0, place] = wave_real
                stacked[1, place] = wave_imag
                tall[place, :extent] = wave_real.astype(jnp.bfloat16)
                tall[place, extent:] = wave_imag.astype(jnp.bfloat16)
        halfway = jnp.dot(tall[...], backward_ref[...], preferred_element_type=jnp.float32)
        for member in range(group):
            for m in range(modes):
                place = places(member, m)
                long[:extent, place] = halfway[place, :extent].astype(jnp.bfloat16)
                long[extent:, place] = halfway[place, extent:].astype(jnp.bfloat16)
        spectrum = jnp.dot(forward_ref[...], long[...], preferred_element_type=jnp.float32)
        for member in range(group):
            q = block * group + member
            magnitude = jnp.full((extent, extent), 0.01, jnp.float32)
            for m in range(modes):
                place = places(member, m)
                real = spectrum[:extent, place]
                imag = spectrum[extent:, place]
                magnitude += real * real + imag * imag
            factor = moduli_ref[q] * lax.rsqrt(magnitude)
            for m in range(modes):
                place = places(member, m)
                long[:extent, place] = (spectrum[:extent, place] * factor).astype(jnp.bfloat16)
                long[extent:, place] = (spectrum[extent:, place] * factor).astype(jnp.bfloat16)
        returned = jnp.dot(backward_ref[...], long[...], preferred_element_type=jnp.float32)
        for member in range(group):
            for m in range(modes):
                place = places(member, m)
                tall[place, :extent] = returned[:extent, place].astype(jnp.bfloat16)
                tall[place, extent:] = returned[extent:, place].astype(jnp.bfloat16)
        new_wave = jnp.dot(tall[...], forward_ref[...], preferred_element_type=jnp.float32)
        for member in range(group):
            q = block * group + member
            row, col = corner(offsets_ref, q)
            here = pl.ds(col, extent)
            object_real = window[member, 0]
            object_imag = window[member, 1]
            sum_real = jnp.zeros((extent, extent), jnp.float32)
            sum_imag = jnp.zeros((extent, extent), jnp.float32)
            for m in range(modes):
                place = places(member, m)
                change_real = new_wave[place, :extent] - stacked[0, place]
                change_imag = new_wave[place, extent:] - stacked[1, place]
                probe_real = probe_ref[0, m]
                probe_imag = probe_ref[1, m]
                sum_real += probe_real * change_real + probe_imag * change_imag
                sum_imag += probe_real * change_imag - probe_imag * change_real
                probe_num[0, m] += object_real * change_real + object_imag * change_imag
                probe_num[1, m] += object_real * change_imag - object_imag * change_real
            for part, value in enumerate((sum_real, sum_imag)):
                for side, moved in enumerate(spread(value, row)):
                    total[part, side, here] += moved
        return carry

    lax.fori_loop(0, positions // group, step, 0)
    for part in range(2):
        upper_ref[part] = total[part, 0]
        lower_ref[part] = total[part, 1].astype(jnp.bfloat16)
        for m in range(modes):
            share_ref[part * modes + m] = probe_num[part, m].astype(jnp.bfloat16)
    share_ref[2 * modes] = probe_den[...].astype(jnp.bfloat16)


def weight_kernel(offsets_ref, above_ref, probe_ref, inverse_ref, own, other):
    extent = probe_ref.shape[-1]
    modes = probe_ref.shape[1]
    cols = inverse_ref.shape[0]
    positions = offsets_ref.shape[1]
    power = jnp.zeros((extent, extent), jnp.float32)
    for part in range(2):
        for m in range(modes):
            value = probe_ref[part, m]
            power += value * value
    largest = jnp.max(power)
    own[...] = jnp.zeros_like(own)
    other[...] = jnp.zeros_like(other)
    line = above_ref[0, cols : cols + PAD_ROWS].astype(jnp.float32)[:8]
    lane = lax.broadcasted_iota(jnp.int32, line.shape, 1)
    for q in range(positions):
        row, col = corner(offsets_ref, q)
        left, unused = spread(power, row)
        own[pl.ds(col, extent)] += left
        above = [
            jnp.max(jnp.where(lane == k * positions + q, line, 0.0)).astype(jnp.int32) for k in range(2)
        ]
        row = STEP * (q // PCOLS) + above[0]
        col = STEP * (q % PCOLS) + above[1]
        unused, right = spread(power, row)
        other[pl.ds(col, extent)] += right
    has_above = lax.axis_index("tile") > 0
    weight = own[...] + jnp.where(has_above, other[...], 0.0)
    inverse_ref[...] = 1.0 / (weight + 0.1 * largest + 1e-06)


def object_kernel(object_ref, upper_ref, received_ref, inverse_ref, new_ref, sent_ref):
    has_above = lax.axis_index("tile") > 0
    for part in range(2):
        received = received_ref[part].astype(jnp.float32)
        wave = upper_ref[part] + jnp.where(has_above, received, 0.0)
        value = object_ref[part, 0] + wave * inverse_ref[...]
        new_ref[part] = value
        sent_ref[part] = value.astype(jnp.bfloat16)


def spectral_kernel(basis_ref, analysis_ref, threshold_ref, own_ref, *refs, sources, sizes):
    others, out_ref = refs[:-1], refs[-1]
    parts, rows, unused = own_ref.shape
    components = threshold_ref.shape[0]
    zs, ms = sizes
    z = lax.axis_index("energy")
    m = lax.axis_index("mode")
    mine = z * ms + m
    labels = [(z ^ dz) * ms + (m ^ dm) for dz, dm in sources]
    chunk = 32
    per_part = rows // chunk

    def step(index, carry):
        part = index // per_part
        here = pl.ds(pl.multiple_of((index % per_part) * chunk, chunk), chunk)
        own = own_ref[part, here]
        values = [own] + [ref[part, here].astype(jnp.float32) for ref in others]
        projected = 0.5 * own
        for k in range(components):
            c = analysis_ref[k, mine] * values[0]
            for label, value in zip(labels, values[1:]):
                c += analysis_ref[k, label] * value
            t = threshold_ref[k]
            c = c - jnp.minimum(jnp.maximum(c, -t), t)
            projected += (0.5 * basis_ref[mine, k]) * c
        out_ref[part, 0, here] = projected
        return carry

    lax.fori_loop(0, parts * per_part, step, 0)


def probe_kernel(probe_ref, own_ref, received_ref, out_ref):
    modes = probe_ref.shape[1]
    density = own_ref[2 * modes].astype(jnp.float32) + received_ref[2 * modes].astype(jnp.float32)
    inverse = 1.0 / (density + 0.1 * jnp.max(density) + 1e-06)
    for part in range(2):
        for m in range(modes):
            k = part * modes + m
            numerator = own_ref[k].astype(jnp.float32) + received_ref[k].astype(jnp.float32)
            out_ref[part, m, 0] = probe_ref[part, m, 0] + (numerator * inverse).T


def call(kernel, inputs, scalars, outputs, scratch=(), limit=4, name=None):
    return pl.pallas_call(
        kernel,
        out_shape=outputs,
        in_specs=[SMEM] * scalars + [VMEM] * (len(inputs) - scalars),
        out_specs=jax.tree.map(lambda _: VMEM, outputs),
        scratch_shapes=list(scratch),
        compiler_params=pltpu.CompilerParams(vmem_limit_bytes=limit << 20),
        name=name,
    )(*inputs)


def body(object_field, probe_field, modulus, offsets, spectra_basis, analysis, threshold):
    extent = probe_field.shape[-1]
    modes = probe_field.shape[1]
    object_field = jnp.transpose(object_field, (0, 1, 3, 2))
    offsets = jnp.transpose(offsets)
    cols, rows = object_field.shape[2:]
    positions = offsets.shape[1]
    tiles = lax.axis_size("tile")
    zs = lax.axis_size("energy")
    ms = lax.axis_size("mode")
    forward, backward = dft_tables(extent)
    shape = jax.ShapeDtypeStruct
    f32, bf16 = jnp.float32, jnp.bfloat16

    message = call(
        round_kernel, (offsets, object_field), 1, shape((2, cols + PAD_ROWS, rows), bf16), name="round"
    )
    if tiles == 2:
        below = above = lax.ppermute(message, "tile", swap_pairs(2, 1))
    else:
        below = lax.ppermute(message, "tile", [(i + 1, i) for i in range(tiles - 1)])
        above = lax.ppermute(message, "tile", [(i, i + 1) for i in range(tiles - 1)])
    turned, moduli = call(
        turn_kernel,
        (probe_field, modulus),
        0,
        (shape((2, modes, extent, extent), f32), shape((positions, extent, extent), f32)),
        name="turn",
    )

    group = 2
    waves = group * modes
    upper, lower, share = call(
        functools.partial(wave_kernel, tiles=tiles, group=group),
        (offsets, message, below, turned, moduli, forward, backward),
        1,
        (
            shape((2, cols, rows), f32),
            shape((2, cols, rows), bf16),
            shape((2 * modes + 1, extent, extent), bf16),
        ),
        (
            pltpu.VMEM((2, 2, cols, LANES), f32),
            pltpu.VMEM((2, 2, cols, LANES), f32),
            pltpu.VMEM((group, 2, extent, extent), f32),
            pltpu.VMEM((2, waves * extent, extent), f32),
            pltpu.VMEM((waves * extent, 2 * extent), bf16),
            pltpu.VMEM((2 * extent, waves * extent), bf16),
            pltpu.VMEM((2, modes, extent, extent), f32),
            pltpu.VMEM((extent, extent), f32),
        ),
        limit=20,
        name="wave",
    )
    if tiles == 2:
        received = lax.ppermute(lower, "tile", swap_pairs(2, 1))
    else:
        received = lax.ppermute(lower, "tile", [(i, i + 1) for i in range(tiles - 1)])
    inverse = call(
        weight_kernel,
        (offsets, above, turned),
        1,
        shape((cols, rows), f32),
        (pltpu.VMEM((cols, LANES), f32), pltpu.VMEM((cols, LANES), f32)),
        name="weight",
    )
    object_new, sent = call(
        object_kernel,
        (object_field, upper, received, inverse),
        0,
        (shape((2, cols, rows), f32), shape((2, cols, rows), bf16)),
        name="object",
    )
    sources = []
    arrived = []
    for dz in range(zs):
        piece = sent if dz == 0 else lax.ppermute(sent, "energy", swap_pairs(zs, dz))
        for dm in range(ms):
            if dz == 0 and dm == 0:
                continue
            sources.append((dz, dm))
            arrived.append(piece if dm == 0 else lax.ppermute(piece, "mode", swap_pairs(ms, dm)))
    object_out = call(
        functools.partial(spectral_kernel, sources=tuple(sources), sizes=(zs, ms)),
        (spectra_basis, analysis, threshold, object_new, *arrived),
        3,
        shape(object_field.shape, f32),
        name="spectral",
    )
    for distance in [1 << k for k in range(1, tiles.bit_length() - 1)]:
        other = lax.ppermute(share, "tile", swap_pairs(tiles, distance))
        share = (share.astype(f32) + other.astype(f32)).astype(bf16)
    other = lax.ppermute(share, "tile", swap_pairs(tiles, 1))
    probe_out = call(
        probe_kernel, (probe_field, share, other), 0, shape(probe_field.shape, f32), name="probes"
    )
    return (jnp.transpose(object_out, (0, 1, 3, 2)), probe_out)


def solution(mesh):
    placed = (
        P(None, ("groups", "energy", "mode"), "tile", None),
        P(None, None, ("groups", "energy", "mode"), None, None),
        P(("groups", "energy", "mode"), "tile", None, None),
        P(("groups", "tile"), None),
        P(),
        P(),
        P(),
    )
    return jax.shard_map(
        body,
        mesh=mesh,
        in_specs=placed,
        out_specs=(
            P(None, ("groups", "energy", "mode"), "tile", None),
            P(None, None, ("groups", "energy", "mode"), None, None),
        ),
        check_vma=False,
    )
```

time: 52.9 us -> 35.9 us (0.68)
  Pallas kernels: 19.6 us -> 12.8 us
  local copies, waits for them, and re-layouts: 8.24 us -> 3.23 us
  waiting for transfers between devices: 13.4 us -> 8.73 us
  other arithmetic: 0.68 us -> 0 us
    pallas_call x6 -> x7, Pallas kernels: 19.6 us -> 12.8 us  [call(): pl.pallas_call(kernel, out_shape=outputs, in_specs=[SMEM] * scalars + [VM...]
    unnamed x23 -> x22, local copies, waits for them, and re-layouts: 7.57 us -> 3.23 us
    ppermute x3, waiting for transfers between devices: 8.18 us -> 5.02 us  [body(): lax.ppermute(sent, 'energy', swap_pairs(zs, dz))]
    ppermute x1, waiting for transfers between devices: 4.05 us -> 1.73 us  [body(): below = above = lax.ppermute(message, 'tile', swap_pairs(2, 1))]
    ppermute x1, waiting for transfers between devices: 1.12 us -> 1.98 us  [body(): received = lax.ppermute(lower, 'tile', swap_pairs(2, 1))]
    convert_element_type x1 -> x0, other arithmetic: 0.68 us -> none  [body(): above[0, rows, :2 * positions].astype(jnp.int32).reshape(positions, 2)]
    convert_element_type x1 -> x0, local copies, waits for them, and re-layouts: 0.68 us -> none  [body(): above[0, rows, :2 * positions].astype(jnp.int32).reshape(positions, 2)]
  transfers between devices with their start and end apart: 10 -> 10, of which waited for: 4 -> 4; matrix products, arithmetic and copies ran while one was open for 3% -> 0% of each run, Pallas kernels for 12% -> 8%
where the time goes in v1:
time: 35.9 us; the launch traced here: 35.7 us
  Pallas kernels  12.8 us (36%)
  starting transfers between devices  10.2 us (28%)
  waiting for transfers between devices  8.73 us (24%)
  local copies, waits for them, and re-layouts  3.23 us (9%)
  between operations  0.74 us (2%)
    pallas_call x7, Pallas kernels, call(): pl.pallas_call(kernel, out_shape=outputs, in_specs=[SMEM] * scalars + [VM...  12.8 us
    ppermute x3, waiting for transfers between devices, body(): lax.ppermute(sent, 'energy', swap_pairs(zs, dz))  5.02 us
    ppermute x3, starting transfers between devices, body(): lax.ppermute(sent, 'energy', swap_pairs(zs, dz))  4.56 us
    unnamed x22, local copies, waits for them, and re-layouts  3.23 us
    ppermute x1, starting transfers between devices, body(): below = above = lax.ppermute(message, 'tile', swap_pairs(2, 1))  3.03 us
    ppermute x1, waiting for transfers between devices, body(): received = lax.ppermute(lower, 'tile', swap_pairs(2, 1))  1.98 us
    ppermute x1, starting transfers between devices, body(): received = lax.ppermute(lower, 'tile', swap_pairs(2, 1))  1.79 us
    ppermute x1, waiting for transfers between devices, body(): below = above = lax.ppermute(message, 'tile', swap_pairs(2, 1))  1.73 us
  transfers between devices with their start and end apart: 10, of which 4 were waited for; matrix products, arithmetic and copies ran while one was open for 0% of the time, Pallas kernels for 8%

profile of v1, /device:TPU:0, one launch (start us, length us, event | category | flops | bytes accessed | tf_op | source)
XLA Modules:
  0.0 35.7 jit_solution(1282218079223538812)
XLA Ops:
  0.6 0.7 %copy-done.7 = s32[8,2]{0,1:T(2,128)S(1)} copy-done((s32[8,2]{0,1:T(2,128)S(1)}, s32[8,2]{0,1:T(2,128)}, u32[]{:S(2)}) %copy-start.7) | copy-done | bytes 88
  1.3 0.9 %copy-done.2 = f32[2,1,128,192]{2,3,1,0:T(8,128)S(1)} copy-done((f32[2,1,128,192]{2,3,1,0:T(8,128)S(1)}, f32[2,1,128,192]{2,3,1,0:T(8,128)}, u32[]{:S(2)}) %copy-start.2) | copy-done | bytes 196632
  2.2 0.6 %round.1.own_ref = bf16[2,208,128]{2,1,0:T(8,128)(2,1)S(1)} custom-call(s32[2,8]{1,0:T(2,128)S(1)} %bitcast.5, f32[2,1,192,128]{3,2,1,0:T(8,128)S(1)} %bitcast.3), custom_call_target="tpu_custom_call" | custom-call | tf_op jit(solution)/shard_map/round/pallas_call | solution.py:283
  2.8 3.0 %collective-permute-start = (bf16[2,208,128]{2,1,0:T(8,128)(2,1)S(1)}, bf16[2,208,128]{2,1,0:T(8,128)(2,1)S(1)}, u32[]{:S(2)}, u32[]{:S(2)}) collective-permute-start(bf16[2,208,128]{2,1,0:T(8,128)(2,1)S(1)} %round.1.own_ref), channel_id=1, source_target_pairs={{0,2},{2,0},{1,3},{3,1},{4,6},{6,4},{5,7},{7,5},{8,10},{10,8},{9,1... | collective-permute-start | bytes 319496 | tf_op jit(solution)/shard_map/ppermute | solution.py:312
  5.8 1.0 %copy-done = f32[2,3,1,128,128]{4,3,2,1,0:T(8,128)S(1)} copy-done((f32[2,3,1,128,128]{4,3,2,1,0:T(8,128)S(1)}, f32[2,3,1,128,128]{4,3,2,1,0:T(8,128)}, u32[]{:S(2)}) %copy-start) | copy-done | bytes 393240
  6.8 0.2 turn.1
  7.1 1.7 %collective-permute-done.below_ref.above_ref = bf16[2,208,128]{2,1,0:T(8,128)(2,1)S(1)} collective-permute-done((bf16[2,208,128]{2,1,0:T(8,128)(2,1)S(1)}, bf16[2,208,128]{2,1,0:T(8,128)(2,1)S(1)}, u32[]{:S(2)}, u32[]{:S(2)}) %collective-permute-start) | collective-permute-done | bytes 106528 | tf_op jit(solution)/shard_map/ppermute | solution.py:312
  8.8 6.3 %wave.1 = (f32[2,192,128]{2,1,0:T(8,128)S(1)}, bf16[2,192,128]{2,1,0:T(8,128)(2,1)S(1)}, bf16[7,128,128]{2,1,0:T(8,128)(2,1)S(1)}) custom-call(s32[2,8]{1,0:T(2,128)S(1)} %bitcast.6, bf16[2,208,128]{2,1,0:T(8,128)(2,1)S(1)} %round.1.own_ref, bf16[2,208,128]{2,1,0:T(8,128)(2,1)S(1)} %collective-permute-done.below_ref.above_ref, ...), custom_call_target="tpu_custom_call" | custom-call | tf_op jit(solution)/shard_map/wave/pallas_call | solution.py:283
  15.2 1.8 %collective-permute-start.1 = (bf16[2,192,128]{2,1,0:T(8,128)(2,1)S(1)}, bf16[2,192,128]{2,1,0:T(8,128)(2,1)S(1)}, u32[]{:S(2)}, u32[]{:S(2)}) collective-permute-start(bf16[2,192,128]{2,1,0:T(8,128)(2,1)S(1)} %get-tuple-element.12), channel_id=1, source_target_pairs={{0,2},{2,0},{1,3},{3,1},{4,6},{6,4},{5,7},{7,5},{8,10},{10,8},{9,1... | collective-permute-start | bytes 294920 | tf_op jit(solution)/shard_map/ppermute | solution.py:349
  16.9 0.3 collective-permute-start.9
  17.3 1.6 %weight.1.inverse_ref = f32[192,128]{1,0:T(8,128)S(1)} custom-call(s32[2,8]{1,0:T(2,128)S(1)} %bitcast.7, bf16[2,208,128]{2,1,0:T(8,128)(2,1)S(1)} %collective-permute-done.below_ref.above_ref, f32[2,3,128,128]{3,2,1,0:T(8,128)S(1)} %get-tuple-element.9.probe_ref), custom_call_target="tpu_custom_call" | custom-call | tf_op jit(solution)/shard_map/weight/pallas_call | solution.py:283
  18.9 0.0 copy-start.1
  18.9 2.0 %collective-permute-done.1.received_ref = bf16[2,192,128]{2,1,0:T(8,128)(2,1)S(1)} collective-permute-done((bf16[2,192,128]{2,1,0:T(8,128)(2,1)S(1)}, bf16[2,192,128]{2,1,0:T(8,128)(2,1)S(1)}, u32[]{:S(2)}, u32[]{:S(2)}) %collective-permute-start.1) | collective-permute-done | bytes 98336 | tf_op jit(solution)/shard_map/ppermute | solution.py:349
  20.9 0.1 object.1
  20.9 3.9 %collective-permute-start.7 = (bf16[2,192,128]{2,1,0:T(8,128)(2,1)S(1)}, bf16[2,192,128]{2,1,0:T(8,128)(2,1)S(1)}, u32[]{:S(2)}, u32[]{:S(2)}) collective-permute-start(bf16[2,192,128]{2,1,0:T(8,128)(2,1)S(1)} %get-tuple-element.14), channel_id=1, source_target_pairs={{0,12},{4,8},{8,4},{12,0},{1,13},{5,9},{9,5},{13,1},{2,14},{6,10},... | collective-permute-start | bytes 294920 | tf_op jit(solution)/shard_map/ppermute | solution.py:370
  24.9 0.6 %collective-permute-start.3 = (bf16[2,192,128]{2,1,0:T(8,128)(2,1)S(1)}, bf16[2,192,128]{2,1,0:T(8,128)(2,1)S(1)}, u32[]{:S(2)}, u32[]{:S(2)}) collective-permute-start(bf16[2,192,128]{2,1,0:T(8,128)(2,1)S(1)} %get-tuple-element.14), channel_id=1, source_target_pairs={{0,4},{4,0},{8,12},{12,8},{1,5},{5,1},{9,13},{13,9},{2,6},{6,2},{1... | collective-permute-start | bytes 294920 | tf_op jit(solution)/shard_map/ppermute | solution.py:370
  25.5 2.6 %collective-permute-done.7.refs_5_ = bf16[2,192,128]{2,1,0:T(8,128)(2,1)S(1)} collective-permute-done((bf16[2,192,128]{2,1,0:T(8,128)(2,1)S(1)}, bf16[2,192,128]{2,1,0:T(8,128)(2,1)S(1)}, u32[]{:S(2)}, u32[]{:S(2)}) %collective-permute-start.7) | collective-permute-done | bytes 98336 | tf_op jit(solution)/shard_map/ppermute | solution.py:370
  28.1 2.4 %collective-permute-done.5.refs_3_ = bf16[2,192,128]{2,1,0:T(8,128)(2,1)S(1)} collective-permute-done((bf16[2,192,128]{2,1,0:T(8,128)(2,1)S(1)}, bf16[2,192,128]{2,1,0:T(8,128)(2,1)S(1)}, u32[]{:S(2)}, u32[]{:S(2)}) %collective-permute-start.5) | collective-permute-done | bytes 98336 | tf_op jit(solution)/shard_map/ppermute | solution.py:370
  30.5 0.0 collective-permute-start.6
  30.5 0.0 collective-permute-done.3.refs_1_
  30.5 0.5 %collective-permute-start.4 = (bf16[2,192,128]{2,1,0:T(8,128)(2,1)S(1)}, bf16[2,192,128]{2,1,0:T(8,128)(2,1)S(1)}, u32[]{:S(2)}, u32[]{:S(2)}) collective-permute-start(bf16[2,192,128]{2,1,0:T(8,128)(2,1)S(1)} %collective-permute-done.3.refs_1_), channel_id=1, source_target_pairs={{0,1},{1,0},{2,3},{3,2},{4,5},{5,4},{6,7},{7,6},{8,9},{9,8},{10,11... | collective-permute-start | bytes 294920 | tf_op jit(solution)/shard_map/ppermute | solution.py:375
  31.1 1.1 %probes.1 = f32[2,3,1,128,128]{4,3,2,1,0:T(8,128)} custom-call(f32[2,3,1,128,128]{4,3,2,1,0:T(8,128)S(1)} %copy-done.1, bf16[7,128,128]{2,1,0:T(8,128)(2,1)S(1)} %get-tuple-element.15.own_ref, bf16[7,128,128]{2,1,0:T(8,128)(2,1)S(1)} %collective-permute-done.9.received_ref), custom_call_target="tpu_custom_call" | custom-call | tf_op jit(solution)/shard_map/probes/pallas_call | solution.py:283
  32.2 0.6 %copy-done.10 = f32[8]{0:T(128)S(1)} copy-done((f32[8]{0:T(128)S(1)}, f32[8]{0:T(128)}, u32[]{:S(2)}) %copy-start.10) | copy-done | bytes 56
  32.8 2.9 %spectral.1 = f32[2,1,192,128]{3,2,1,0:T(8,128)} custom-call(f32[8,8]{1,0:T(8,128)S(1)} %copy-done.8, f32[8,8]{1,0:T(8,128)S(1)} %copy-done.9, f32[8]{0:T(128)S(1)} %copy-done.10, f32[2,192,128]{2,1,0:T(8,128)S(1)} %get-tuple-element.13.own_ref, bf16[2,192,128]{2,1,0:T(8,128)(2,1)S(1)} %collective-permute-done.2.refs_0_, ...), custom_call_target="tpu_custom_call" | custom-call | tf_op jit(solution)/shard_map/spectral/pallas_call | solution.py:283
  (25 shorter events, 0.1 us)
Async XLA Ops:
  0.6 0.7 %copy-start.7 = (s32[8,2]{0,1:T(2,128)S(1)}, s32[8,2]{0,1:T(2,128)}, u32[]{:S(2)}) copy-start(s32[8,2]{0,1:T(2,128)} %param.12) | copy-start | bytes 196
  1.3 0.9 %copy-start.2 = (f32[2,1,128,192]{2,3,1,0:T(8,128)S(1)}, f32[2,1,128,192]{2,3,1,0:T(8,128)}, u32[]{:S(2)}) copy-start(f32[2,1,128,192]{2,3,1,0:T(8,128)} %param.9) | copy-start | bytes 589828
  2.2 3.6 %copy-start.4 = (bf16[1,8,128,128]{3,2,1,0:T(8,128)(2,1)S(1)}, bf16[1,8,128,128]{3,2,1,0:T(8,128)(2,1)}, u32[]{:S(2)}) copy-start(bf16[1,8,128,128]{3,2,1,0:T(8,128)(2,1)} %moduli_ref.1) | copy-start | bytes 786436
  2.8 6.0 %collective-permute-start = (bf16[2,208,128]{2,1,0:T(8,128)(2,1)S(1)}, bf16[2,208,128]{2,1,0:T(8,128)(2,1)S(1)}, u32[]{:S(2)}, u32[]{:S(2)}) collective-permute-start(bf16[2,208,128]{2,1,0:T(8,128)(2,1)S(1)} %round.1.own_ref), channel_id=1, source_target_pairs={{0,2},{2,0},{1,3},{3,1},{4,6},{6,4},{5,7},{7,5},{8,10},{10,8},{9,1... | collective-permute-start | bytes 319496 | tf_op jit(solution)/shard_map/ppermute | solution.py:312
  5.8 1.0 %copy-start = (f32[2,3,1,128,128]{4,3,2,1,0:T(8,128)S(1)}, f32[2,3,1,128,128]{4,3,2,1,0:T(8,128)}, u32[]{:S(2)}) copy-start(f32[2,3,1,128,128]{4,3,2,1,0:T(8,128)} %probe_ref.3) | copy-start | bytes 1179652
  6.8 2.0 %copy-start.5 = (bf16[256,256]{1,0:T(8,128)(2,1)S(1)}, bf16[256,256]{1,0:T(8,128)(2,1)}, u32[]{:S(2)}) copy-start(bf16[256,256]{1,0:T(8,128)(2,1)} %constant.5.clone.backward_ref) | copy-start | bytes 393220
  6.8 2.0 %copy-start.6 = (bf16[256,256]{1,0:T(8,128)(2,1)S(1)}, bf16[256,256]{1,0:T(8,128)(2,1)}, u32[]{:S(2)}) copy-start(bf16[256,256]{1,0:T(8,128)(2,1)} %constant.4.clone.forward_ref) | copy-start | bytes 393220
  15.2 5.7 %collective-permute-start.1 = (bf16[2,192,128]{2,1,0:T(8,128)(2,1)S(1)}, bf16[2,192,128]{2,1,0:T(8,128)(2,1)S(1)}, u32[]{:S(2)}, u32[]{:S(2)}) collective-permute-start(bf16[2,192,128]{2,1,0:T(8,128)(2,1)S(1)} %get-tuple-element.12), channel_id=1, source_target_pairs={{0,2},{2,0},{1,3},{3,1},{4,6},{6,4},{5,7},{7,5},{8,10},{10,8},{9,1... | collective-permute-start | bytes 294920 | tf_op jit(solution)/shard_map/ppermute | solution.py:349
  16.9 3.9 %copy-start.3 = (f32[2,1,128,192]{2,3,1,0:T(8,128)S(1)}, f32[2,1,128,192]{2,3,1,0:T(8,128)}, u32[]{:S(2)}) copy-start(f32[2,1,128,192]{2,3,1,0:T(8,128)} %param.9) | copy-start | bytes 589828
  16.9 14.1 %collective-permute-start.9 = (bf16[7,128,128]{2,1,0:T(8,128)(2,1)S(1)}, bf16[7,128,128]{2,1,0:T(8,128)(2,1)S(1)}, u32[]{:S(2)}, u32[]{:S(2)}) collective-permute-start(bf16[7,128,128]{2,1,0:T(8,128)(2,1)S(1)} %get-tuple-element.15.own_ref), channel_id=1, source_target_pairs={{0,2},{2,0},{1,3},{3,1},{4,6},{6,4},{5,7},{7,5},{8,10},{10,8},{9,1... | collective-permute-start | bytes 688136 | tf_op jit(solution)/shard_map/ppermute | solution.py:386
  18.9 12.1 %copy-start.1 = (f32[2,3,1,128,128]{4,3,2,1,0:T(8,128)S(1)}, f32[2,3,1,128,128]{4,3,2,1,0:T(8,128)}, u32[]{:S(2)}) copy-start(f32[2,3,1,128,128]{4,3,2,1,0:T(8,128)} %probe_ref.3) | copy-start | bytes 1179652
  20.9 7.2 %collective-permute-start.7 = (bf16[2,192,128]{2,1,0:T(8,128)(2,1)S(1)}, bf16[2,192,128]{2,1,0:T(8,128)(2,1)S(1)}, u32[]{:S(2)}, u32[]{:S(2)}) collective-permute-start(bf16[2,192,128]{2,1,0:T(8,128)(2,1)S(1)} %get-tuple-element.14), channel_id=1, source_target_pairs={{0,12},{4,8},{8,4},{12,0},{1,13},{5,9},{9,5},{13,1},{2,14},{6,10},... | collective-permute-start | bytes 294920 | tf_op jit(solution)/shard_map/ppermute | solution.py:370
  24.9 5.7 %collective-permute-start.5 = (bf16[2,192,128]{2,1,0:T(8,128)(2,1)S(1)}, bf16[2,192,128]{2,1,0:T(8,128)(2,1)S(1)}, u32[]{:S(2)}, u32[]{:S(2)}) collective-permute-start(bf16[2,192,128]{2,1,0:T(8,128)(2,1)S(1)} %get-tuple-element.14), channel_id=1, source_target_pairs={{0,8},{4,12},{8,0},{12,4},{1,9},{5,13},{9,1},{13,5},{2,10},{6,14},... | collective-permute-start | bytes 294920 | tf_op jit(solution)/shard_map/ppermute | solution.py:370
  24.9 5.7 %collective-permute-start.3 = (bf16[2,192,128]{2,1,0:T(8,128)(2,1)S(1)}, bf16[2,192,128]{2,1,0:T(8,128)(2,1)S(1)}, u32[]{:S(2)}, u32[]{:S(2)}) collective-permute-start(bf16[2,192,128]{2,1,0:T(8,128)(2,1)S(1)} %get-tuple-element.14), channel_id=1, source_target_pairs={{0,4},{4,0},{8,12},{12,8},{1,5},{5,1},{9,13},{13,9},{2,6},{6,2},{1... | collective-permute-start | bytes 294920 | tf_op jit(solution)/shard_map/ppermute | solution.py:370
  25.5 6.6 %collective-permute-start.2 = (bf16[2,192,128]{2,1,0:T(8,128)(2,1)S(1)}, bf16[2,192,128]{2,1,0:T(8,128)(2,1)S(1)}, u32[]{:S(2)}, u32[]{:S(2)}) collective-permute-start(bf16[2,192,128]{2,1,0:T(8,128)(2,1)S(1)} %get-tuple-element.14), channel_id=1, source_target_pairs={{0,1},{1,0},{2,3},{3,2},{4,5},{5,4},{6,7},{7,6},{8,9},{9,8},{10,11... | collective-permute-start | bytes 294920 | tf_op jit(solution)/shard_map/ppermute | solution.py:375
  28.1 4.0 %collective-permute-start.8 = (bf16[2,192,128]{2,1,0:T(8,128)(2,1)S(1)}, bf16[2,192,128]{2,1,0:T(8,128)(2,1)S(1)}, u32[]{:S(2)}, u32[]{:S(2)}) collective-permute-start(bf16[2,192,128]{2,1,0:T(8,128)(2,1)S(1)} %collective-permute-done.7.refs_5_), channel_id=1, source_target_pairs={{0,1},{1,0},{2,3},{3,2},{4,5},{5,4},{6,7},{7,6},{8,9},{9,8},{10,11... | collective-permute-start | bytes 294920 | tf_op jit(solution)/shard_map/ppermute | solution.py:375
  30.5 1.6 %collective-permute-start.6 = (bf16[2,192,128]{2,1,0:T(8,128)(2,1)S(1)}, bf16[2,192,128]{2,1,0:T(8,128)(2,1)S(1)}, u32[]{:S(2)}, u32[]{:S(2)}) collective-permute-start(bf16[2,192,128]{2,1,0:T(8,128)(2,1)S(1)} %collective-permute-done.5.refs_3_), channel_id=1, source_target_pairs={{0,1},{1,0},{2,3},{3,2},{4,5},{5,4},{6,7},{7,6},{8,9},{9,8},{10,11... | collective-permute-start | bytes 294920 | tf_op jit(solution)/shard_map/ppermute | solution.py:375
  30.5 1.6 %collective-permute-start.4 = (bf16[2,192,128]{2,1,0:T(8,128)(2,1)S(1)}, bf16[2,192,128]{2,1,0:T(8,128)(2,1)S(1)}, u32[]{:S(2)}, u32[]{:S(2)}) collective-permute-start(bf16[2,192,128]{2,1,0:T(8,128)(2,1)S(1)} %collective-permute-done.3.refs_1_), channel_id=1, source_target_pairs={{0,1},{1,0},{2,3},{3,2},{4,5},{5,4},{6,7},{7,6},{8,9},{9,8},{10,11... | collective-permute-start | bytes 294920 | tf_op jit(solution)/shard_map/ppermute | solution.py:375
  31.0 1.1 %copy-start.8 = (f32[8,8]{1,0:T(8,128)S(1)}, f32[8,8]{1,0:T(8,128)}, u32[]{:S(2)}) copy-start(f32[8,8]{1,0:T(8,128)} %basis_ref.1) | copy-start | bytes 772
  31.0 1.1 %copy-start.9 = (f32[8,8]{1,0:T(8,128)S(1)}, f32[8,8]{1,0:T(8,128)}, u32[]{:S(2)}) copy-start(f32[8,8]{1,0:T(8,128)} %analysis_ref.1) | copy-start | bytes 772
  32.1 0.7 %copy-start.10 = (f32[8]{0:T(128)S(1)}, f32[8]{0:T(128)}, u32[]{:S(2)}) copy-start(f32[8]{0:T(128)} %threshold_ref.1) | copy-start | bytes 100

commit v2 on v1

v2 whole, which is shorter than its diff:
```python
import functools
import math

import jax
import jax.numpy as jnp
import ml_dtypes
import numpy as np
from jax import lax
from jax.experimental import pallas as pl
from jax.experimental.pallas import tpu as pltpu
from jax.sharding import PartitionSpec as P

PCOLS = 2
STEP = 32
LANES = 128
PAD_ROWS = 16


def swap_pairs(size, distance):
    return [(i, i ^ distance) for i in range(size)]


def dft_tables(extent):
    counter = np.arange(extent)
    phases = -2.0 * math.pi / extent * (counter[:, None] * counter[None, :] % extent)
    cosine = np.cos(phases) / math.sqrt(extent)
    sine = np.sin(phases) / math.sqrt(extent)
    forward = np.block([[cosine, -sine], [sine, cosine]])
    backward = np.block([[cosine, sine], [-sine, cosine]])
    return (
        jnp.asarray(forward.astype(np.float32).astype(ml_dtypes.bfloat16)),
        jnp.asarray(backward.astype(np.float32).astype(ml_dtypes.bfloat16)),
    )


def corner(offsets, q):
    row = STEP * (q // PCOLS) + offsets[0, q]
    col = STEP * (q % PCOLS) + offsets[1, q]
    return row, col


def spread(block, row):
    lane = lax.broadcasted_iota(jnp.int32, block.shape, 1)
    turned = pltpu.roll(block, row, 1)
    left = jnp.where(lane >= row, turned, 0.0)
    right = jnp.where(lane < row, turned, 0.0)
    return left, right


def round_kernel(offsets_hbm, object_hbm, message_ref, object_ref, offsets_ref, sems):
    cols, rows = object_ref.shape[1:]
    positions = offsets_ref.shape[1]
    copies = [pltpu.make_async_copy(offsets_hbm, offsets_ref, sems.at[2])]
    copies += [
        pltpu.make_async_copy(object_hbm.at[part, 0], object_ref.at[part], sems.at[part])
        for part in range(2)
    ]
    for copy in copies:
        copy.start()
    copies[0].wait()
    lane = lax.broadcasted_iota(jnp.int32, (PAD_ROWS, rows), 1)
    line = jnp.zeros((PAD_ROWS, rows), jnp.float32)
    for k in range(2):
        for q in range(positions):
            value = offsets_ref[k, q].astype(jnp.float32)
            line = jnp.where(lane == k * positions + q, value, line)
    for part in range(2):
        copies[1 + part].wait()
        message_ref[part, :cols] = object_ref[part].astype(jnp.bfloat16)
        message_ref[part, cols:] = line.astype(jnp.bfloat16)


def turn_kernel(
    offsets_hbm,
    analysis_hbm,
    basis_hbm,
    threshold_hbm,
    forward_hbm,
    backward_hbm,
    probe_hbm,
    moduli_hbm,
    offsets_out_ref,
    forward_ref,
    backward_ref,
    turned_ref,
    moduli_out_ref,
    power_ref,
    weight_ref,
    analysis_table_ref,
    last_table_ref,
    offsets_ref,
    analysis_ref,
    basis_ref,
    threshold_ref,
    probe_ref,
    moduli_ref,
    sems,
    *,
    sources,
    sizes,
):
    modes = probe_ref.shape[1]
    extent = probe_ref.shape[-1]
    positions = offsets_ref.shape[1]
    pairs = [
        (offsets_hbm, offsets_ref),
        (probe_hbm, probe_ref),
        (moduli_hbm, moduli_ref),
        (analysis_hbm, analysis_ref),
        (basis_hbm, basis_ref),
        (threshold_hbm, threshold_ref),
        (forward_hbm, forward_ref),
        (backward_hbm, backward_ref),
        (offsets_hbm, offsets_out_ref),
    ]
    copies = [
        pltpu.make_async_copy(source, target, sems.at[k])
        for k, (source, target) in enumerate(pairs)
    ]
    for copy in copies:
        copy.start()
    for copy in copies[3:6]:
        copy.wait()
    _, ms = sizes
    z = lax.axis_index("energy")
    m = lax.axis_index("mode")
    tile = analysis_table_ref.shape[2:]
    for k in range(threshold_ref.shape[0]):
        for number, (dz, dm) in enumerate(sources):
            label = (z ^ dz) * ms + (m ^ dm)
            analysis_table_ref[number, k] = jnp.full(tile, analysis_ref[k, label])
        last_table_ref[0, k] = jnp.full(tile, 0.5 * basis_ref[z * ms + m, k])
        last_table_ref[1, k] = jnp.full(tile, threshold_ref[k])
    copies[0].wait()
    copies[1].wait()
    power = jnp.zeros((extent, extent), jnp.float32)
    for part in range(2):
        for m in range(modes):
            value = probe_ref[part, m, 0].T
            turned_ref[part, m] = value
            power += value * value
    power_ref[...] = power
    weight_ref[...] = jnp.full_like(weight_ref, 0.1 * jnp.max(power) + 1e-06)
    for q in range(positions):
        row, col = corner(offsets_ref, q)
        left, _ = spread(power, row)
        weight_ref[pl.ds(col, extent)] += left
    copies[2].wait()
    for q in range(positions):
        moduli_out_ref[q] = moduli_ref[0, q].astype(jnp.float32).T
    for copy in copies[6:]:
        copy.wait()


def cut(extended, offsets_ref, q, extent):
    row, col = corner(offsets_ref, q)
    here = pl.ds(col, extent)
    lane = lax.broadcasted_iota(jnp.int32, (extent, extent), 1)
    found = []
    for part in range(2):
        left = pltpu.roll(extended[part, 0, here], extent - row, 1)
        right = pltpu.roll(extended[part, 1, here], extent - row, 1)
        found.append(jnp.where(lane < extent - row, left, right))
    return found


def extend(extended, own_ref, below_ref, tiles):
    cols = extended.shape[2]
    has_below = lax.axis_index("tile") < tiles - 1
    for part in range(2):
        extended[part, 0] = own_ref[part, :cols].astype(jnp.float32)
        below = below_ref[part, :cols].astype(jnp.float32)
        extended[part, 1] = jnp.where(has_below, below, 0.0)


def side_by_side(blocks):
    return jnp.concatenate(blocks, axis=1)


def stack_up(blocks):
    return jnp.concatenate(blocks, axis=0)


def wave_kernel(
    offsets_ref,
    own_ref,
    below_ref,
    probe_ref,
    moduli_ref,
    forward_ref,
    backward_ref,
    upper_ref,
    lower_ref,
    change_ref,
    extended,
    total,
    *,
    tiles,
    group,
):
    extent = probe_ref.shape[-1]
    modes = probe_ref.shape[1]
    positions = offsets_ref.shape[1]
    waves = group * modes
    extend(extended, own_ref, below_ref, tiles)
    total[...] = jnp.zeros_like(total)
    low = slice(0, extent)
    high = slice(extent, 2 * extent)

    def dot(left, right):
        return jnp.dot(left, right, preferred_element_type=jnp.float32)

    def span(w):
        return slice(w * extent, (w + 1) * extent)

    for block in range(positions // group):
        rounded = []
        for member in range(group):
            q = block * group + member
            object_real, object_imag = cut(extended, offsets_ref, q, extent)
            for m in range(modes):
                probe_real = probe_ref[0, m]
                probe_imag = probe_ref[1, m]
                wave_real = probe_real * object_real - probe_imag * object_imag
                wave_imag = probe_real * object_imag + probe_imag * object_real
                change_ref[q, m, 0] = wave_real
                change_ref[q, m, 1] = wave_imag
                rounded.append(side_by_side([wave_real, wave_imag]).astype(jnp.bfloat16))
        halfway = dot(stack_up(rounded), backward_ref[...]).astype(jnp.bfloat16)
        standing = side_by_side(
            [stack_up([halfway[span(w), low], halfway[span(w), high]]) for w in range(waves)]
        )
        spectrum = dot(forward_ref[...], standing)
        scaled = []
        for member in range(group):
            q = block * group + member
            magnitude = jnp.full((extent, extent), 0.01, jnp.float32)
            for m in range(modes):
                place = span(member * modes + m)
                real = spectrum[low, place]
                imag = spectrum[high, place]
                magnitude += real * real + imag * imag
            factor = moduli_ref[q] * lax.rsqrt(magnitude)
            for m in range(modes):
                place = span(member * modes + m)
                scaled.append(
                    stack_up([spectrum[low, place] * factor, spectrum[high, place] * factor]).astype(
                        jnp.bfloat16
                    )
                )
        returned = dot(backward_ref[...], side_by_side(scaled)).astype(jnp.bfloat16)
        lying = stack_up(
            [side_by_side([returned[low, span(w)], returned[high, span(w)]]) for w in range(waves)]
        )
        new_wave = dot(lying, forward_ref[...])
        for member in range(group):
            q = block * group + member
            row, col = corner(offsets_ref, q)
            here = pl.ds(col, extent)
            sum_real = jnp.zeros((extent, extent), jnp.float32)
            sum_imag = jnp.zeros((extent, extent), jnp.float32)
            for m in range(modes):
                place = span(member * modes + m)
                change_real = new_wave[place, low] - change_ref[q, m, 0]
                change_imag = new_wave[place, high] - change_ref[q, m, 1]
                change_ref[q, m, 0] = change_real
                change_ref[q, m, 1] = change_imag
                probe_real = probe_ref[0, m]
                probe_imag = probe_ref[1, m]
                sum_real += probe_real * change_real + probe_imag * change_imag
                sum_imag += probe_real * change_imag - probe_imag * change_real
            for part, value in enumerate((sum_real, sum_imag)):
                for side, moved in enumerate(spread(value, row)):
                    total[part, side, here] += moved

    for part in range(2):
        upper_ref[part] = total[part, 0]
        lower_ref[part] = total[part, 1].astype(jnp.bfloat16)


def share_kernel(
    offsets_ref, own_ref, below_ref, change_ref, share_ref, extended, window, *, tiles
):
    extent = change_ref.shape[-1]
    positions, modes = change_ref.shape[:2]
    extend(extended, own_ref, below_ref, tiles)
    density = jnp.zeros((extent, extent), jnp.float32)
    for q in range(positions):
        object_real, object_imag = cut(extended, offsets_ref, q, extent)
        window[q, 0] = object_real
        window[q, 1] = object_imag
        density += object_real * object_real + object_imag * object_imag
    share_ref[2 * modes] = density.astype(jnp.bfloat16)
    chunk = 16

    def step(index, carry):
        here = pl.ds(pl.multiple_of(index * chunk, chunk), chunk)
        for m in range(modes):
            sum_real = jnp.zeros((chunk, extent), jnp.float32)
            sum_imag = jnp.zeros((chunk, extent), jnp.float32)
            for q in range(positions):
                object_real = window[q, 0, here]
                object_imag = window[q, 1, here]
                change_real = change_ref[q, m, 0, here]
                change_imag = change_ref[q, m, 1, here]
                sum_real += object_real * change_real + object_imag * change_imag
                sum_imag += object_real * change_imag - object_imag * change_real
            share_ref[m, here] = sum_real.astype(jnp.bfloat16)
            share_ref[modes + m, here] = sum_imag.astype(jnp.bfloat16)
        return carry

    lax.fori_loop(0, extent // chunk, step, 0)


def weight_kernel(above_ref, power_ref, weight_ref, inverse_ref, other, *, positions):
    extent = power_ref.shape[-1]
    cols = inverse_ref.shape[0]
    power = power_ref[...]
    other[...] = jnp.zeros_like(other)
    line = above_ref[0, cols : cols + PAD_ROWS].astype(jnp.float32)[:8]
    lane = lax.broadcasted_iota(jnp.int32, line.shape, 1)
    for q in range(positions):
        above = [
            jnp.max(jnp.where(lane == k * positions + q, line, 0.0)).astype(jnp.int32) for k in range(2)
        ]
        row = STEP * (q // PCOLS) + above[0]
        col = STEP * (q % PCOLS) + above[1]
        _, right = spread(power, row)
        other[pl.ds(col, extent)] += right
    has_above = lax.axis_index("tile") > 0
    inverse_ref[...] = 1.0 / (weight_ref[...] + jnp.where(has_above, other[...], 0.0))


def object_kernel(object_ref, upper_ref, received_ref, inverse_ref, new_ref, sent_ref):
    has_above = lax.axis_index("tile") > 0
    for part in range(2):
        received = received_ref[part].astype(jnp.float32)
        wave = upper_ref[part] + jnp.where(has_above, received, 0.0)
        value = object_ref[part] + wave * inverse_ref[...]
        new_ref[part] = value
        sent_ref[part] = value.astype(jnp.bfloat16)


def mix_kernel(table_ref, *refs, first, chained, chunk):
    mixed_ref = refs[-1]
    refs = refs[:-1]
    before, refs = (refs[0], refs[1:]) if chained else (None, refs)
    components, parts, rows, lanes = mixed_ref.shape
    per_part = rows // chunk
    height = table_ref.shape[2]

    def step(index, carry):
        part = index // per_part
        here = pl.ds(pl.multiple_of((index % per_part) * chunk, chunk), chunk)
        folded = (chunk // height, height, lanes)
        values = [ref[part, here].astype(jnp.float32).reshape(folded) for ref in refs]
        for k in range(components):
            terms = [table_ref[first + n, k] * value for n, value in enumerate(values)]
            if before is not None:
                terms.insert(0, before[k, part, here].reshape(folded))
            mixed_ref[k, part, here] = functools.reduce(jnp.add, terms).reshape(chunk, lanes)
        return carry

    lax.fori_loop(0, parts * per_part, step, 0)


def spectral_kernel(table_ref, last_ref, own_ref, mixed_ref, *refs, first, chunk):
    refs, out_ref = refs[:-1], refs[-1]
    parts, rows, lanes = own_ref.shape
    components = last_ref.shape[1]
    per_part = rows // chunk
    height = table_ref.shape[2]

    def step(index, carry):
        part = index // per_part
        here = pl.ds(pl.multiple_of((index % per_part) * chunk, chunk), chunk)
        folded = (chunk // height, height, lanes)
        values = [ref[part, here].astype(jnp.float32).reshape(folded) for ref in refs]
        terms = [0.5 * own_ref[part, here].reshape(folded)]
        for k in range(components):
            c = mixed_ref[k, part, here].reshape(folded)
            for n, value in enumerate(values):
                c += table_ref[first + n, k] * value
            t = last_ref[1, k]
            c = c - jnp.minimum(jnp.maximum(c, -t), t)
            terms.append(last_ref[0, k] * c)
        while len(terms) > 1:
            terms = [sum(terms[k : k + 2][1:], terms[k]) for k in range(0, len(terms), 2)]
        out_ref[part, 0, here] = terms[0].reshape(chunk, lanes)
        return carry

    lax.fori_loop(0, parts * per_part, step, 0)


def probe_kernel(probe_ref, own_ref, received_ref, out_ref):
    modes = probe_ref.shape[1]
    density = own_ref[2 * modes].astype(jnp.float32) + received_ref[2 * modes].astype(jnp.float32)
    inverse = 1.0 / (density + 0.1 * jnp.max(density) + 1e-06)
    for part in range(2):
        for m in range(modes):
            k = part * modes + m
            numerator = own_ref[k].astype(jnp.float32) + received_ref[k].astype(jnp.float32)
            out_ref[part, m, 0] = (probe_ref[part, m] + numerator * inverse).T


def call(kernel, inputs, places, outputs, scratch=(), limit=4):
    inputs = [
        pltpu.with_memory_space_constraint(x, pltpu.HBM) if p == "h" else x
        for x, p in zip(inputs, places)
    ]
    kinds = {"s": pltpu.SMEM, "v": pltpu.VMEM, "h": pltpu.HBM}
    return pl.pallas_call(
        kernel,
        out_shape=outputs,
        in_specs=[pl.BlockSpec(memory_space=kinds[p]) for p in places],
        out_specs=jax.tree.map(lambda _: pl.BlockSpec(memory_space=pltpu.VMEM), outputs),
        scratch_shapes=list(scratch),
        compiler_params=pltpu.CompilerParams(vmem_limit_bytes=limit << 20),
    )(*inputs)


def body(object_field, probe_field, modulus, offsets, spectra_basis, analysis, threshold):
    extent = probe_field.shape[-1]
    modes = probe_field.shape[1]
    object_field = jnp.transpose(object_field, (0, 1, 3, 2))
    offsets = jnp.transpose(offsets)
    cols, rows = object_field.shape[2:]
    positions = offsets.shape[1]
    tiles = lax.axis_size("tile")
    zs = lax.axis_size("energy")
    ms = lax.axis_size("mode")
    forward, backward = dft_tables(extent)
    shape = jax.ShapeDtypeStruct
    f32, bf16 = jnp.float32, jnp.bfloat16

    message, object_here = call(
        round_kernel,
        (offsets, object_field),
        "hh",
        (shape((2, cols + PAD_ROWS, rows), bf16), shape((2, cols, rows), f32)),
        (pltpu.SMEM((2, positions), jnp.int32), pltpu.SemaphoreType.DMA((3,))),
    )
    if tiles == 2:
        below = above = lax.ppermute(message, "tile", swap_pairs(2, 1))
    else:
        below = lax.ppermute(message, "tile", [(i + 1, i) for i in range(tiles - 1)])
        above = lax.ppermute(message, "tile", [(i, i + 1) for i in range(tiles - 1)])

    far = zs // 2
    stages = [
        [(dz, dm) for dz in (0, 1) for dm in range(ms)],
        [(dz, dm) for dz in range(2, zs) for dm in range(ms) if dz != far] + [(far, 0)],
        [(far, dm) for dm in range(1, ms)],
    ]
    sources = sum(stages, [])
    components = threshold.shape[0]
    offsets, forward, backward, turned, moduli, power, weight, table, last_table = call(
        functools.partial(turn_kernel, sources=tuple(sources), sizes=(zs, ms)),
        (offsets, analysis, spectra_basis, threshold, forward, backward, probe_field, modulus),
        "hhhhhhhh",
        (
            shape((2, positions), jnp.int32),
            shape(forward.shape, bf16),
            shape(backward.shape, bf16),
            shape((2, modes, extent, extent), f32),
            shape((positions, extent, extent), f32),
            shape((extent, extent), f32),
            shape((cols, rows), f32),
            shape((len(sources), components, 8, LANES), f32),
            shape((2, components, 8, LANES), f32),
        ),
        (
            pltpu.SMEM((2, positions), jnp.int32),
            pltpu.SMEM(analysis.shape, f32),
            pltpu.SMEM(spectra_basis.shape, f32),
            pltpu.SMEM(threshold.shape, f32),
            pltpu.VMEM(probe_field.shape, f32),
            pltpu.VMEM(modulus.shape, bf16),
            pltpu.SemaphoreType.DMA((9,)),
        ),
        limit=8,
    )
    upper, lower, change = call(
        functools.partial(wave_kernel, tiles=tiles, group=2),
        (offsets, message, below, turned, moduli, forward, backward),
        "svvvvvv",
        (
            shape((2, cols, rows), f32),
            shape((2, cols, rows), bf16),
            shape((positions, modes, 2, extent, extent), f32),
        ),
        (
            pltpu.VMEM((2, 2, cols, LANES), f32),
            pltpu.VMEM((2, 2, cols, LANES), f32),
        ),
        limit=24,
    )
    if tiles == 2:
        received = lax.ppermute(lower, "tile", swap_pairs(2, 1))
    else:
        received = lax.ppermute(lower, "tile", [(i, i + 1) for i in range(tiles - 1)])
    inverse = call(
        functools.partial(weight_kernel, positions=positions),
        (above, power, weight),
        "vvv",
        shape((cols, rows), f32),
        (pltpu.VMEM((cols, rows), f32),),
    )
    share = call(
        functools.partial(share_kernel, tiles=tiles),
        (offsets, message, below, change),
        "svvv",
        shape((2 * modes + 1, extent, extent), bf16),
        (
            pltpu.VMEM((2, 2, cols, LANES), f32),
            pltpu.VMEM((positions, 2, extent, extent), f32),
        ),
        limit=8,
    )
    object_new, sent = call(
        object_kernel,
        (object_here, upper, received, inverse),
        "vvvv",
        (shape((2, cols, rows), f32), shape((2, cols, rows), bf16)),
    )
    pieces = {(0, 0): sent}
    for dz in range(1, zs):
        pieces[dz, 0] = lax.ppermute(sent, "energy", swap_pairs(zs, dz))
    for dz in range(zs):
        for dm in range(1, ms):
            pieces[dz, dm] = lax.ppermute(pieces[dz, 0], "mode", swap_pairs(ms, dm))
    mixed = None
    first = 0
    for stage in stages[:2]:
        inputs = [table] + ([] if mixed is None else [mixed]) + [pieces[s] for s in stage]
        mixed = call(
            functools.partial(mix_kernel, first=first, chained=mixed is not None, chunk=64),
            inputs,
            "v" * len(inputs),
            shape((components, 2, cols, rows), f32),
        )
        first += len(stage)
    inputs = [table, last_table, object_new, mixed] + [pieces[s] for s in stages[2]]
    object_out = call(
        functools.partial(spectral_kernel, first=first, chunk=64),
        inputs,
        "v" * len(inputs),
        shape(object_field.shape, f32),
    )
    for distance in [1 << k for k in range(1, tiles.bit_length() - 1)]:
        other = lax.ppermute(share, "tile", swap_pairs(tiles, distance))
        share = (share.astype(f32) + other.astype(f32)).astype(bf16)
    other = lax.ppermute(share, "tile", swap_pairs(tiles, 1))
    probe_out = call(probe_kernel, (turned, share, other), "vvv", shape(probe_field.shape, f32))
    return (jnp.transpose(object_out, (0, 1, 3, 2)), probe_out)


def solution(mesh):
    placed = (
        P(None, ("groups", "energy", "mode"), "tile", None),
        P(None, None, ("groups", "energy", "mode"), None, None),
        P(("groups", "energy", "mode"), "tile", None, None),
        P(("groups", "tile"), None),
        P(),
        P(),
        P(),
    )
    return jax.shard_map(
        body,
        mesh=mesh,
        in_specs=placed,
        out_specs=(
            P(None, ("groups", "energy", "mode"), "tile", None),
            P(None, None, ("groups", "energy", "mode"), None, None),
        ),
        check_vma=False,
    )
```

time: 35.9 us -> 31.6 us (0.88)
  local copies, waits for them, and re-layouts: 3.23 us -> 0 us
  Pallas kernels: 12.8 us -> 12.2 us
  starting transfers between devices: 10.2 us -> 9.68 us
    unnamed x22 -> x0, local copies, waits for them, and re-layouts: 3.23 us -> none
    ppermute x7, waiting for transfers between devices: 5.03 us -> 7.2 us  [the longest x3 7.19 us: body(): pieces[dz, 0] = lax.ppermute(sent, 'energy', swap_pairs(zs, dz))]
    ppermute x1, waiting for transfers between devices: 1.98 us -> 0.36 us  [body(): received = lax.ppermute(lower, 'tile', swap_pairs(2, 1))]
    pallas_call x7 -> x10, Pallas kernels: 12.8 us -> 12.2 us  [call(): pl.pallas_call(kernel, out_shape=outputs, in_specs=[pl.BlockSpec(memory_s...]
    ppermute x7, starting transfers between devices: 5.06 us -> 4.5 us  [the longest x3 4.48 us: body(): pieces[dz, 0] = lax.ppermute(sent, 'energy', swap_pairs(zs, dz))]
    ppermute x1, waiting for transfers between devices: 1.73 us -> 1.29 us  [body(): below = above = lax.ppermute(message, 'tile', swap_pairs(2, 1))]
  transfers between devices with their start and end apart: 10 -> 10, of which waited for: 4 -> 5; matrix products, arithmetic and copies ran while one was open for 0% -> 0% of each run, Pallas kernels for 8% -> 19%
where the time goes in v2:
time: 31.6 us; the launch traced here: 31.4 us
  Pallas kernels  12.2 us (39%)
  starting transfers between devices  9.68 us (31%)
  waiting for transfers between devices  8.86 us (28%)
  between operations  0.71 us (2%)
    pallas_call x10, Pallas kernels, call(): pl.pallas_call(kernel, out_shape=outputs, in_specs=[pl.BlockSpec(memory_s...  12.2 us
    ppermute x3, waiting for transfers between devices, body(): pieces[dz, 0] = lax.ppermute(sent, 'energy', swap_pairs(zs, dz))  7.19 us
    ppermute x3, starting transfers between devices, body(): pieces[dz, 0] = lax.ppermute(sent, 'energy', swap_pairs(zs, dz))  4.48 us
    ppermute x1, starting transfers between devices, body(): below = above = lax.ppermute(message, 'tile', swap_pairs(2, 1))  3.03 us
    ppermute x1, starting transfers between devices, body(): received = lax.ppermute(lower, 'tile', swap_pairs(2, 1))  1.75 us
    ppermute x1, waiting for transfers between devices, body(): below = above = lax.ppermute(message, 'tile', swap_pairs(2, 1))  1.29 us
  transfers between devices with their start and end apart: 10, of which 5 were waited for; matrix products, arithmetic and copies ran while one was open for 0% of the time, Pallas kernels for 19%

profile of v2, /device:TPU:0, one launch (start us, length us, event | category | flops | bytes accessed | tf_op | source)
XLA Modules:
  0.0 31.4 jit_solution(15106462847344126016)
XLA Ops:
  0.6 1.0 %shard_map.105 = (bf16[2,208,128]{2,1,0:T(8,128)(2,1)S(1)}, f32[2,192,128]{2,1,0:T(8,128)S(1)}) custom-call(s32[2,8]{1,0:T(2,128)} %bitcast.5, f32[2,1,192,128]{3,2,1,0:T(8,128)} %bitcast.4), custom_call_target="tpu_custom_call" | custom-call | tf_op jit(solution)/shard_map/pallas_call | solution.py:412
  1.6 3.0 %collective-permute-start = (bf16[2,208,128]{2,1,0:T(8,128)(2,1)S(1)}, bf16[2,208,128]{2,1,0:T(8,128)(2,1)S(1)}, u32[]{:S(2)}, u32[]{:S(2)}) collective-permute-start(bf16[2,208,128]{2,1,0:T(8,128)(2,1)S(1)} %get-tuple-element.22.own_ref), channel_id=1, source_target_pairs={{0,2},{2,0},{1,3},{3,1},{4,6},{6,4},{5,7},{7,5},{8,10},{10,8},{9,1... | collective-permute-start | bytes 319496 | tf_op jit(solution)/shard_map/ppermute | solution.py:444
  4.6 1.7 %shard_map.104 = (s32[2,8]{1,0:T(2,128)S(1)}, bf16[256,256]{1,0:T(8,128)(2,1)S(1)}, bf16[256,256]{1,0:T(8,128)(2,1)S(1)}, f32[2,3,128,128]{3,2,1,0:T(8,128)S(1)}...) custom-call(s32[2,8]{1,0:T(2,128)} %bitcast.6, ...), custom_call_target="tpu_custom_call" | custom-call | tf_op jit(solution)/shard_map/pallas_call | solution.py:412
  6.3 1.3 %collective-permute-done.below_ref.above_ref = bf16[2,208,128]{2,1,0:T(8,128)(2,1)S(1)} collective-permute-done((bf16[2,208,128]{2,1,0:T(8,128)(2,1)S(1)}, bf16[2,208,128]{2,1,0:T(8,128)(2,1)S(1)}, u32[]{:S(2)}, u32[]{:S(2)}) %collective-permute-start) | collective-permute-done | bytes 106528 | tf_op jit(solution)/shard_map/ppermute | solution.py:444
  7.6 4.1 %shard_map.106 = (f32[2,192,128]{2,1,0:T(8,128)S(1)}, bf16[2,192,128]{2,1,0:T(8,128)(2,1)S(1)}, f32[8,3,2,128,128]{4,3,2,1,0:T(8,128)S(1)}) custom-call(s32[2,8]{1,0:T(2,128)S(1)} %get-tuple-element.21.offsets_ref, bf16[2,208,128]{2,1,0:T(8,128)(2,1)S(1)} %get-tuple-element.22.own_ref, bf16[2,208,128]{2,1,0:T(8,128)(2,1)S(1)} %collective-permute-done.below_ref.above_ref, ...), custom_call_target="tpu_custom_call" | custom-call | tf_op jit(solution)/shard_map/pallas_call | solution.py:412
  11.7 1.8 %collective-permute-start.1 = (bf16[2,192,128]{2,1,0:T(8,128)(2,1)S(1)}, bf16[2,192,128]{2,1,0:T(8,128)(2,1)S(1)}, u32[]{:S(2)}, u32[]{:S(2)}) collective-permute-start(bf16[2,192,128]{2,1,0:T(8,128)(2,1)S(1)} %get-tuple-element.28), channel_id=1, source_target_pairs={{0,2},{2,0},{1,3},{3,1},{4,6},{6,4},{5,7},{7,5},{8,10},{10,8},{9,1... | collective-permute-start | bytes 294920 | tf_op jit(solution)/shard_map/ppermute | solution.py:499
  13.4 1.7 %shard_map.112.own_ref = bf16[7,128,128]{2,1,0:T(8,128)(2,1)S(1)} custom-call(s32[2,8]{1,0:T(2,128)S(1)} %get-tuple-element.21.offsets_ref, bf16[2,208,128]{2,1,0:T(8,128)(2,1)S(1)} %get-tuple-element.22.own_ref, bf16[2,208,128]{2,1,0:T(8,128)(2,1)S(1)} %collective-permute-done.below_ref.above_ref, f32[8,3,2,128,128]{4,3,2,1,0:T(8,128)S(1)} %get-tuple-element.33.change_ref), custom_call_target="tpu_custom_call" | custom-call | tf_op jit(solution)/shard_map/pallas_call | solution.py:412
  15.1 0.4 %collective-permute-start.9 = (bf16[7,128,128]{2,1,0:T(8,128)(2,1)S(1)}, bf16[7,128,128]{2,1,0:T(8,128)(2,1)S(1)}, u32[]{:S(2)}, u32[]{:S(2)}) collective-permute-start(bf16[7,128,128]{2,1,0:T(8,128)(2,1)S(1)} %shard_map.112.own_ref), channel_id=1, source_target_pairs={{0,2},{2,0},{1,3},{3,1},{4,6},{6,4},{5,7},{7,5},{8,10},{10,8},{9,1... | collective-permute-start | bytes 688136 | tf_op jit(solution)/shard_map/ppermute | solution.py:553
  15.5 0.6 %shard_map.107.inverse_ref = f32[192,128]{1,0:T(8,128)S(1)} custom-call(bf16[2,208,128]{2,1,0:T(8,128)(2,1)S(1)} %collective-permute-done.below_ref.above_ref, f32[128,128]{1,0:T(8,128)S(1)} %get-tuple-element.29.power_ref, f32[192,128]{1,0:T(8,128)S(1)} %get-tuple-element.30.weight_ref), custom_call_target="tpu_custom_call" | custom-call | tf_op jit(solution)/shard_map/pallas_call | solution.py:412
  16.2 0.4 %collective-permute-done.1.received_ref = bf16[2,192,128]{2,1,0:T(8,128)(2,1)S(1)} collective-permute-done((bf16[2,192,128]{2,1,0:T(8,128)(2,1)S(1)}, bf16[2,192,128]{2,1,0:T(8,128)(2,1)S(1)}, u32[]{:S(2)}, u32[]{:S(2)}) %collective-permute-start.1) | collective-permute-done | bytes 98336 | tf_op jit(solution)/shard_map/ppermute | solution.py:499
  16.5 0.1 shard_map.108
  16.6 1.9 %collective-permute-start.3 = (bf16[2,192,128]{2,1,0:T(8,128)(2,1)S(1)}, bf16[2,192,128]{2,1,0:T(8,128)(2,1)S(1)}, u32[]{:S(2)}, u32[]{:S(2)}) collective-permute-start(bf16[2,192,128]{2,1,0:T(8,128)(2,1)S(1)} %get-tuple-element.32.refs_0_), channel_id=1, source_target_pairs={{0,4},{4,0},{8,12},{12,8},{1,5},{5,1},{9,13},{13,9},{2,6},{6,2},{1... | collective-permute-start | bytes 294920 | tf_op jit(solution)/shard_map/ppermute | solution.py:528
  18.4 2.5 %collective-permute-start.5 = (bf16[2,192,128]{2,1,0:T(8,128)(2,1)S(1)}, bf16[2,192,128]{2,1,0:T(8,128)(2,1)S(1)}, u32[]{:S(2)}, u32[]{:S(2)}) collective-permute-start(bf16[2,192,128]{2,1,0:T(8,128)(2,1)S(1)} %get-tuple-element.32.refs_0_), channel_id=1, source_target_pairs={{0,12},{4,8},{8,4},{12,0},{1,13},{5,9},{9,5},{13,1},{2,14},{6,10},... | collective-permute-start | bytes 294920 | tf_op jit(solution)/shard_map/ppermute | solution.py:528
  20.9 0.1 collective-permute-start.7
  21.1 1.4 %collective-permute-done.3.refs_2_ = bf16[2,192,128]{2,1,0:T(8,128)(2,1)S(1)} collective-permute-done((bf16[2,192,128]{2,1,0:T(8,128)(2,1)S(1)}, bf16[2,192,128]{2,1,0:T(8,128)(2,1)S(1)}, u32[]{:S(2)}, u32[]{:S(2)}) %collective-permute-start.3) | collective-permute-done | bytes 98336 | tf_op jit(solution)/shard_map/ppermute | solution.py:528
  22.4 2.8 %collective-permute-done.5.refs_1_ = bf16[2,192,128]{2,1,0:T(8,128)(2,1)S(1)} collective-permute-done((bf16[2,192,128]{2,1,0:T(8,128)(2,1)S(1)}, bf16[2,192,128]{2,1,0:T(8,128)(2,1)S(1)}, u32[]{:S(2)}, u32[]{:S(2)}) %collective-permute-start.5) | collective-permute-done | bytes 98336 | tf_op jit(solution)/shard_map/ppermute | solution.py:528
  25.2 3.0 %collective-permute-done.7.refs_3_ = bf16[2,192,128]{2,1,0:T(8,128)(2,1)S(1)} collective-permute-done((bf16[2,192,128]{2,1,0:T(8,128)(2,1)S(1)}, bf16[2,192,128]{2,1,0:T(8,128)(2,1)S(1)}, u32[]{:S(2)}, u32[]{:S(2)}) %collective-permute-start.7) | collective-permute-done | bytes 98336 | tf_op jit(solution)/shard_map/ppermute | solution.py:528
  28.3 0.0 collective-permute-start.8
  28.3 0.0 collective-permute-done.9.received_ref
  28.3 1.1 %shard_map.113 = f32[2,3,1,128,128]{4,3,2,1,0:T(8,128)} custom-call(f32[2,3,128,128]{3,2,1,0:T(8,128)S(1)} %get-tuple-element.23.probe_ref, bf16[7,128,128]{2,1,0:T(8,128)(2,1)S(1)} %shard_map.112.own_ref, bf16[7,128,128]{2,1,0:T(8,128)(2,1)S(1)} %collective-permute-done.9.received_ref), custom_call_target="tpu_custom_call" | custom-call | tf_op jit(solution)/shard_map/pallas_call | solution.py:412
  29.3 0.0 collective-permute-done.2.refs_1_
  29.3 0.5 %shard_map.109.refs_0_ = f32[8,2,192,128]{3,2,1,0:T(8,128)S(1)} custom-call(f32[8,8,8,128]{3,2,1,0:T(8,128)S(1)} %get-tuple-element.18.table_ref, bf16[2,192,128]{2,1,0:T(8,128)(2,1)S(1)} %get-tuple-element.32.refs_0_, bf16[2,192,128]{2,1,0:T(8,128)(2,1)S(1)} %collective-permute-done.2.refs_1_, bf16[2,192,128]{2,1,0:T(8,128)(2,1)S(1)} %collective-permute-done.3.refs_2_, ...), custom_call_target="tpu_custom_call" | custom-call | tf_op jit(solution)/shard_map/pallas_call | solution.py:412
  29.8 0.4 %shard_map.110.mixed_ref = f32[8,2,192,128]{3,2,1,0:T(8,128)S(1)} custom-call(f32[8,8,8,128]{3,2,1,0:T(8,128)S(1)} %get-tuple-element.18.table_ref, f32[8,2,192,128]{3,2,1,0:T(8,128)S(1)} %shard_map.109.refs_0_, bf16[2,192,128]{2,1,0:T(8,128)(2,1)S(1)} %collective-permute-done.5.refs_1_, bf16[2,192,128]{2,1,0:T(8,128)(2,1)S(1)} %collective-permute-done.6.refs_2_, ...), custom_call_target="tpu_custom_call" | custom-call | tf_op jit(solution)/shard_map/pallas_call | solution.py:412
  30.3 1.2 %shard_map.111 = f32[2,1,192,128]{3,2,1,0:T(8,128)} custom-call(f32[8,8,8,128]{3,2,1,0:T(8,128)S(1)} %get-tuple-element.18.table_ref, f32[2,8,8,128]{3,2,1,0:T(8,128)S(1)} %get-tuple-element.19.last_ref, f32[2,192,128]{2,1,0:T(8,128)S(1)} %get-tuple-element.31.own_ref, f32[8,2,192,128]{3,2,1,0:T(8,128)S(1)} %shard_map.110.mixed_ref, ...), custom_call_target="tpu_custom_call" | custom-call | tf_op jit(solution)/shard_map/pallas_call | solution.py:412
  (6 shorter events, 0.0 us)
Async XLA Ops:
  1.6 6.0 %collective-permute-start = (bf16[2,208,128]{2,1,0:T(8,128)(2,1)S(1)}, bf16[2,208,128]{2,1,0:T(8,128)(2,1)S(1)}, u32[]{:S(2)}, u32[]{:S(2)}) collective-permute-start(bf16[2,208,128]{2,1,0:T(8,128)(2,1)S(1)} %get-tuple-element.22.own_ref), channel_id=1, source_target_pairs={{0,2},{2,0},{1,3},{3,1},{4,6},{6,4},{5,7},{7,5},{8,10},{10,8},{9,1... | collective-permute-start | bytes 319496 | tf_op jit(solution)/shard_map/ppermute | solution.py:444
  11.7 4.8 %collective-permute-start.1 = (bf16[2,192,128]{2,1,0:T(8,128)(2,1)S(1)}, bf16[2,192,128]{2,1,0:T(8,128)(2,1)S(1)}, u32[]{:S(2)}, u32[]{:S(2)}) collective-permute-start(bf16[2,192,128]{2,1,0:T(8,128)(2,1)S(1)} %get-tuple-element.28), channel_id=1, source_target_pairs={{0,2},{2,0},{1,3},{3,1},{4,6},{6,4},{5,7},{7,5},{8,10},{10,8},{9,1... | collective-permute-start | bytes 294920 | tf_op jit(solution)/shard_map/ppermute | solution.py:499
  15.1 13.1 %collective-permute-start.9 = (bf16[7,128,128]{2,1,0:T(8,128)(2,1)S(1)}, bf16[7,128,128]{2,1,0:T(8,128)(2,1)S(1)}, u32[]{:S(2)}, u32[]{:S(2)}) collective-permute-start(bf16[7,128,128]{2,1,0:T(8,128)(2,1)S(1)} %shard_map.112.own_ref), channel_id=1, source_target_pairs={{0,2},{2,0},{1,3},{3,1},{4,6},{6,4},{5,7},{7,5},{8,10},{10,8},{9,1... | collective-permute-start | bytes 688136 | tf_op jit(solution)/shard_map/ppermute | solution.py:553
  16.6 5.9 %collective-permute-start.3 = (bf16[2,192,128]{2,1,0:T(8,128)(2,1)S(1)}, bf16[2,192,128]{2,1,0:T(8,128)(2,1)S(1)}, u32[]{:S(2)}, u32[]{:S(2)}) collective-permute-start(bf16[2,192,128]{2,1,0:T(8,128)(2,1)S(1)} %get-tuple-element.32.refs_0_), channel_id=1, source_target_pairs={{0,4},{4,0},{8,12},{12,8},{1,5},{5,1},{9,13},{13,9},{2,6},{6,2},{1... | collective-permute-start | bytes 294920 | tf_op jit(solution)/shard_map/ppermute | solution.py:528
  18.4 6.8 %collective-permute-start.5 = (bf16[2,192,128]{2,1,0:T(8,128)(2,1)S(1)}, bf16[2,192,128]{2,1,0:T(8,128)(2,1)S(1)}, u32[]{:S(2)}, u32[]{:S(2)}) collective-permute-start(bf16[2,192,128]{2,1,0:T(8,128)(2,1)S(1)} %get-tuple-element.32.refs_0_), channel_id=1, source_target_pairs={{0,12},{4,8},{8,4},{12,0},{1,13},{5,9},{9,5},{13,1},{2,14},{6,10},... | collective-permute-start | bytes 294920 | tf_op jit(solution)/shard_map/ppermute | solution.py:528
  20.9 7.3 %collective-permute-start.7 = (bf16[2,192,128]{2,1,0:T(8,128)(2,1)S(1)}, bf16[2,192,128]{2,1,0:T(8,128)(2,1)S(1)}, u32[]{:S(2)}, u32[]{:S(2)}) collective-permute-start(bf16[2,192,128]{2,1,0:T(8,128)(2,1)S(1)} %get-tuple-element.32.refs_0_), channel_id=1, source_target_pairs={{0,8},{4,12},{8,0},{12,4},{1,9},{5,13},{9,1},{13,5},{2,10},{6,14},... | collective-permute-start | bytes 294920 | tf_op jit(solution)/shard_map/ppermute | solution.py:528
  21.1 8.3 %collective-permute-start.2 = (bf16[2,192,128]{2,1,0:T(8,128)(2,1)S(1)}, bf16[2,192,128]{2,1,0:T(8,128)(2,1)S(1)}, u32[]{:S(2)}, u32[]{:S(2)}) collective-permute-start(bf16[2,192,128]{2,1,0:T(8,128)(2,1)S(1)} %get-tuple-element.32.refs_0_), channel_id=1, source_target_pairs={{0,1},{1,0},{2,3},{3,2},{4,5},{5,4},{6,7},{7,6},{8,9},{9,8},{10,11... | collective-permute-start | bytes 294920 | tf_op jit(solution)/shard_map/ppermute | solution.py:531
  22.4 6.9 %collective-permute-start.4 = (bf16[2,192,128]{2,1,0:T(8,128)(2,1)S(1)}, bf16[2,192,128]{2,1,0:T(8,128)(2,1)S(1)}, u32[]{:S(2)}, u32[]{:S(2)}) collective-permute-start(bf16[2,192,128]{2,1,0:T(8,128)(2,1)S(1)} %collective-permute-done.3.refs_2_), channel_id=1, source_target_pairs={{0,1},{1,0},{2,3},{3,2},{4,5},{5,4},{6,7},{7,6},{8,9},{9,8},{10,11... | collective-permute-start | bytes 294920 | tf_op jit(solution)/shard_map/ppermute | solution.py:531
  25.2 4.6 %collective-permute-start.6 = (bf16[2,192,128]{2,1,0:T(8,128)(2,1)S(1)}, bf16[2,192,128]{2,1,0:T(8,128)(2,1)S(1)}, u32[]{:S(2)}, u32[]{:S(2)}) collective-permute-start(bf16[2,192,128]{2,1,0:T(8,128)(2,1)S(1)} %collective-permute-done.5.refs_1_), channel_id=1, source_target_pairs={{0,1},{1,0},{2,3},{3,2},{4,5},{5,4},{6,7},{7,6},{8,9},{9,8},{10,11... | collective-permute-start | bytes 294920 | tf_op jit(solution)/shard_map/ppermute | solution.py:531
  28.3 2.0 %collective-permute-start.8 = (bf16[2,192,128]{2,1,0:T(8,128)(2,1)S(1)}, bf16[2,192,128]{2,1,0:T(8,128)(2,1)S(1)}, u32[]{:S(2)}, u32[]{:S(2)}) collective-permute-start(bf16[2,192,128]{2,1,0:T(8,128)(2,1)S(1)} %collective-permute-done.7.refs_3_), channel_id=1, source_target_pairs={{0,1},{1,0},{2,3},{3,2},{4,5},{5,4},{6,7},{7,6},{8,9},{9,8},{10,11... | collective-permute-start | bytes 294920 | tf_op jit(solution)/shard_map/ppermute | solution.py:531

commit v3 on v2

--- a/solution.py
+++ b/solution.py
@@ -13,7 +13,7 @@
 PCOLS = 2
 STEP = 32
 LANES = 128
-PAD_ROWS = 16
+PAD_ROWS = 8
 
 
 def swap_pairs(size, distance):
@@ -64,10 +64,10 @@
         for q in range(positions):
             value = offsets_ref[k, q].astype(jnp.float32)
             line = jnp.where(lane == k * positions + q, value, line)
+    message_ref[2 * cols :] = line.astype(jnp.bfloat16)
     for part in range(2):
         copies[1 + part].wait()
-        message_ref[part, :cols] = object_ref[part].astype(jnp.bfloat16)
-        message_ref[part, cols:] = line.astype(jnp.bfloat16)
+        message_ref[part * cols : (part + 1) * cols] = object_ref[part].astype(jnp.bfloat16)
 
 
 def turn_kernel(
@@ -168,9 +168,9 @@
     cols = extended.shape[2]
     has_below = lax.axis_index("tile") < tiles - 1
     for part in range(2):
-        extended[part, 0] = own_ref[part, :cols].astype(jnp.float32)
-        below = below_ref[part, :cols].astype(jnp.float32)
-        extended[part, 1] = jnp.where(has_below, below, 0.0)
+        here = slice(part * cols, (part + 1) * cols)
+        extended[part, 0] = own_ref[here].astype(jnp.float32)
+        extended[part, 1] = jnp.where(has_below, below_ref[here].astype(jnp.float32), 0.0)
 
 
 def side_by_side(blocks):
@@ -192,6 +192,7 @@
     upper_ref,
     lower_ref,
     change_ref,
+    window_ref,
     extended,
     total,
     *,
@@ -213,11 +214,15 @@
     def span(w):
         return slice(w * extent, (w + 1) * extent)
 
-    for block in range(positions // group):
+    def members(block):
+        return [(member, block * group + member) for member in range(group)]
+
+    def enter(block):
         rounded = []
-        for member in range(group):
-            q = block * group + member
+        for member, q in members(block):
             object_real, object_imag = cut(extended, offsets_ref, q, extent)
+            window_ref[q, 0] = object_real
+            window_ref[q, 1] = object_imag
             for m in range(modes):
                 probe_real = probe_ref[0, m]
                 probe_imag = probe_ref[1, m]
@@ -226,14 +231,18 @@
                 change_ref[q, m, 0] = wave_real
                 change_ref[q, m, 1] = wave_imag
                 rounded.append(side_by_side([wave_real, wave_imag]).astype(jnp.bfloat16))
-        halfway = dot(stack_up(rounded), backward_ref[...]).astype(jnp.bfloat16)
-        standing = side_by_side(
+        return stack_up(rounded)
+
+    def first_half(block, lying):
+        halfway = dot(lying, backward_ref[...]).astype(jnp.bfloat16)
+        return side_by_side(
             [stack_up([halfway[span(w), low], halfway[span(w), high]]) for w in range(waves)]
         )
+
+    def project(block, standing):
         spectrum = dot(forward_ref[...], standing)
         scaled = []
-        for member in range(group):
-            q = block * group + member
+        for member, q in members(block):
             magnitude = jnp.full((extent, extent), 0.01, jnp.float32)
             for m in range(modes):
                 place = span(member * modes + m)
@@ -248,13 +257,17 @@
                         jnp.bfloat16
                     )
                 )
-        returned = dot(backward_ref[...], side_by_side(scaled)).astype(jnp.bfloat16)
-        lying = stack_up(
+        return side_by_side(scaled)
+
+    def second_half(block, standing):
+        returned = dot(backward_ref[...], standing).astype(jnp.bfloat16)
+        return stack_up(
             [side_by_side([returned[low, span(w)], returned[high, span(w)]]) for w in range(waves)]
         )
+
+    def leave(block, lying):
         new_wave = dot(lying, forward_ref[...])
-        for member in range(group):
-            q = block * group + member
+        for member, q in members(block):
             row, col = corner(offsets_ref, q)
             here = pl.ds(col, extent)
             sum_real = jnp.zeros((extent, extent), jnp.float32)
@@ -273,43 +286,43 @@
                 for side, moved in enumerate(spread(value, row)):
                     total[part, side, here] += moved
 
+    stages = [[enter], [first_half], [project], [second_half, leave]]
+    blocks = positions // group
+    held = [None] * blocks
+    for tick in range(blocks + len(stages) - 1):
+        for depth in range(len(stages)):
+            block = tick - depth
+            if not 0 <= block < blocks:
+                continue
+            for stage in stages[depth]:
+                held[block] = stage(block) if stage is enter else stage(block, held[block])
+
     for part in range(2):
         upper_ref[part] = total[part, 0]
         lower_ref[part] = total[part, 1].astype(jnp.bfloat16)
 
 
-def share_kernel(
-    offsets_ref, own_ref, below_ref, change_ref, share_ref, extended, window, *, tiles
-):
+def share_kernel(change_ref, window_ref, share_ref):
     extent = change_ref.shape[-1]
     positions, modes = change_ref.shape[:2]
-    extend(extended, own_ref, below_ref, tiles)
-    density = jnp.zeros((extent, extent), jnp.float32)
-    for q in range(positions):
-        object_real, object_imag = cut(extended, offsets_ref, q, extent)
-        window[q, 0] = object_real
-        window[q, 1] = object_imag
-        density += object_real * object_real + object_imag * object_imag
-    share_ref[2 * modes] = density.astype(jnp.bfloat16)
-    chunk = 16
-
-    def step(index, carry):
-        here = pl.ds(pl.multiple_of(index * chunk, chunk), chunk)
-        for m in range(modes):
-            sum_real = jnp.zeros((chunk, extent), jnp.float32)
-            sum_imag = jnp.zeros((chunk, extent), jnp.float32)
-            for q in range(positions):
-                object_real = window[q, 0, here]
-                object_imag = window[q, 1, here]
+    chunk = 32
+    for start in range(0, extent, chunk):
+        here = pl.ds(start, chunk)
+        density = jnp.zeros((chunk, extent), jnp.float32)
+        sums = [[jnp.zeros((chunk, extent), jnp.float32) for _ in range(2)] for _ in range(modes)]
+        for q in range(positions):
+            object_real = window_ref[q, 0, here]
+            object_imag = window_ref[q, 1, here]
+            density += object_real * object_real + object_imag * object_imag
+            for m in range(modes):
                 change_real = change_ref[q, m, 0, here]
                 change_imag = change_ref[q, m, 1, here]
-                sum_real += object_real * change_real + object_imag * change_imag
-                sum_imag += object_real * change_imag - object_imag * change_real
-            share_ref[m, here] = sum_real.astype(jnp.bfloat16)
-            share_ref[modes + m, here] = sum_imag.astype(jnp.bfloat16)
-        return carry
-
-    lax.fori_loop(0, extent // chunk, step, 0)
+                sums[m][0] += object_real * change_real + object_imag * change_imag
+                sums[m][1] += object_real * change_imag - object_imag * change_real
+        for m in range(modes):
+            for part in range(2):
+                share_ref[part * modes + m, here] = sums[m][part].astype(jnp.bfloat16)
+        share_ref[2 * modes, here] = density.astype(jnp.bfloat16)
 
 
 def weight_kernel(above_ref, power_ref, weight_ref, inverse_ref, other, *, positions):
@@ -317,14 +330,14 @@
     cols = inverse_ref.shape[0]
     power = power_ref[...]
     other[...] = jnp.zeros_like(other)
-    line = above_ref[0, cols : cols + PAD_ROWS].astype(jnp.float32)[:8]
+    line = above_ref[2 * cols :].astype(jnp.float32)
     lane = lax.broadcasted_iota(jnp.int32, line.shape, 1)
+    above = [
+        jnp.max(jnp.where(lane == k, line, 0.0)).astype(jnp.int32) for k in range(2 * positions)
+    ]
     for q in range(positions):
-        above = [
-            jnp.max(jnp.where(lane == k * positions + q, line, 0.0)).astype(jnp.int32) for k in range(2)
-        ]
-        row = STEP * (q // PCOLS) + above[0]
-        col = STEP * (q % PCOLS) + above[1]
+        row = STEP * (q // PCOLS) + above[q]
+        col = STEP * (q % PCOLS) + above[positions + q]
         _, right = spread(power, row)
         other[pl.ds(col, extent)] += right
     has_above = lax.axis_index("tile") > 0
@@ -346,50 +359,47 @@
     refs = refs[:-1]
     before, refs = (refs[0], refs[1:]) if chained else (None, refs)
     components, parts, rows, lanes = mixed_ref.shape
-    per_part = rows // chunk
     height = table_ref.shape[2]
-
-    def step(index, carry):
-        part = index // per_part
-        here = pl.ds(pl.multiple_of((index % per_part) * chunk, chunk), chunk)
-        folded = (chunk // height, height, lanes)
-        values = [ref[part, here].astype(jnp.float32).reshape(folded) for ref in refs]
-        for k in range(components):
-            terms = [table_ref[first + n, k] * value for n, value in enumerate(values)]
-            if before is not None:
-                terms.insert(0, before[k, part, here].reshape(folded))
-            mixed_ref[k, part, here] = functools.reduce(jnp.add, terms).reshape(chunk, lanes)
-        return carry
-
-    lax.fori_loop(0, parts * per_part, step, 0)
+    folded = (chunk // height, height, lanes)
+    for part in range(parts):
+        for start in range(0, rows, chunk):
+            here = pl.ds(start, chunk)
+            values = [ref[part, here].astype(jnp.float32).reshape(folded) for ref in refs]
+            for k in range(components):
+                terms = [table_ref[first + n, k] * value for n, value in enumerate(values)]
+                if before is not None:
+                    terms.insert(0, before[k, part, here].reshape(folded))
+                mixed_ref[k, part, here] = functools.reduce(jnp.add, terms).reshape(chunk, lanes)
 
 
 def spectral_kernel(table_ref, last_ref, own_ref, mixed_ref, *refs, first, chunk):
-    refs, out_ref = refs[:-1], refs[-1]
+    refs, (out_hbm, result, sems) = refs[:-3], refs[-3:]
     parts, rows, lanes = own_ref.shape
     components = last_ref.shape[1]
-    per_part = rows // chunk
     height = table_ref.shape[2]
-
-    def step(index, carry):
-        part = index // per_part
-        here = pl.ds(pl.multiple_of((index % per_part) * chunk, chunk), chunk)
-        folded = (chunk // height, height, lanes)
-        values = [ref[part, here].astype(jnp.float32).reshape(folded) for ref in refs]
-        terms = [0.5 * own_ref[part, here].reshape(folded)]
-        for k in range(components):
-            c = mixed_ref[k, part, here].reshape(folded)
-            for n, value in enumerate(values):
-                c += table_ref[first + n, k] * value
-            t = last_ref[1, k]
-            c = c - jnp.minimum(jnp.maximum(c, -t), t)
-            terms.append(last_ref[0, k] * c)
-        while len(terms) > 1:
-            terms = [sum(terms[k : k + 2][1:], terms[k]) for k in range(0, len(terms), 2)]
-        out_ref[part, 0, here] = terms[0].reshape(chunk, lanes)
-        return carry
-
-    lax.fori_loop(0, parts * per_part, step, 0)
+    folded = (chunk // height, height, lanes)
+    copies = []
+    for part in range(parts):
+        for start in range(0, rows, chunk):
+            here = pl.ds(start, chunk)
+            values = [ref[part, here].astype(jnp.float32).reshape(folded) for ref in refs]
+            terms = [0.5 * own_ref[part, here].reshape(folded)]
+            for k in range(components):
+                c = mixed_ref[k, part, here].reshape(folded)
+                for n, value in enumerate(values):
+                    c += table_ref[first + n, k] * value
+                t = last_ref[1, k]
+                c = c - jnp.minimum(jnp.maximum(c, -t), t)
+                terms.append(last_ref[0, k] * c)
+            while len(terms) > 1:
+                terms = [sum(terms[k : k + 2][1:], terms[k]) for k in range(0, len(terms), 2)]
+            result[part, here] = terms[0].reshape(chunk, lanes)
+        copies.append(
+            pltpu.make_async_copy(result.at[part], out_hbm.at[part, 0], sems.at[part])
+        )
+        copies[-1].start()
+    for copy in copies:
+        copy.wait()
 
 
 def probe_kernel(probe_ref, own_ref, received_ref, out_ref):
@@ -403,17 +413,17 @@
             out_ref[part, m, 0] = (probe_ref[part, m] + numerator * inverse).T
 
 
-def call(kernel, inputs, places, outputs, scratch=(), limit=4):
+def call(kernel, inputs, places, outputs, scratch=(), limit=4, out="v"):
+    kinds = {"s": pltpu.SMEM, "v": pltpu.VMEM, "h": pltpu.HBM}
     inputs = [
         pltpu.with_memory_space_constraint(x, pltpu.HBM) if p == "h" else x
         for x, p in zip(inputs, places)
     ]
-    kinds = {"s": pltpu.SMEM, "v": pltpu.VMEM, "h": pltpu.HBM}
     return pl.pallas_call(
         kernel,
         out_shape=outputs,
         in_specs=[pl.BlockSpec(memory_space=kinds[p]) for p in places],
-        out_specs=jax.tree.map(lambda _: pl.BlockSpec(memory_space=pltpu.VMEM), outputs),
+        out_specs=jax.tree.map(lambda _: pl.BlockSpec(memory_space=kinds[out]), outputs),
         scratch_shapes=list(scratch),
         compiler_params=pltpu.CompilerParams(vmem_limit_bytes=limit << 20),
     )(*inputs)
@@ -437,7 +447,7 @@
         round_kernel,
         (offsets, object_field),
         "hh",
-        (shape((2, cols + PAD_ROWS, rows), bf16), shape((2, cols, rows), f32)),
+        (shape((2 * cols + PAD_ROWS, rows), bf16), shape((2, cols, rows), f32)),
         (pltpu.SMEM((2, positions), jnp.int32), pltpu.SemaphoreType.DMA((3,))),
     )
     if tiles == 2:
@@ -446,10 +456,11 @@
         below = lax.ppermute(message, "tile", [(i + 1, i) for i in range(tiles - 1)])
         above = lax.ppermute(message, "tile", [(i, i + 1) for i in range(tiles - 1)])
 
-    far = zs // 2
+    near, far = gather_order(zs)[0], gather_order(zs)[-1]
+    middle = [dz for dz in range(1, zs) if dz not in (near, far)]
     stages = [
-        [(dz, dm) for dz in (0, 1) for dm in range(ms)],
-        [(dz, dm) for dz in range(2, zs) for dm in range(ms) if dz != far] + [(far, 0)],
+        [(dz, dm) for dz in (0, near) for dm in range(ms)],
+        [(dz, dm) for dz in middle for dm in range(ms)] + [(far, 0)],
         [(far, dm) for dm in range(1, ms)],
     ]
     sources = sum(stages, [])
@@ -480,7 +491,7 @@
         ),
         limit=8,
     )
-    upper, lower, change = call(
+    upper, lower, change, window = call(
         functools.partial(wave_kernel, tiles=tiles, group=2),
         (offsets, message, below, turned, moduli, forward, backward),
         "svvvvvv",
@@ -488,6 +499,7 @@
             shape((2, cols, rows), f32),
             shape((2, cols, rows), bf16),
             shape((positions, modes, 2, extent, extent), f32),
+            shape((positions, 2, extent, extent), f32),
         ),
         (
             pltpu.VMEM((2, 2, cols, LANES), f32),
@@ -506,17 +518,7 @@
         shape((cols, rows), f32),
         (pltpu.VMEM((cols, rows), f32),),
     )
-    share = call(
-        functools.partial(share_kernel, tiles=tiles),
-        (offsets, message, below, change),
-        "svvv",
-        shape((2 * modes + 1, extent, extent), bf16),
-        (
-            pltpu.VMEM((2, 2, cols, LANES), f32),
-            pltpu.VMEM((positions, 2, extent, extent), f32),
-        ),
-        limit=8,
-    )
+    share = call(share_kernel, (change, window), "vv", shape((2 * modes + 1, extent, extent), bf16))
     object_new, sent = call(
         object_kernel,
         (object_here, upper, received, inverse),
@@ -546,6 +548,8 @@
         inputs,
         "v" * len(inputs),
         shape(object_field.shape, f32),
+        (pltpu.VMEM((2, cols, rows), f32), pltpu.SemaphoreType.DMA((2,))),
+        out="h",
     )
     for distance in [1 << k for k in range(1, tiles.bit_length() - 1)]:
         other = lax.ppermute(share, "tile", swap_pairs(tiles, distance))
@@ -553,6 +557,10 @@
     other = lax.ppermute(share, "tile", swap_pairs(tiles, 1))
     probe_out = call(probe_kernel, (turned, share, other), "vvv", shape(probe_field.shape, f32))
     return (jnp.transpose(object_out, (0, 1, 3, 2)), probe_out)
+
+
+def gather_order(zs):
+    return [zs // 2] + [dz for dz in range(1, zs) if dz != zs // 2]
 
 
 def solution(mesh):

time: 31.6 us -> 30.9 us (0.978)
  Pallas kernels: 12.2 us -> 10.2 us
  waiting for transfers between devices: 8.86 us -> 10 us
    ppermute x1, waiting for transfers between devices: 0.36 us -> 2.56 us  [body(): received = lax.ppermute(lower, 'tile', swap_pairs(2, 1))]
    pallas_call x10, Pallas kernels: 12.2 us -> 10.2 us  [call(): pl.pallas_call(kernel, out_shape=outputs, in_specs=[pl.BlockSpec(memory_s...]
    ppermute x3, waiting for transfers between devices: 7.19 us -> 6.3 us  [body(): pieces[dz, 0] = lax.ppermute(sent, 'energy', swap_pairs(zs, dz))]
  transfers between devices with their start and end apart: 10 -> 10, of which waited for: 5 -> 5; matrix products, arithmetic and copies ran while one was open for 0% -> 0% of each run, Pallas kernels for 19% -> 15%
where the time goes in v3:
time: 30.9 us; the launch traced here: 30.7 us
  Pallas kernels  10.2 us (33%)
  waiting for transfers between devices  10 us (32%)
  starting transfers between devices  9.84 us (32%)
  between operations  0.7 us (2%)
    pallas_call x10, Pallas kernels, call(): pl.pallas_call(kernel, out_shape=outputs, in_specs=[pl.BlockSpec(memory_s...  10.2 us
    ppermute x3, waiting for transfers between devices, body(): pieces[dz, 0] = lax.ppermute(sent, 'energy', swap_pairs(zs, dz))  6.3 us
    ppermute x3, starting transfers between devices, body(): pieces[dz, 0] = lax.ppermute(sent, 'energy', swap_pairs(zs, dz))  4.54 us
    ppermute x1, starting transfers between devices, body(): below = above = lax.ppermute(message, 'tile', swap_pairs(2, 1))  3.03 us
    ppermute x1, waiting for transfers between devices, body(): received = lax.ppermute(lower, 'tile', swap_pairs(2, 1))  2.56 us
    ppermute x1, starting transfers between devices, body(): received = lax.ppermute(lower, 'tile', swap_pairs(2, 1))  1.89 us
    ppermute x1, waiting for transfers between devices, body(): below = above = lax.ppermute(message, 'tile', swap_pairs(2, 1))  1.16 us
  transfers between devices with their start and end apart: 10, of which 5 were waited for; matrix products, arithmetic and copies ran while one was open for 0% of the time, Pallas kernels for 15%

profile of v3, /device:TPU:0, one launch (start us, length us, event | category | flops | bytes accessed | tf_op | source)
XLA Modules:
  0.0 30.7 jit_solution(10043393309256041336)
XLA Ops:
  0.6 1.0 %shard_map.105 = (bf16[392,128]{1,0:T(8,128)(2,1)S(1)}, f32[2,192,128]{2,1,0:T(8,128)S(1)}) custom-call(s32[2,8]{1,0:T(2,128)} %bitcast.5, f32[2,1,192,128]{3,2,1,0:T(8,128)} %bitcast.4), custom_call_target="tpu_custom_call" | custom-call | tf_op jit(solution)/shard_map/pallas_call | solution.py:422
  1.6 3.0 %collective-permute-start = (bf16[392,128]{1,0:T(8,128)(2,1)S(1)}, bf16[392,128]{1,0:T(8,128)(2,1)S(1)}, u32[]{:S(2)}, u32[]{:S(2)}) collective-permute-start(bf16[392,128]{1,0:T(8,128)(2,1)S(1)} %get-tuple-element.23.own_ref), channel_id=1, source_target_pairs={{0,2},{2,0},{1,3},{3,1},{4,6},{6,4},{5,7},{7,5},{8,10},{10,8},{9,1... | collective-permute-start | bytes 301064 | tf_op jit(solution)/shard_map/ppermute | solution.py:454
  4.6 1.7 %shard_map.104 = (s32[2,8]{1,0:T(2,128)S(1)}, bf16[256,256]{1,0:T(8,128)(2,1)S(1)}, bf16[256,256]{1,0:T(8,128)(2,1)S(1)}, f32[2,3,128,128]{3,2,1,0:T(8,128)S(1)}...) custom-call(s32[2,8]{1,0:T(2,128)} %bitcast.6, ...), custom_call_target="tpu_custom_call" | custom-call | tf_op jit(solution)/shard_map/pallas_call | solution.py:422
  6.3 1.2 %collective-permute-done.below_ref.above_ref = bf16[392,128]{1,0:T(8,128)(2,1)S(1)} collective-permute-done((bf16[392,128]{1,0:T(8,128)(2,1)S(1)}, bf16[392,128]{1,0:T(8,128)(2,1)S(1)}, u32[]{:S(2)}, u32[]{:S(2)}) %collective-permute-start) | collective-permute-done | bytes 100384 | tf_op jit(solution)/shard_map/ppermute | solution.py:454
  7.5 3.6 %shard_map.106 = (f32[2,192,128]{2,1,0:T(8,128)S(1)}, bf16[2,192,128]{2,1,0:T(8,128)(2,1)S(1)}, f32[8,3,2,128,128]{4,3,2,1,0:T(8,128)S(1)}, f32[8,2,128,128]{3,2,1,0:T(8,128)S(1)}) custom-call(s32[2,8]{1,0:T(2,128)S(1)} %get-tuple-element.22.offsets_ref, bf16[392,128]{1,0:T(8,128)(2,1)S(1)} %get-tuple-element.23.own_ref, ...), custom_call_target="tpu_custom_call" | custom-call | tf_op jit(solution)/shard_map/pallas_call | solution.py:422
  11.1 1.9 %collective-permute-start.1 = (bf16[2,192,128]{2,1,0:T(8,128)(2,1)S(1)}, bf16[2,192,128]{2,1,0:T(8,128)(2,1)S(1)}, u32[]{:S(2)}, u32[]{:S(2)}) collective-permute-start(bf16[2,192,128]{2,1,0:T(8,128)(2,1)S(1)} %get-tuple-element.29), channel_id=1, source_target_pairs={{0,2},{2,0},{1,3},{3,1},{4,6},{6,4},{5,7},{7,5},{8,10},{10,8},{9,1... | collective-permute-start | bytes 294920 | tf_op jit(solution)/shard_map/ppermute | solution.py:511
  13.0 0.7 %shard_map.112.own_ref = bf16[7,128,128]{2,1,0:T(8,128)(2,1)S(1)} custom-call(f32[8,3,2,128,128]{4,3,2,1,0:T(8,128)S(1)} %get-tuple-element.34.change_ref, f32[8,2,128,128]{3,2,1,0:T(8,128)S(1)} %get-tuple-element.35.window_ref), custom_call_target="tpu_custom_call" | custom-call | tf_op jit(solution)/shard_map/pallas_call | solution.py:422
  13.7 0.3 collective-permute-start.9
  13.9 0.3 %shard_map.107.inverse_ref = f32[192,128]{1,0:T(8,128)S(1)} custom-call(bf16[392,128]{1,0:T(8,128)(2,1)S(1)} %collective-permute-done.below_ref.above_ref, f32[128,128]{1,0:T(8,128)S(1)} %get-tuple-element.30.power_ref, f32[192,128]{1,0:T(8,128)S(1)} %get-tuple-element.31.weight_ref), custom_call_target="tpu_custom_call" | custom-call | tf_op jit(solution)/shard_map/pallas_call | solution.py:422
  14.3 2.6 %collective-permute-done.1.received_ref = bf16[2,192,128]{2,1,0:T(8,128)(2,1)S(1)} collective-permute-done((bf16[2,192,128]{2,1,0:T(8,128)(2,1)S(1)}, bf16[2,192,128]{2,1,0:T(8,128)(2,1)S(1)}, u32[]{:S(2)}, u32[]{:S(2)}) %collective-permute-start.1) | collective-permute-done | bytes 98336 | tf_op jit(solution)/shard_map/ppermute | solution.py:511
  16.8 0.1 shard_map.108
  16.9 3.0 %collective-permute-start.3 = (bf16[2,192,128]{2,1,0:T(8,128)(2,1)S(1)}, bf16[2,192,128]{2,1,0:T(8,128)(2,1)S(1)}, u32[]{:S(2)}, u32[]{:S(2)}) collective-permute-start(bf16[2,192,128]{2,1,0:T(8,128)(2,1)S(1)} %get-tuple-element.33.refs_0_), channel_id=1, source_target_pairs={{0,8},{4,12},{8,0},{12,4},{1,9},{5,13},{9,1},{13,5},{2,10},{6,14},... | collective-permute-start | bytes 294920 | tf_op jit(solution)/shard_map/ppermute | solution.py:530
  19.9 1.6 %collective-permute-start.5 = (bf16[2,192,128]{2,1,0:T(8,128)(2,1)S(1)}, bf16[2,192,128]{2,1,0:T(8,128)(2,1)S(1)}, u32[]{:S(2)}, u32[]{:S(2)}) collective-permute-start(bf16[2,192,128]{2,1,0:T(8,128)(2,1)S(1)} %get-tuple-element.33.refs_0_), channel_id=1, source_target_pairs={{0,4},{4,0},{8,12},{12,8},{1,5},{5,1},{9,13},{13,9},{2,6},{6,2},{1... | collective-permute-start | bytes 294920 | tf_op jit(solution)/shard_map/ppermute | solution.py:530
  21.4 0.0 collective-permute-start.7
  21.4 0.0 collective-permute-start.2
  21.4 3.2 %collective-permute-done.3.refs_2_ = bf16[2,192,128]{2,1,0:T(8,128)(2,1)S(1)} collective-permute-done((bf16[2,192,128]{2,1,0:T(8,128)(2,1)S(1)}, bf16[2,192,128]{2,1,0:T(8,128)(2,1)S(1)}, u32[]{:S(2)}, u32[]{:S(2)}) %collective-permute-start.3) | collective-permute-done | bytes 98336 | tf_op jit(solution)/shard_map/ppermute | solution.py:530
  24.7 0.0 collective-permute-start.4
  24.7 0.4 %collective-permute-done.5.refs_1_ = bf16[2,192,128]{2,1,0:T(8,128)(2,1)S(1)} collective-permute-done((bf16[2,192,128]{2,1,0:T(8,128)(2,1)S(1)}, bf16[2,192,128]{2,1,0:T(8,128)(2,1)S(1)}, u32[]{:S(2)}, u32[]{:S(2)}) %collective-permute-start.5) | collective-permute-done | bytes 98336 | tf_op jit(solution)/shard_map/ppermute | solution.py:530
  25.1 0.1 collective-permute-start.6
  25.2 2.6 %collective-permute-done.7.refs_3_ = bf16[2,192,128]{2,1,0:T(8,128)(2,1)S(1)} collective-permute-done((bf16[2,192,128]{2,1,0:T(8,128)(2,1)S(1)}, bf16[2,192,128]{2,1,0:T(8,128)(2,1)S(1)}, u32[]{:S(2)}, u32[]{:S(2)}) %collective-permute-start.7) | collective-permute-done | bytes 98336 | tf_op jit(solution)/shard_map/ppermute | solution.py:530
  27.9 1.1 %shard_map.113 = f32[2,3,1,128,128]{4,3,2,1,0:T(8,128)} custom-call(f32[2,3,128,128]{3,2,1,0:T(8,128)S(1)} %get-tuple-element.24.probe_ref, bf16[7,128,128]{2,1,0:T(8,128)(2,1)S(1)} %shard_map.112.own_ref, bf16[7,128,128]{2,1,0:T(8,128)(2,1)S(1)} %collective-permute-done.9.received_ref), custom_call_target="tpu_custom_call" | custom-call | tf_op jit(solution)/shard_map/pallas_call | solution.py:422
  28.9 0.4 %shard_map.109.refs_0_ = f32[8,2,192,128]{3,2,1,0:T(8,128)S(1)} custom-call(f32[8,8,8,128]{3,2,1,0:T(8,128)S(1)} %get-tuple-element.19.table_ref, bf16[2,192,128]{2,1,0:T(8,128)(2,1)S(1)} %get-tuple-element.33.refs_0_, bf16[2,192,128]{2,1,0:T(8,128)(2,1)S(1)} %collective-permute-done.2.refs_1_, bf16[2,192,128]{2,1,0:T(8,128)(2,1)S(1)} %collective-permute-done.3.refs_2_, ...), custom_call_target="tpu_custom_call" | custom-call | tf_op jit(solution)/shard_map/pallas_call | solution.py:422
  29.3 0.3 %shard_map.110.mixed_ref = f32[8,2,192,128]{3,2,1,0:T(8,128)S(1)} custom-call(f32[8,8,8,128]{3,2,1,0:T(8,128)S(1)} %get-tuple-element.19.table_ref, f32[8,2,192,128]{3,2,1,0:T(8,128)S(1)} %shard_map.109.refs_0_, bf16[2,192,128]{2,1,0:T(8,128)(2,1)S(1)} %collective-permute-done.5.refs_1_, bf16[2,192,128]{2,1,0:T(8,128)(2,1)S(1)} %collective-permute-done.6.refs_2_, ...), custom_call_target="tpu_custom_call" | custom-call | tf_op jit(solution)/shard_map/pallas_call | solution.py:422
  29.7 1.1 %shard_map.111 = f32[2,1,192,128]{3,2,1,0:T(8,128)} custom-call(f32[8,8,8,128]{3,2,1,0:T(8,128)S(1)} %get-tuple-element.19.table_ref, f32[2,8,8,128]{3,2,1,0:T(8,128)S(1)} %get-tuple-element.20.last_ref, f32[2,192,128]{2,1,0:T(8,128)S(1)} %get-tuple-element.32.own_ref, f32[8,2,192,128]{3,2,1,0:T(8,128)S(1)} %shard_map.110.mixed_ref, ...), custom_call_target="tpu_custom_call" | custom-call | tf_op jit(solution)/shard_map/pallas_call | solution.py:422
  (6 shorter events, 0.0 us)
Async XLA Ops:
  1.6 5.9 %collective-permute-start = (bf16[392,128]{1,0:T(8,128)(2,1)S(1)}, bf16[392,128]{1,0:T(8,128)(2,1)S(1)}, u32[]{:S(2)}, u32[]{:S(2)}) collective-permute-start(bf16[392,128]{1,0:T(8,128)(2,1)S(1)} %get-tuple-element.23.own_ref), channel_id=1, source_target_pairs={{0,2},{2,0},{1,3},{3,1},{4,6},{6,4},{5,7},{7,5},{8,10},{10,8},{9,1... | collective-permute-start | bytes 301064 | tf_op jit(solution)/shard_map/ppermute | solution.py:454
  11.1 5.7 %collective-permute-start.1 = (bf16[2,192,128]{2,1,0:T(8,128)(2,1)S(1)}, bf16[2,192,128]{2,1,0:T(8,128)(2,1)S(1)}, u32[]{:S(2)}, u32[]{:S(2)}) collective-permute-start(bf16[2,192,128]{2,1,0:T(8,128)(2,1)S(1)} %get-tuple-element.29), channel_id=1, source_target_pairs={{0,2},{2,0},{1,3},{3,1},{4,6},{6,4},{5,7},{7,5},{8,10},{10,8},{9,1... | collective-permute-start | bytes 294920 | tf_op jit(solution)/shard_map/ppermute | solution.py:511
  13.7 14.2 %collective-permute-start.9 = (bf16[7,128,128]{2,1,0:T(8,128)(2,1)S(1)}, bf16[7,128,128]{2,1,0:T(8,128)(2,1)S(1)}, u32[]{:S(2)}, u32[]{:S(2)}) collective-permute-start(bf16[7,128,128]{2,1,0:T(8,128)(2,1)S(1)} %shard_map.112.own_ref), channel_id=1, source_target_pairs={{0,2},{2,0},{1,3},{3,1},{4,6},{6,4},{5,7},{7,5},{8,10},{10,8},{9,1... | collective-permute-start | bytes 688136 | tf_op jit(solution)/shard_map/ppermute | solution.py:557
  16.9 7.8 %collective-permute-start.3 = (bf16[2,192,128]{2,1,0:T(8,128)(2,1)S(1)}, bf16[2,192,128]{2,1,0:T(8,128)(2,1)S(1)}, u32[]{:S(2)}, u32[]{:S(2)}) collective-permute-start(bf16[2,192,128]{2,1,0:T(8,128)(2,1)S(1)} %get-tuple-element.33.refs_0_), channel_id=1, source_target_pairs={{0,8},{4,12},{8,0},{12,4},{1,9},{5,13},{9,1},{13,5},{2,10},{6,14},... | collective-permute-start | bytes 294920 | tf_op jit(solution)/shard_map/ppermute | solution.py:530
  19.9 5.2 %collective-permute-start.5 = (bf16[2,192,128]{2,1,0:T(8,128)(2,1)S(1)}, bf16[2,192,128]{2,1,0:T(8,128)(2,1)S(1)}, u32[]{:S(2)}, u32[]{:S(2)}) collective-permute-start(bf16[2,192,128]{2,1,0:T(8,128)(2,1)S(1)} %get-tuple-element.33.refs_0_), channel_id=1, source_target_pairs={{0,4},{4,0},{8,12},{12,8},{1,5},{5,1},{9,13},{13,9},{2,6},{6,2},{1... | collective-permute-start | bytes 294920 | tf_op jit(solution)/shard_map/ppermute | solution.py:530
  21.4 6.4 %collective-permute-start.7 = (bf16[2,192,128]{2,1,0:T(8,128)(2,1)S(1)}, bf16[2,192,128]{2,1,0:T(8,128)(2,1)S(1)}, u32[]{:S(2)}, u32[]{:S(2)}) collective-permute-start(bf16[2,192,128]{2,1,0:T(8,128)(2,1)S(1)} %get-tuple-element.33.refs_0_), channel_id=1, source_target_pairs={{0,12},{4,8},{8,4},{12,0},{1,13},{5,9},{9,5},{13,1},{2,14},{6,10},... | collective-permute-start | bytes 294920 | tf_op jit(solution)/shard_map/ppermute | solution.py:530
  21.4 7.5 %collective-permute-start.2 = (bf16[2,192,128]{2,1,0:T(8,128)(2,1)S(1)}, bf16[2,192,128]{2,1,0:T(8,128)(2,1)S(1)}, u32[]{:S(2)}, u32[]{:S(2)}) collective-permute-start(bf16[2,192,128]{2,1,0:T(8,128)(2,1)S(1)} %get-tuple-element.33.refs_0_), channel_id=1, source_target_pairs={{0,1},{1,0},{2,3},{3,2},{4,5},{5,4},{6,7},{7,6},{8,9},{9,8},{10,11... | collective-permute-start | bytes 294920 | tf_op jit(solution)/shard_map/ppermute | solution.py:533
  24.7 4.2 %collective-permute-start.4 = (bf16[2,192,128]{2,1,0:T(8,128)(2,1)S(1)}, bf16[2,192,128]{2,1,0:T(8,128)(2,1)S(1)}, u32[]{:S(2)}, u32[]{:S(2)}) collective-permute-start(bf16[2,192,128]{2,1,0:T(8,128)(2,1)S(1)} %collective-permute-done.3.refs_2_), channel_id=1, source_target_pairs={{0,1},{1,0},{2,3},{3,2},{4,5},{5,4},{6,7},{7,6},{8,9},{9,8},{10,11... | collective-permute-start | bytes 294920 | tf_op jit(solution)/shard_map/ppermute | solution.py:533
  25.1 4.2 %collective-permute-start.6 = (bf16[2,192,128]{2,1,0:T(8,128)(2,1)S(1)}, bf16[2,192,128]{2,1,0:T(8,128)(2,1)S(1)}, u32[]{:S(2)}, u32[]{:S(2)}) collective-permute-start(bf16[2,192,128]{2,1,0:T(8,128)(2,1)S(1)} %collective-permute-done.5.refs_1_), channel_id=1, source_target_pairs={{0,1},{1,0},{2,3},{3,2},{4,5},{5,4},{6,7},{7,6},{8,9},{9,8},{10,11... | collective-permute-start | bytes 294920 | tf_op jit(solution)/shard_map/ppermute | solution.py:533
  27.9 1.8 %collective-permute-start.8 = (bf16[2,192,128]{2,1,0:T(8,128)(2,1)S(1)}, bf16[2,192,128]{2,1,0:T(8,128)(2,1)S(1)}, u32[]{:S(2)}, u32[]{:S(2)}) collective-permute-start(bf16[2,192,128]{2,1,0:T(8,128)(2,1)S(1)} %collective-permute-done.7.refs_3_), channel_id=1, source_target_pairs={{0,1},{1,0},{2,3},{3,2},{4,5},{5,4},{6,7},{7,6},{8,9},{9,8},{10,11... | collective-permute-start | bytes 294920 | tf_op jit(solution)/shard_map/ppermute | solution.py:533

commit v4 on v3

--- a/solution.py
+++ b/solution.py
@@ -372,13 +372,14 @@
                 mixed_ref[k, part, here] = functools.reduce(jnp.add, terms).reshape(chunk, lanes)
 
 
-def spectral_kernel(table_ref, last_ref, own_ref, mixed_ref, *refs, first, chunk):
-    refs, (out_hbm, result, sems) = refs[:-3], refs[-3:]
+def finish_kernel(probe_ref, table_ref, last_ref, own_ref, mixed_ref, *refs, first, chunk):
+    refs, (out_hbm, probe_hbm, result, sems) = refs[:-4], refs[-4:]
     parts, rows, lanes = own_ref.shape
     components = last_ref.shape[1]
     height = table_ref.shape[2]
     folded = (chunk // height, height, lanes)
-    copies = []
+    copies = [pltpu.make_async_copy(probe_ref, probe_hbm, sems.at[0])]
+    copies[0].start()
     for part in range(parts):
         for start in range(0, rows, chunk):
             here = pl.ds(start, chunk)
@@ -394,15 +395,14 @@
             while len(terms) > 1:
                 terms = [sum(terms[k : k + 2][1:], terms[k]) for k in range(0, len(terms), 2)]
             result[part, here] = terms[0].reshape(chunk, lanes)
-        copies.append(
-            pltpu.make_async_copy(result.at[part], out_hbm.at[part, 0], sems.at[part])
-        )
-        copies[-1].start()
+            source, target = result.at[part, here], out_hbm.at[part, 0, here]
+            copies.append(pltpu.make_async_copy(source, target, sems.at[len(copies)]))
+            copies[-1].start()
     for copy in copies:
         copy.wait()
 
 
-def probe_kernel(probe_ref, own_ref, received_ref, out_ref):
+def probe_kernel(probe_ref, own_ref, received_ref, new_ref):
     modes = probe_ref.shape[1]
     density = own_ref[2 * modes].astype(jnp.float32) + received_ref[2 * modes].astype(jnp.float32)
     inverse = 1.0 / (density + 0.1 * jnp.max(density) + 1e-06)
@@ -410,7 +410,7 @@
         for m in range(modes):
             k = part * modes + m
             numerator = own_ref[k].astype(jnp.float32) + received_ref[k].astype(jnp.float32)
-            out_ref[part, m, 0] = (probe_ref[part, m] + numerator * inverse).T
+            new_ref[part, m, 0] = (probe_ref[part, m] + numerator * inverse).T
 
 
 def call(kernel, inputs, places, outputs, scratch=(), limit=4, out="v"):
@@ -456,7 +456,7 @@
         below = lax.ppermute(message, "tile", [(i + 1, i) for i in range(tiles - 1)])
         above = lax.ppermute(message, "tile", [(i, i + 1) for i in range(tiles - 1)])
 
-    near, far = gather_order(zs)[0], gather_order(zs)[-1]
+    near, far = zs - 1, zs // 2
     middle = [dz for dz in range(1, zs) if dz not in (near, far)]
     stages = [
         [(dz, dm) for dz in (0, near) for dm in range(ms)],
@@ -542,25 +542,21 @@
             shape((components, 2, cols, rows), f32),
         )
         first += len(stage)
-    inputs = [table, last_table, object_new, mixed] + [pieces[s] for s in stages[2]]
-    object_out = call(
-        functools.partial(spectral_kernel, first=first, chunk=64),
-        inputs,
-        "v" * len(inputs),
-        shape(object_field.shape, f32),
-        (pltpu.VMEM((2, cols, rows), f32), pltpu.SemaphoreType.DMA((2,))),
-        out="h",
-    )
     for distance in [1 << k for k in range(1, tiles.bit_length() - 1)]:
         other = lax.ppermute(share, "tile", swap_pairs(tiles, distance))
         share = (share.astype(f32) + other.astype(f32)).astype(bf16)
     other = lax.ppermute(share, "tile", swap_pairs(tiles, 1))
-    probe_out = call(probe_kernel, (turned, share, other), "vvv", shape(probe_field.shape, f32))
+    probe_new = call(probe_kernel, (turned, share, other), "vvv", shape(probe_field.shape, f32))
+    inputs = [probe_new, table, last_table, object_new, mixed] + [pieces[s] for s in stages[2]]
+    object_out, probe_out = call(
+        functools.partial(finish_kernel, first=first, chunk=64),
+        inputs,
+        "v" * len(inputs),
+        (shape(object_field.shape, f32), shape(probe_field.shape, f32)),
+        (pltpu.VMEM((2, cols, rows), f32), pltpu.SemaphoreType.DMA((1 + 2 * cols // 64,))),
+        out="h",
+    )
     return (jnp.transpose(object_out, (0, 1, 3, 2)), probe_out)
-
-
-def gather_order(zs):
-    return [zs // 2] + [dz for dz in range(1, zs) if dz != zs // 2]
 
 
 def solution(mesh):

time: 30.9 us -> 29.5 us (0.955)
  waiting for transfers between devices: 10 us -> 8.82 us
  Pallas kernels: 10.2 us -> 9.43 us
  starting transfers between devices: 9.84 us -> 10.3 us
    ppermute x3, waiting for transfers between devices: 6.3 us -> 5.02 us  [body(): pieces[dz, 0] = lax.ppermute(sent, 'energy', swap_pairs(zs, dz))]
    pallas_call x10, Pallas kernels: 10.2 us -> 9.43 us  [call(): pl.pallas_call(kernel, out_shape=outputs, in_specs=[pl.BlockSpec(memory_s...]
    ppermute x4, starting transfers between devices: 0.11 us -> 0.52 us  [body(): pieces[dz, dm] = lax.ppermute(pieces[dz, 0], 'mode', swap_pairs(ms, dm))]
  transfers between devices with their start and end apart: 10 -> 10, of which waited for: 5 -> 5; matrix products, arithmetic and copies ran while one was open for 0% -> 0% of each run, Pallas kernels for 15% -> 13%
where the time goes in v4:
time: 29.5 us; the launch traced here: 29.3 us
  starting transfers between devices  10.3 us (35%)
  Pallas kernels  9.43 us (32%)
  waiting for transfers between devices  8.82 us (30%)
  between operations  0.72 us (2%)
    pallas_call x10, Pallas kernels, call(): pl.pallas_call(kernel, out_shape=outputs, in_specs=[pl.BlockSpec(memory_s...  9.43 us
    ppermute x3, waiting for transfers between devices, body(): pieces[dz, 0] = lax.ppermute(sent, 'energy', swap_pairs(zs, dz))  5.02 us
    ppermute x3, starting transfers between devices, body(): pieces[dz, 0] = lax.ppermute(sent, 'energy', swap_pairs(zs, dz))  4.62 us
    ppermute x1, starting transfers between devices, body(): below = above = lax.ppermute(message, 'tile', swap_pairs(2, 1))  3.03 us
    ppermute x1, waiting for transfers between devices, body(): received = lax.ppermute(lower, 'tile', swap_pairs(2, 1))  2.56 us
    ppermute x1, starting transfers between devices, body(): received = lax.ppermute(lower, 'tile', swap_pairs(2, 1))  1.89 us
    ppermute x1, waiting for transfers between devices, body(): below = above = lax.ppermute(message, 'tile', swap_pairs(2, 1))  1.16 us
  transfers between devices with their start and end apart: 10, of which 5 were waited for; matrix products, arithmetic and copies ran while one was open for 0% of the time, Pallas kernels for 13%

profile of v4, /device:TPU:0, one launch (start us, length us, event | category | flops | bytes accessed | tf_op | source)
XLA Modules:
  0.0 29.3 jit_solution(939439018287273377)
XLA Ops:
  0.6 1.0 %shard_map.105 = (bf16[392,128]{1,0:T(8,128)(2,1)S(1)}, f32[2,192,128]{2,1,0:T(8,128)S(1)}) custom-call(s32[2,8]{1,0:T(2,128)} %bitcast.4, f32[2,1,192,128]{3,2,1,0:T(8,128)} %bitcast.3), custom_call_target="tpu_custom_call" | custom-call | tf_op jit(solution)/shard_map/pallas_call | solution.py:422
  1.6 3.0 %collective-permute-start = (bf16[392,128]{1,0:T(8,128)(2,1)S(1)}, bf16[392,128]{1,0:T(8,128)(2,1)S(1)}, u32[]{:S(2)}, u32[]{:S(2)}) collective-permute-start(bf16[392,128]{1,0:T(8,128)(2,1)S(1)} %get-tuple-element.23.own_ref), channel_id=1, source_target_pairs={{0,2},{2,0},{1,3},{3,1},{4,6},{6,4},{5,7},{7,5},{8,10},{10,8},{9,1... | collective-permute-start | bytes 301064 | tf_op jit(solution)/shard_map/ppermute | solution.py:454
  4.6 1.7 %shard_map.104 = (s32[2,8]{1,0:T(2,128)S(1)}, bf16[256,256]{1,0:T(8,128)(2,1)S(1)}, bf16[256,256]{1,0:T(8,128)(2,1)S(1)}, f32[2,3,128,128]{3,2,1,0:T(8,128)S(1)}...) custom-call(s32[2,8]{1,0:T(2,128)} %bitcast.5, ...), custom_call_target="tpu_custom_call" | custom-call | tf_op jit(solution)/shard_map/pallas_call | solution.py:422
  6.3 1.2 %collective-permute-done.below_ref.above_ref = bf16[392,128]{1,0:T(8,128)(2,1)S(1)} collective-permute-done((bf16[392,128]{1,0:T(8,128)(2,1)S(1)}, bf16[392,128]{1,0:T(8,128)(2,1)S(1)}, u32[]{:S(2)}, u32[]{:S(2)}) %collective-permute-start) | collective-permute-done | bytes 100384 | tf_op jit(solution)/shard_map/ppermute | solution.py:454
  7.5 3.6 %shard_map.106 = (f32[2,192,128]{2,1,0:T(8,128)S(1)}, bf16[2,192,128]{2,1,0:T(8,128)(2,1)S(1)}, f32[8,3,2,128,128]{4,3,2,1,0:T(8,128)S(1)}, f32[8,2,128,128]{3,2,1,0:T(8,128)S(1)}) custom-call(s32[2,8]{1,0:T(2,128)S(1)} %get-tuple-element.22.offsets_ref, bf16[392,128]{1,0:T(8,128)(2,1)S(1)} %get-tuple-element.23.own_ref, ...), custom_call_target="tpu_custom_call" | custom-call | tf_op jit(solution)/shard_map/pallas_call | solution.py:422
  11.1 1.9 %collective-permute-start.2 = (bf16[2,192,128]{2,1,0:T(8,128)(2,1)S(1)}, bf16[2,192,128]{2,1,0:T(8,128)(2,1)S(1)}, u32[]{:S(2)}, u32[]{:S(2)}) collective-permute-start(bf16[2,192,128]{2,1,0:T(8,128)(2,1)S(1)} %get-tuple-element.33), channel_id=1, source_target_pairs={{0,2},{2,0},{1,3},{3,1},{4,6},{6,4},{5,7},{7,5},{8,10},{10,8},{9,1... | collective-permute-start | bytes 294920 | tf_op jit(solution)/shard_map/ppermute | solution.py:511
  13.0 0.7 %shard_map.107.own_ref = bf16[7,128,128]{2,1,0:T(8,128)(2,1)S(1)} custom-call(f32[8,3,2,128,128]{4,3,2,1,0:T(8,128)S(1)} %get-tuple-element.27.change_ref, f32[8,2,128,128]{3,2,1,0:T(8,128)S(1)} %get-tuple-element.28.window_ref), custom_call_target="tpu_custom_call" | custom-call | tf_op jit(solution)/shard_map/pallas_call | solution.py:422
  13.7 0.3 collective-permute-start.1
  13.9 0.3 %shard_map.109.inverse_ref = f32[192,128]{1,0:T(8,128)S(1)} custom-call(bf16[392,128]{1,0:T(8,128)(2,1)S(1)} %collective-permute-done.below_ref.above_ref, f32[128,128]{1,0:T(8,128)S(1)} %get-tuple-element.34.power_ref, f32[192,128]{1,0:T(8,128)S(1)} %get-tuple-element.35.weight_ref), custom_call_target="tpu_custom_call" | custom-call | tf_op jit(solution)/shard_map/pallas_call | solution.py:422
  14.3 2.6 %collective-permute-done.2.received_ref = bf16[2,192,128]{2,1,0:T(8,128)(2,1)S(1)} collective-permute-done((bf16[2,192,128]{2,1,0:T(8,128)(2,1)S(1)}, bf16[2,192,128]{2,1,0:T(8,128)(2,1)S(1)}, u32[]{:S(2)}, u32[]{:S(2)}) %collective-permute-start.2) | collective-permute-done | bytes 98336 | tf_op jit(solution)/shard_map/ppermute | solution.py:511
  16.8 0.1 shard_map.110
  16.9 4.0 %collective-permute-start.4 = (bf16[2,192,128]{2,1,0:T(8,128)(2,1)S(1)}, bf16[2,192,128]{2,1,0:T(8,128)(2,1)S(1)}, u32[]{:S(2)}, u32[]{:S(2)}) collective-permute-start(bf16[2,192,128]{2,1,0:T(8,128)(2,1)S(1)} %get-tuple-element.37.refs_0_), channel_id=1, source_target_pairs={{0,12},{4,8},{8,4},{12,0},{1,13},{5,9},{9,5},{13,1},{2,14},{6,10},... | collective-permute-start | bytes 294920 | tf_op jit(solution)/shard_map/ppermute | solution.py:530
  20.9 0.6 %collective-permute-start.8 = (bf16[2,192,128]{2,1,0:T(8,128)(2,1)S(1)}, bf16[2,192,128]{2,1,0:T(8,128)(2,1)S(1)}, u32[]{:S(2)}, u32[]{:S(2)}) collective-permute-start(bf16[2,192,128]{2,1,0:T(8,128)(2,1)S(1)} %get-tuple-element.37.refs_0_), channel_id=1, source_target_pairs={{0,8},{4,12},{8,0},{12,4},{1,9},{5,13},{9,1},{13,5},{2,10},{6,14},... | collective-permute-start | bytes 294920 | tf_op jit(solution)/shard_map/ppermute | solution.py:530
  21.5 2.4 %collective-permute-done.4.refs_2_ = bf16[2,192,128]{2,1,0:T(8,128)(2,1)S(1)} collective-permute-done((bf16[2,192,128]{2,1,0:T(8,128)(2,1)S(1)}, bf16[2,192,128]{2,1,0:T(8,128)(2,1)S(1)}, u32[]{:S(2)}, u32[]{:S(2)}) %collective-permute-start.4) | collective-permute-done | bytes 98336 | tf_op jit(solution)/shard_map/ppermute | solution.py:530
  24.0 0.0 collective-permute-start.5
  24.0 2.6 %collective-permute-done.6.refs_1_ = bf16[2,192,128]{2,1,0:T(8,128)(2,1)S(1)} collective-permute-done((bf16[2,192,128]{2,1,0:T(8,128)(2,1)S(1)}, bf16[2,192,128]{2,1,0:T(8,128)(2,1)S(1)}, u32[]{:S(2)}, u32[]{:S(2)}) %collective-permute-start.6) | collective-permute-done | bytes 98336 | tf_op jit(solution)/shard_map/ppermute | solution.py:530
  26.5 0.0 collective-permute-start.7
  26.6 0.5 %collective-permute-start.9 = (bf16[2,192,128]{2,1,0:T(8,128)(2,1)S(1)}, bf16[2,192,128]{2,1,0:T(8,128)(2,1)S(1)}, u32[]{:S(2)}, u32[]{:S(2)}) collective-permute-start(bf16[2,192,128]{2,1,0:T(8,128)(2,1)S(1)} %collective-permute-done.8.refs_3_), channel_id=1, source_target_pairs={{0,1},{1,0},{2,3},{3,2},{4,5},{5,4},{6,7},{7,6},{8,9},{9,8},{10,11... | collective-permute-start | bytes 294920 | tf_op jit(solution)/shard_map/ppermute | solution.py:533
  27.1 0.3 %shard_map.108.probe_ref = f32[2,3,1,128,128]{4,3,2,1,0:T(8,128)S(1)} custom-call(f32[2,3,128,128]{3,2,1,0:T(8,128)S(1)} %get-tuple-element.21.probe_ref, bf16[7,128,128]{2,1,0:T(8,128)(2,1)S(1)} %shard_map.107.own_ref, bf16[7,128,128]{2,1,0:T(8,128)(2,1)S(1)} %collective-permute-done.1.received_ref), custom_call_target="tpu_custom_call" | custom-call | tf_op jit(solution)/shard_map/pallas_call | solution.py:422
  27.4 0.0 collective-permute-done.5.refs_3_
  27.4 0.4 %shard_map.111.refs_0_ = f32[8,2,192,128]{3,2,1,0:T(8,128)S(1)} custom-call(f32[8,8,8,128]{3,2,1,0:T(8,128)S(1)} %get-tuple-element.29.table_ref, bf16[2,192,128]{2,1,0:T(8,128)(2,1)S(1)} %get-tuple-element.37.refs_0_, bf16[2,192,128]{2,1,0:T(8,128)(2,1)S(1)} %collective-permute-done.3.refs_1_, bf16[2,192,128]{2,1,0:T(8,128)(2,1)S(1)} %collective-permute-done.4.refs_2_, ...), custom_call_target="tpu_custom_call" | custom-call | tf_op jit(solution)/shard_map/pallas_call | solution.py:422
  27.8 0.1 collective-permute-done.7.refs_2_
  27.8 0.3 %shard_map.112.mixed_ref = f32[8,2,192,128]{3,2,1,0:T(8,128)S(1)} custom-call(f32[8,8,8,128]{3,2,1,0:T(8,128)S(1)} %get-tuple-element.29.table_ref, f32[8,2,192,128]{3,2,1,0:T(8,128)S(1)} %shard_map.111.refs_0_, bf16[2,192,128]{2,1,0:T(8,128)(2,1)S(1)} %collective-permute-done.6.refs_1_, bf16[2,192,128]{2,1,0:T(8,128)(2,1)S(1)} %collective-permute-done.7.refs_2_, ...), custom_call_target="tpu_custom_call" | custom-call | tf_op jit(solution)/shard_map/pallas_call | solution.py:422
  28.2 1.1 %shard_map.113 = (f32[2,1,192,128]{3,2,1,0:T(8,128)}, f32[2,3,1,128,128]{4,3,2,1,0:T(8,128)}) custom-call(f32[2,3,1,128,128]{4,3,2,1,0:T(8,128)S(1)} %shard_map.108.probe_ref, f32[8,8,8,128]{3,2,1,0:T(8,128)S(1)} %get-tuple-element.29.table_ref, f32[2,8,8,128]{3,2,1,0:T(8,128)S(1)} %get-tuple-element.30.last_ref, ...), custom_call_target="tpu_custom_call" | custom-call | tf_op jit(solution)/shard_map/pallas_call | solution.py:422
  (6 shorter events, 0.0 us)
Async XLA Ops:
  1.6 5.9 %collective-permute-start = (bf16[392,128]{1,0:T(8,128)(2,1)S(1)}, bf16[392,128]{1,0:T(8,128)(2,1)S(1)}, u32[]{:S(2)}, u32[]{:S(2)}) collective-permute-start(bf16[392,128]{1,0:T(8,128)(2,1)S(1)} %get-tuple-element.23.own_ref), channel_id=1, source_target_pairs={{0,2},{2,0},{1,3},{3,1},{4,6},{6,4},{5,7},{7,5},{8,10},{10,8},{9,1... | collective-permute-start | bytes 301064 | tf_op jit(solution)/shard_map/ppermute | solution.py:454
  11.1 5.7 %collective-permute-start.2 = (bf16[2,192,128]{2,1,0:T(8,128)(2,1)S(1)}, bf16[2,192,128]{2,1,0:T(8,128)(2,1)S(1)}, u32[]{:S(2)}, u32[]{:S(2)}) collective-permute-start(bf16[2,192,128]{2,1,0:T(8,128)(2,1)S(1)} %get-tuple-element.33), channel_id=1, source_target_pairs={{0,2},{2,0},{1,3},{3,1},{4,6},{6,4},{5,7},{7,5},{8,10},{10,8},{9,1... | collective-permute-start | bytes 294920 | tf_op jit(solution)/shard_map/ppermute | solution.py:511
  13.7 13.4 %collective-permute-start.1 = (bf16[7,128,128]{2,1,0:T(8,128)(2,1)S(1)}, bf16[7,128,128]{2,1,0:T(8,128)(2,1)S(1)}, u32[]{:S(2)}, u32[]{:S(2)}) collective-permute-start(bf16[7,128,128]{2,1,0:T(8,128)(2,1)S(1)} %shard_map.107.own_ref), channel_id=1, source_target_pairs={{0,2},{2,0},{1,3},{3,1},{4,6},{6,4},{5,7},{7,5},{8,10},{10,8},{9,1... | collective-permute-start | bytes 688136 | tf_op jit(solution)/shard_map/ppermute | solution.py:548
  16.9 7.1 %collective-permute-start.4 = (bf16[2,192,128]{2,1,0:T(8,128)(2,1)S(1)}, bf16[2,192,128]{2,1,0:T(8,128)(2,1)S(1)}, u32[]{:S(2)}, u32[]{:S(2)}) collective-permute-start(bf16[2,192,128]{2,1,0:T(8,128)(2,1)S(1)} %get-tuple-element.37.refs_0_), channel_id=1, source_target_pairs={{0,12},{4,8},{8,4},{12,0},{1,13},{5,9},{9,5},{13,1},{2,14},{6,10},... | collective-permute-start | bytes 294920 | tf_op jit(solution)/shard_map/ppermute | solution.py:530
  20.9 5.7 %collective-permute-start.6 = (bf16[2,192,128]{2,1,0:T(8,128)(2,1)S(1)}, bf16[2,192,128]{2,1,0:T(8,128)(2,1)S(1)}, u32[]{:S(2)}, u32[]{:S(2)}) collective-permute-start(bf16[2,192,128]{2,1,0:T(8,128)(2,1)S(1)} %get-tuple-element.37.refs_0_), channel_id=1, source_target_pairs={{0,4},{4,0},{8,12},{12,8},{1,5},{5,1},{9,13},{13,9},{2,6},{6,2},{1... | collective-permute-start | bytes 294920 | tf_op jit(solution)/shard_map/ppermute | solution.py:530
  20.9 5.7 %collective-permute-start.8 = (bf16[2,192,128]{2,1,0:T(8,128)(2,1)S(1)}, bf16[2,192,128]{2,1,0:T(8,128)(2,1)S(1)}, u32[]{:S(2)}, u32[]{:S(2)}) collective-permute-start(bf16[2,192,128]{2,1,0:T(8,128)(2,1)S(1)} %get-tuple-element.37.refs_0_), channel_id=1, source_target_pairs={{0,8},{4,12},{8,0},{12,4},{1,9},{5,13},{9,1},{13,5},{2,10},{6,14},... | collective-permute-start | bytes 294920 | tf_op jit(solution)/shard_map/ppermute | solution.py:530
  21.5 5.8 %collective-permute-start.3 = (bf16[2,192,128]{2,1,0:T(8,128)(2,1)S(1)}, bf16[2,192,128]{2,1,0:T(8,128)(2,1)S(1)}, u32[]{:S(2)}, u32[]{:S(2)}) collective-permute-start(bf16[2,192,128]{2,1,0:T(8,128)(2,1)S(1)} %get-tuple-element.37.refs_0_), channel_id=1, source_target_pairs={{0,1},{1,0},{2,3},{3,2},{4,5},{5,4},{6,7},{7,6},{8,9},{9,8},{10,11... | collective-permute-start | bytes 294920 | tf_op jit(solution)/shard_map/ppermute | solution.py:533
  24.0 3.4 %collective-permute-start.5 = (bf16[2,192,128]{2,1,0:T(8,128)(2,1)S(1)}, bf16[2,192,128]{2,1,0:T(8,128)(2,1)S(1)}, u32[]{:S(2)}, u32[]{:S(2)}) collective-permute-start(bf16[2,192,128]{2,1,0:T(8,128)(2,1)S(1)} %collective-permute-done.4.refs_2_), channel_id=1, source_target_pairs={{0,1},{1,0},{2,3},{3,2},{4,5},{5,4},{6,7},{7,6},{8,9},{9,8},{10,11... | collective-permute-start | bytes 294920 | tf_op jit(solution)/shard_map/ppermute | solution.py:533
  26.5 1.3 %collective-permute-start.7 = (bf16[2,192,128]{2,1,0:T(8,128)(2,1)S(1)}, bf16[2,192,128]{2,1,0:T(8,128)(2,1)S(1)}, u32[]{:S(2)}, u32[]{:S(2)}) collective-permute-start(bf16[2,192,128]{2,1,0:T(8,128)(2,1)S(1)} %collective-permute-done.6.refs_1_), channel_id=1, source_target_pairs={{0,1},{1,0},{2,3},{3,2},{4,5},{5,4},{6,7},{7,6},{8,9},{9,8},{10,11... | collective-permute-start | bytes 294920 | tf_op jit(solution)/shard_map/ppermute | solution.py:533
  26.6 1.6 %collective-permute-start.9 = (bf16[2,192,128]{2,1,0:T(8,128)(2,1)S(1)}, bf16[2,192,128]{2,1,0:T(8,128)(2,1)S(1)}, u32[]{:S(2)}, u32[]{:S(2)}) collective-permute-start(bf16[2,192,128]{2,1,0:T(8,128)(2,1)S(1)} %collective-permute-done.8.refs_3_), channel_id=1, source_target_pairs={{0,1},{1,0},{2,3},{3,2},{4,5},{5,4},{6,7},{7,6},{8,9},{9,8},{10,11... | collective-permute-start | bytes 294920 | tf_op jit(solution)/shard_map/ppermute | solution.py:533

commit v5 on v4

--- a/solution.py
+++ b/solution.py
@@ -88,6 +88,7 @@
     weight_ref,
     analysis_table_ref,
     last_table_ref,
+    late_table_ref,
     offsets_ref,
     analysis_ref,
     basis_ref,
@@ -125,12 +126,17 @@
     z = lax.axis_index("energy")
     m = lax.axis_index("mode")
     tile = analysis_table_ref.shape[2:]
+    late = [0.0] * len(sources)
     for k in range(threshold_ref.shape[0]):
+        half = 0.5 * basis_ref[z * ms + m, k]
         for number, (dz, dm) in enumerate(sources):
             label = (z ^ dz) * ms + (m ^ dm)
-            analysis_table_ref[number, k] = jnp.full(tile, analysis_ref[k, label])
-        last_table_ref[0, k] = jnp.full(tile, 0.5 * basis_ref[z * ms + m, k])
-        last_table_ref[1, k] = jnp.full(tile, threshold_ref[k])
+            weight = half * analysis_ref[k, label]
+            analysis_table_ref[number, k] = jnp.full(tile, weight)
+            late[number] += weight
+        last_table_ref[k] = jnp.full(tile, jnp.maximum(half, -half) * threshold_ref[k])
+    for number in range(len(sources)):
+        late_table_ref[number] = jnp.full(tile, late[number])
     copies[0].wait()
     copies[1].wait()
     power = jnp.zeros((extent, extent), jnp.float32)
@@ -157,9 +163,10 @@
     here = pl.ds(col, extent)
     lane = lax.broadcasted_iota(jnp.int32, (extent, extent), 1)
     found = []
-    for part in range(2):
-        left = pltpu.roll(extended[part, 0, here], extent - row, 1)
-        right = pltpu.roll(extended[part, 1, here], extent - row, 1)
+    amount = lax.rem(extent - row, extent)
+    for part in range(2):
+        left = pltpu.roll(extended[part, 0, here], amount, 1)
+        right = pltpu.roll(extended[part, 1, here], amount, 1)
         found.append(jnp.where(lane < extent - row, left, right))
     return found
 
@@ -357,26 +364,31 @@
 def mix_kernel(table_ref, *refs, first, chained, chunk):
     mixed_ref = refs[-1]
     refs = refs[:-1]
-    before, refs = (refs[0], refs[1:]) if chained else (None, refs)
-    components, parts, rows, lanes = mixed_ref.shape
-    height = table_ref.shape[2]
+    before, own_ref, refs = (refs[0], refs[1], refs[2:]) if chained else (None, None, refs)
+    parts, rows, lanes = mixed_ref.shape[1:]
+    components, height = table_ref.shape[1:3]
     folded = (chunk // height, height, lanes)
     for part in range(parts):
         for start in range(0, rows, chunk):
             here = pl.ds(start, chunk)
             values = [ref[part, here].astype(jnp.float32).reshape(folded) for ref in refs]
+            base = 0.5 * own_ref[part, here].reshape(folded) if chained else None
             for k in range(components):
                 terms = [table_ref[first + n, k] * value for n, value in enumerate(values)]
-                if before is not None:
+                if chained:
                     terms.insert(0, before[k, part, here].reshape(folded))
-                mixed_ref[k, part, here] = functools.reduce(jnp.add, terms).reshape(chunk, lanes)
-
-
-def finish_kernel(probe_ref, table_ref, last_ref, own_ref, mixed_ref, *refs, first, chunk):
+                total = functools.reduce(jnp.add, terms)
+                mixed_ref[k, part, here] = total.reshape(chunk, lanes)
+                if chained:
+                    base += total
+            if chained:
+                mixed_ref[components, part, here] = base.reshape(chunk, lanes)
+
+
+def finish_kernel(probe_ref, table_ref, last_ref, late_ref, mixed_ref, *refs, first, chunk):
     refs, (out_hbm, probe_hbm, result, sems) = refs[:-4], refs[-4:]
-    parts, rows, lanes = own_ref.shape
-    components = last_ref.shape[1]
-    height = table_ref.shape[2]
+    parts, rows, lanes = mixed_ref.shape[1:]
+    components, height = table_ref.shape[1:3]
     folded = (chunk // height, height, lanes)
     copies = [pltpu.make_async_copy(probe_ref, probe_hbm, sems.at[0])]
     copies[0].start()
@@ -384,17 +396,16 @@
         for start in range(0, rows, chunk):
             here = pl.ds(start, chunk)
             values = [ref[part, here].astype(jnp.float32).reshape(folded) for ref in refs]
-            terms = [0.5 * own_ref[part, here].reshape(folded)]
+            found = mixed_ref[components, part, here].reshape(folded)
+            for n, value in enumerate(values):
+                found += late_ref[first + n] * value
             for k in range(components):
                 c = mixed_ref[k, part, here].reshape(folded)
                 for n, value in enumerate(values):
                     c += table_ref[first + n, k] * value
-                t = last_ref[1, k]
-                c = c - jnp.minimum(jnp.maximum(c, -t), t)
-                terms.append(last_ref[0, k] * c)
-            while len(terms) > 1:
-                terms = [sum(terms[k : k + 2][1:], terms[k]) for k in range(0, len(terms), 2)]
-            result[part, here] = terms[0].reshape(chunk, lanes)
+                t = last_ref[k]
+                found -= jnp.minimum(jnp.maximum(c, -t), t)
+            result[part, here] = found.reshape(chunk, lanes)
             source, target = result.at[part, here], out_hbm.at[part, 0, here]
             copies.append(pltpu.make_async_copy(source, target, sems.at[len(copies)]))
             copies[-1].start()
@@ -465,7 +476,7 @@
     ]
     sources = sum(stages, [])
     components = threshold.shape[0]
-    offsets, forward, backward, turned, moduli, power, weight, table, last_table = call(
+    offsets, forward, backward, turned, moduli, power, weight, table, last_table, late_table = call(
         functools.partial(turn_kernel, sources=tuple(sources), sizes=(zs, ms)),
         (offsets, analysis, spectra_basis, threshold, forward, backward, probe_field, modulus),
         "hhhhhhhh",
@@ -478,7 +489,8 @@
             shape((extent, extent), f32),
             shape((cols, rows), f32),
             shape((len(sources), components, 8, LANES), f32),
-            shape((2, components, 8, LANES), f32),
+            shape((components, 8, LANES), f32),
+            shape((len(sources), 8, LANES), f32),
         ),
         (
             pltpu.SMEM((2, positions), jnp.int32),
@@ -533,13 +545,14 @@
             pieces[dz, dm] = lax.ppermute(pieces[dz, 0], "mode", swap_pairs(ms, dm))
     mixed = None
     first = 0
-    for stage in stages[:2]:
-        inputs = [table] + ([] if mixed is None else [mixed]) + [pieces[s] for s in stage]
+    for number, stage in enumerate(stages[:2]):
+        before = [] if mixed is None else [mixed, object_new]
+        inputs = [table] + before + [pieces[s] for s in stage]
         mixed = call(
             functools.partial(mix_kernel, first=first, chained=mixed is not None, chunk=64),
             inputs,
             "v" * len(inputs),
-            shape((components, 2, cols, rows), f32),
+            shape((components + number, 2, cols, rows), f32),
         )
         first += len(stage)
     for distance in [1 << k for k in range(1, tiles.bit_length() - 1)]:
@@ -547,7 +560,7 @@
         share = (share.astype(f32) + other.astype(f32)).astype(bf16)
     other = lax.ppermute(share, "tile", swap_pairs(tiles, 1))
     probe_new = call(probe_kernel, (turned, share, other), "vvv", shape(probe_field.shape, f32))
-    inputs = [probe_new, table, last_table, object_new, mixed] + [pieces[s] for s in stages[2]]
+    inputs = [probe_new, table, last_table, late_table, mixed] + [pieces[s] for s in stages[2]]
     object_out, probe_out = call(
         functools.partial(finish_kernel, first=first, chunk=64),
         inputs,

time: 29.5 us -> 29.4 us (level)
  no operation moved by 1% of the time
where the time goes in v5:
time: 29.4 us; the launch traced here: 29.2 us
  starting transfers between devices  10.3 us (35%)
  Pallas kernels  9.45 us (32%)
  waiting for transfers between devices  8.74 us (30%)
  between operations  0.72 us (2%)
    pallas_call x10, Pallas kernels, call(): pl.pallas_call(kernel, out_shape=outputs, in_specs=[pl.BlockSpec(memory_s...  9.45 us
    ppermute x3, waiting for transfers between devices, body(): pieces[dz, 0] = lax.ppermute(sent, 'energy', swap_pairs(zs, dz))  5.02 us
    ppermute x3, starting transfers between devices, body(): pieces[dz, 0] = lax.ppermute(sent, 'energy', swap_pairs(zs, dz))  4.62 us
    ppermute x1, starting transfers between devices, body(): below = above = lax.ppermute(message, 'tile', swap_pairs(2, 1))  3.03 us
    ppermute x1, waiting for transfers between devices, body(): received = lax.ppermute(lower, 'tile', swap_pairs(2, 1))  2.56 us
    ppermute x1, starting transfers between devices, body(): received = lax.ppermute(lower, 'tile', swap_pairs(2, 1))  1.9 us
    ppermute x1, waiting for transfers between devices, body(): below = above = lax.ppermute(message, 'tile', swap_pairs(2, 1))  1.08 us
  transfers between devices with their start and end apart: 10, of which 5 were waited for; matrix products, arithmetic and copies ran while one was open for 0% of the time, Pallas kernels for 13%

profile of v5, /device:TPU:0, one launch (start us, length us, event | category | flops | bytes accessed | tf_op | source)
XLA Modules:
  0.0 29.2 jit_solution(3382023870909359570)
XLA Ops:
  0.6 1.0 %shard_map.105 = (bf16[392,128]{1,0:T(8,128)(2,1)S(1)}, f32[2,192,128]{2,1,0:T(8,128)S(1)}) custom-call(s32[2,8]{1,0:T(2,128)} %bitcast.4, f32[2,1,192,128]{3,2,1,0:T(8,128)} %bitcast.3), custom_call_target="tpu_custom_call" | custom-call | tf_op jit(solution)/shard_map/pallas_call | solution.py:433
  1.6 3.0 %collective-permute-start = (bf16[392,128]{1,0:T(8,128)(2,1)S(1)}, bf16[392,128]{1,0:T(8,128)(2,1)S(1)}, u32[]{:S(2)}, u32[]{:S(2)}) collective-permute-start(bf16[392,128]{1,0:T(8,128)(2,1)S(1)} %get-tuple-element.24.own_ref), channel_id=1, source_target_pairs={{0,2},{2,0},{1,3},{3,1},{4,6},{6,4},{5,7},{7,5},{8,10},{10,8},{9,1... | collective-permute-start | bytes 301064 | tf_op jit(solution)/shard_map/ppermute | solution.py:465
  4.6 1.8 %shard_map.104 = (s32[2,8]{1,0:T(2,128)S(1)}, bf16[256,256]{1,0:T(8,128)(2,1)S(1)}, bf16[256,256]{1,0:T(8,128)(2,1)S(1)}, f32[2,3,128,128]{3,2,1,0:T(8,128)S(1)}...) custom-call(s32[2,8]{1,0:T(2,128)} %bitcast.5, ...), custom_call_target="tpu_custom_call" | custom-call | tf_op jit(solution)/shard_map/pallas_call | solution.py:433
  6.4 1.1 %collective-permute-done.below_ref.above_ref = bf16[392,128]{1,0:T(8,128)(2,1)S(1)} collective-permute-done((bf16[392,128]{1,0:T(8,128)(2,1)S(1)}, bf16[392,128]{1,0:T(8,128)(2,1)S(1)}, u32[]{:S(2)}, u32[]{:S(2)}) %collective-permute-start) | collective-permute-done | bytes 100384 | tf_op jit(solution)/shard_map/ppermute | solution.py:465
  7.5 3.6 %shard_map.106 = (f32[2,192,128]{2,1,0:T(8,128)S(1)}, bf16[2,192,128]{2,1,0:T(8,128)(2,1)S(1)}, f32[8,3,2,128,128]{4,3,2,1,0:T(8,128)S(1)}, f32[8,2,128,128]{3,2,1,0:T(8,128)S(1)}) custom-call(s32[2,8]{1,0:T(2,128)S(1)} %get-tuple-element.23.offsets_ref, bf16[392,128]{1,0:T(8,128)(2,1)S(1)} %get-tuple-element.24.own_ref, ...), custom_call_target="tpu_custom_call" | custom-call | tf_op jit(solution)/shard_map/pallas_call | solution.py:433
  11.1 1.9 %collective-permute-start.2 = (bf16[2,192,128]{2,1,0:T(8,128)(2,1)S(1)}, bf16[2,192,128]{2,1,0:T(8,128)(2,1)S(1)}, u32[]{:S(2)}, u32[]{:S(2)}) collective-permute-start(bf16[2,192,128]{2,1,0:T(8,128)(2,1)S(1)} %get-tuple-element.35), channel_id=1, source_target_pairs={{0,2},{2,0},{1,3},{3,1},{4,6},{6,4},{5,7},{7,5},{8,10},{10,8},{9,1... | collective-permute-start | bytes 294920 | tf_op jit(solution)/shard_map/ppermute | solution.py:523
  13.0 0.7 %shard_map.107.own_ref = bf16[7,128,128]{2,1,0:T(8,128)(2,1)S(1)} custom-call(f32[8,3,2,128,128]{4,3,2,1,0:T(8,128)S(1)} %get-tuple-element.28.change_ref, f32[8,2,128,128]{3,2,1,0:T(8,128)S(1)} %get-tuple-element.29.window_ref), custom_call_target="tpu_custom_call" | custom-call | tf_op jit(solution)/shard_map/pallas_call | solution.py:433
  13.7 0.3 collective-permute-start.1
  13.9 0.3 %shard_map.109.inverse_ref = f32[192,128]{1,0:T(8,128)S(1)} custom-call(bf16[392,128]{1,0:T(8,128)(2,1)S(1)} %collective-permute-done.below_ref.above_ref, f32[128,128]{1,0:T(8,128)S(1)} %get-tuple-element.36.power_ref, f32[192,128]{1,0:T(8,128)S(1)} %get-tuple-element.37.weight_ref), custom_call_target="tpu_custom_call" | custom-call | tf_op jit(solution)/shard_map/pallas_call | solution.py:433
  14.3 2.6 %collective-permute-done.2.received_ref = bf16[2,192,128]{2,1,0:T(8,128)(2,1)S(1)} collective-permute-done((bf16[2,192,128]{2,1,0:T(8,128)(2,1)S(1)}, bf16[2,192,128]{2,1,0:T(8,128)(2,1)S(1)}, u32[]{:S(2)}, u32[]{:S(2)}) %collective-permute-start.2) | collective-permute-done | bytes 98336 | tf_op jit(solution)/shard_map/ppermute | solution.py:523
  16.8 0.1 shard_map.110
  16.9 4.0 %collective-permute-start.4 = (bf16[2,192,128]{2,1,0:T(8,128)(2,1)S(1)}, bf16[2,192,128]{2,1,0:T(8,128)(2,1)S(1)}, u32[]{:S(2)}, u32[]{:S(2)}) collective-permute-start(bf16[2,192,128]{2,1,0:T(8,128)(2,1)S(1)} %get-tuple-element.38.refs_0_), channel_id=1, source_target_pairs={{0,12},{4,8},{8,4},{12,0},{1,13},{5,9},{9,5},{13,1},{2,14},{6,10},... | collective-permute-start | bytes 294920 | tf_op jit(solution)/shard_map/ppermute | solution.py:542
  20.9 0.0 collective-permute-start.6
  20.9 0.6 %collective-permute-start.8 = (bf16[2,192,128]{2,1,0:T(8,128)(2,1)S(1)}, bf16[2,192,128]{2,1,0:T(8,128)(2,1)S(1)}, u32[]{:S(2)}, u32[]{:S(2)}) collective-permute-start(bf16[2,192,128]{2,1,0:T(8,128)(2,1)S(1)} %get-tuple-element.38.refs_0_), channel_id=1, source_target_pairs={{0,8},{4,12},{8,0},{12,4},{1,9},{5,13},{9,1},{13,5},{2,10},{6,14},... | collective-permute-start | bytes 294920 | tf_op jit(solution)/shard_map/ppermute | solution.py:542
  21.5 0.0 collective-permute-start.3
  21.5 2.4 %collective-permute-done.4.refs_2_ = bf16[2,192,128]{2,1,0:T(8,128)(2,1)S(1)} collective-permute-done((bf16[2,192,128]{2,1,0:T(8,128)(2,1)S(1)}, bf16[2,192,128]{2,1,0:T(8,128)(2,1)S(1)}, u32[]{:S(2)}, u32[]{:S(2)}) %collective-permute-start.4) | collective-permute-done | bytes 98336 | tf_op jit(solution)/shard_map/ppermute | solution.py:542
  24.0 2.6 %collective-permute-done.6.refs_2_ = bf16[2,192,128]{2,1,0:T(8,128)(2,1)S(1)} collective-permute-done((bf16[2,192,128]{2,1,0:T(8,128)(2,1)S(1)}, bf16[2,192,128]{2,1,0:T(8,128)(2,1)S(1)}, u32[]{:S(2)}, u32[]{:S(2)}) %collective-permute-start.6) | collective-permute-done | bytes 98336 | tf_op jit(solution)/shard_map/ppermute | solution.py:542
  26.6 0.0 collective-permute-done.8.refs_4_
  26.6 0.5 %collective-permute-start.9 = (bf16[2,192,128]{2,1,0:T(8,128)(2,1)S(1)}, bf16[2,192,128]{2,1,0:T(8,128)(2,1)S(1)}, u32[]{:S(2)}, u32[]{:S(2)}) collective-permute-start(bf16[2,192,128]{2,1,0:T(8,128)(2,1)S(1)} %collective-permute-done.8.refs_4_), channel_id=1, source_target_pairs={{0,1},{1,0},{2,3},{3,2},{4,5},{5,4},{6,7},{7,6},{8,9},{9,8},{10,11... | collective-permute-start | bytes 294920 | tf_op jit(solution)/shard_map/ppermute | solution.py:545
  27.1 0.3 %shard_map.108.probe_ref = f32[2,3,1,128,128]{4,3,2,1,0:T(8,128)S(1)} custom-call(f32[2,3,128,128]{3,2,1,0:T(8,128)S(1)} %get-tuple-element.22.probe_ref, bf16[7,128,128]{2,1,0:T(8,128)(2,1)S(1)} %shard_map.107.own_ref, bf16[7,128,128]{2,1,0:T(8,128)(2,1)S(1)} %collective-permute-done.1.received_ref), custom_call_target="tpu_custom_call" | custom-call | tf_op jit(solution)/shard_map/pallas_call | solution.py:433
  27.4 0.4 %shard_map.111.refs_0_ = f32[8,2,192,128]{3,2,1,0:T(8,128)S(1)} custom-call(f32[8,8,8,128]{3,2,1,0:T(8,128)S(1)} %get-tuple-element.30.table_ref, bf16[2,192,128]{2,1,0:T(8,128)(2,1)S(1)} %get-tuple-element.38.refs_0_, bf16[2,192,128]{2,1,0:T(8,128)(2,1)S(1)} %collective-permute-done.3.refs_1_, bf16[2,192,128]{2,1,0:T(8,128)(2,1)S(1)} %collective-permute-done.4.refs_2_, ...), custom_call_target="tpu_custom_call" | custom-call | tf_op jit(solution)/shard_map/pallas_call | solution.py:433
  27.8 0.1 collective-permute-done.7.refs_3_
  27.9 0.4 %shard_map.112.mixed_ref = f32[9,2,192,128]{3,2,1,0:T(8,128)S(1)} custom-call(f32[8,8,8,128]{3,2,1,0:T(8,128)S(1)} %get-tuple-element.30.table_ref, f32[8,2,192,128]{3,2,1,0:T(8,128)S(1)} %shard_map.111.refs_0_, f32[2,192,128]{2,1,0:T(8,128)S(1)} %get-tuple-element.39.refs_1_, bf16[2,192,128]{2,1,0:T(8,128)(2,1)S(1)} %collective-permute-done.6.refs_2_, ...), custom_call_target="tpu_custom_call" | custom-call | tf_op jit(solution)/shard_map/pallas_call | solution.py:433
  28.3 1.0 %shard_map.113 = (f32[2,1,192,128]{3,2,1,0:T(8,128)}, f32[2,3,1,128,128]{4,3,2,1,0:T(8,128)}) custom-call(f32[2,3,1,128,128]{4,3,2,1,0:T(8,128)S(1)} %shard_map.108.probe_ref, f32[8,8,8,128]{3,2,1,0:T(8,128)S(1)} %get-tuple-element.30.table_ref, f32[8,8,128]{2,1,0:T(8,128)S(1)} %get-tuple-element.31.last_ref, f32[8,8,128]{2,1,0:T(8,128)S(1)} %get-tuple-element.32.late_ref, ...), custom_call_target="tpu_custom_call" | custom-call | tf_op jit(solution)/shard_map/pallas_call | solution.py:433
  (6 shorter events, 0.0 us)
Async XLA Ops:
  1.6 5.9 %collective-permute-start = (bf16[392,128]{1,0:T(8,128)(2,1)S(1)}, bf16[392,128]{1,0:T(8,128)(2,1)S(1)}, u32[]{:S(2)}, u32[]{:S(2)}) collective-permute-start(bf16[392,128]{1,0:T(8,128)(2,1)S(1)} %get-tuple-element.24.own_ref), channel_id=1, source_target_pairs={{0,2},{2,0},{1,3},{3,1},{4,6},{6,4},{5,7},{7,5},{8,10},{10,8},{9,1... | collective-permute-start | bytes 301064 | tf_op jit(solution)/shard_map/ppermute | solution.py:465
  11.1 5.7 %collective-permute-start.2 = (bf16[2,192,128]{2,1,0:T(8,128)(2,1)S(1)}, bf16[2,192,128]{2,1,0:T(8,128)(2,1)S(1)}, u32[]{:S(2)}, u32[]{:S(2)}) collective-permute-start(bf16[2,192,128]{2,1,0:T(8,128)(2,1)S(1)} %get-tuple-element.35), channel_id=1, source_target_pairs={{0,2},{2,0},{1,3},{3,1},{4,6},{6,4},{5,7},{7,5},{8,10},{10,8},{9,1... | collective-permute-start | bytes 294920 | tf_op jit(solution)/shard_map/ppermute | solution.py:523
  13.7 13.4 %collective-permute-start.1 = (bf16[7,128,128]{2,1,0:T(8,128)(2,1)S(1)}, bf16[7,128,128]{2,1,0:T(8,128)(2,1)S(1)}, u32[]{:S(2)}, u32[]{:S(2)}) collective-permute-start(bf16[7,128,128]{2,1,0:T(8,128)(2,1)S(1)} %shard_map.107.own_ref), channel_id=1, source_target_pairs={{0,2},{2,0},{1,3},{3,1},{4,6},{6,4},{5,7},{7,5},{8,10},{10,8},{9,1... | collective-permute-start | bytes 688136 | tf_op jit(solution)/shard_map/ppermute | solution.py:561
  16.9 7.1 %collective-permute-start.4 = (bf16[2,192,128]{2,1,0:T(8,128)(2,1)S(1)}, bf16[2,192,128]{2,1,0:T(8,128)(2,1)S(1)}, u32[]{:S(2)}, u32[]{:S(2)}) collective-permute-start(bf16[2,192,128]{2,1,0:T(8,128)(2,1)S(1)} %get-tuple-element.38.refs_0_), channel_id=1, source_target_pairs={{0,12},{4,8},{8,4},{12,0},{1,13},{5,9},{9,5},{13,1},{2,14},{6,10},... | collective-permute-start | bytes 294920 | tf_op jit(solution)/shard_map/ppermute | solution.py:542
  20.9 5.7 %collective-permute-start.6 = (bf16[2,192,128]{2,1,0:T(8,128)(2,1)S(1)}, bf16[2,192,128]{2,1,0:T(8,128)(2,1)S(1)}, u32[]{:S(2)}, u32[]{:S(2)}) collective-permute-start(bf16[2,192,128]{2,1,0:T(8,128)(2,1)S(1)} %get-tuple-element.38.refs_0_), channel_id=1, source_target_pairs={{0,4},{4,0},{8,12},{12,8},{1,5},{5,1},{9,13},{13,9},{2,6},{6,2},{1... | collective-permute-start | bytes 294920 | tf_op jit(solution)/shard_map/ppermute | solution.py:542
  20.9 5.7 %collective-permute-start.8 = (bf16[2,192,128]{2,1,0:T(8,128)(2,1)S(1)}, bf16[2,192,128]{2,1,0:T(8,128)(2,1)S(1)}, u32[]{:S(2)}, u32[]{:S(2)}) collective-permute-start(bf16[2,192,128]{2,1,0:T(8,128)(2,1)S(1)} %get-tuple-element.38.refs_0_), channel_id=1, source_target_pairs={{0,8},{4,12},{8,0},{12,4},{1,9},{5,13},{9,1},{13,5},{2,10},{6,14},... | collective-permute-start | bytes 294920 | tf_op jit(solution)/shard_map/ppermute | solution.py:542
  21.5 5.8 %collective-permute-start.3 = (bf16[2,192,128]{2,1,0:T(8,128)(2,1)S(1)}, bf16[2,192,128]{2,1,0:T(8,128)(2,1)S(1)}, u32[]{:S(2)}, u32[]{:S(2)}) collective-permute-start(bf16[2,192,128]{2,1,0:T(8,128)(2,1)S(1)} %get-tuple-element.38.refs_0_), channel_id=1, source_target_pairs={{0,1},{1,0},{2,3},{3,2},{4,5},{5,4},{6,7},{7,6},{8,9},{9,8},{10,11... | collective-permute-start | bytes 294920 | tf_op jit(solution)/shard_map/ppermute | solution.py:545
  24.0 3.4 %collective-permute-start.5 = (bf16[2,192,128]{2,1,0:T(8,128)(2,1)S(1)}, bf16[2,192,128]{2,1,0:T(8,128)(2,1)S(1)}, u32[]{:S(2)}, u32[]{:S(2)}) collective-permute-start(bf16[2,192,128]{2,1,0:T(8,128)(2,1)S(1)} %collective-permute-done.4.refs_2_), channel_id=1, source_target_pairs={{0,1},{1,0},{2,3},{3,2},{4,5},{5,4},{6,7},{7,6},{8,9},{9,8},{10,11... | collective-permute-start | bytes 294920 | tf_op jit(solution)/shard_map/ppermute | solution.py:545
  26.5 1.3 %collective-permute-start.7 = (bf16[2,192,128]{2,1,0:T(8,128)(2,1)S(1)}, bf16[2,192,128]{2,1,0:T(8,128)(2,1)S(1)}, u32[]{:S(2)}, u32[]{:S(2)}) collective-permute-start(bf16[2,192,128]{2,1,0:T(8,128)(2,1)S(1)} %collective-permute-done.6.refs_2_), channel_id=1, source_target_pairs={{0,1},{1,0},{2,3},{3,2},{4,5},{5,4},{6,7},{7,6},{8,9},{9,8},{10,11... | collective-permute-start | bytes 294920 | tf_op jit(solution)/shard_map/ppermute | solution.py:545
  26.6 1.7 %collective-permute-start.9 = (bf16[2,192,128]{2,1,0:T(8,128)(2,1)S(1)}, bf16[2,192,128]{2,1,0:T(8,128)(2,1)S(1)}, u32[]{:S(2)}, u32[]{:S(2)}) collective-permute-start(bf16[2,192,128]{2,1,0:T(8,128)(2,1)S(1)} %collective-permute-done.8.refs_4_), channel_id=1, source_target_pairs={{0,1},{1,0},{2,3},{3,2},{4,5},{5,4},{6,7},{7,6},{8,9},{9,8},{10,11... | collective-permute-start | bytes 294920 | tf_op jit(solution)/shard_map/ppermute | solution.py:545

commit v6 on v5

--- a/solution.py
+++ b/solution.py
@@ -57,6 +57,9 @@
     ]
     for copy in copies:
         copy.start()
+    for part in range(2):
+        copies[1 + part].wait()
+        message_ref[part * cols : (part + 1) * cols] = object_ref[part].astype(jnp.bfloat16)
     copies[0].wait()
     lane = lax.broadcasted_iota(jnp.int32, (PAD_ROWS, rows), 1)
     line = jnp.zeros((PAD_ROWS, rows), jnp.float32)
@@ -65,9 +68,6 @@
             value = offsets_ref[k, q].astype(jnp.float32)
             line = jnp.where(lane == k * positions + q, value, line)
     message_ref[2 * cols :] = line.astype(jnp.bfloat16)
-    for part in range(2):
-        copies[1 + part].wait()
-        message_ref[part * cols : (part + 1) * cols] = object_ref[part].astype(jnp.bfloat16)
 
 
 def turn_kernel(
@@ -196,7 +196,7 @@
     moduli_ref,
     forward_ref,
     backward_ref,
-    upper_ref,
+    sums_ref,
     lower_ref,
     change_ref,
     window_ref,
@@ -290,14 +290,15 @@
                 sum_real += probe_real * change_real + probe_imag * change_imag
                 sum_imag += probe_real * change_imag - probe_imag * change_real
             for part, value in enumerate((sum_real, sum_imag)):
-                for side, moved in enumerate(spread(value, row)):
-                    total[part, side, here] += moved
+                sums_ref[q, part] = value
+                _, right = spread(value, row)
+                total[part, here] += right
 
     stages = [[enter], [first_half], [project], [second_half, leave]]
     blocks = positions // group
     held = [None] * blocks
     for tick in range(blocks + len(stages) - 1):
-        for depth in range(len(stages)):
+        for depth in (1, 0, 2, 3):
             block = tick - depth
             if not 0 <= block < blocks:
                 continue
@@ -305,8 +306,18 @@
                 held[block] = stage(block) if stage is enter else stage(block, held[block])
 
     for part in range(2):
-        upper_ref[part] = total[part, 0]
-        lower_ref[part] = total[part, 1].astype(jnp.bfloat16)
+        lower_ref[part] = total[part].astype(jnp.bfloat16)
+
+
+def upper_kernel(offsets_ref, sums_ref, upper_ref):
+    extent = sums_ref.shape[-1]
+    upper_ref[...] = jnp.zeros_like(upper_ref)
+    for q in range(sums_ref.shape[0]):
+        row, col = corner(offsets_ref, q)
+        here = pl.ds(col, extent)
+        for part in range(2):
+            left, _ = spread(sums_ref[q, part], row)
+            upper_ref[part, here] += left
 
 
 def share_kernel(change_ref, window_ref, share_ref):
@@ -503,19 +514,19 @@
         ),
         limit=8,
     )
-    upper, lower, change, window = call(
+    sums, lower, change, window = call(
         functools.partial(wave_kernel, tiles=tiles, group=2),
         (offsets, message, below, turned, moduli, forward, backward),
         "svvvvvv",
         (
-            shape((2, cols, rows), f32),
+            shape((positions, 2, extent, extent), f32),
             shape((2, cols, rows), bf16),
             shape((positions, modes, 2, extent, extent), f32),
             shape((positions, 2, extent, extent), f32),
         ),
         (
             pltpu.VMEM((2, 2, cols, LANES), f32),
-            pltpu.VMEM((2, 2, cols, LANES), f32),
+            pltpu.VMEM((2, cols, rows), f32),
         ),
         limit=24,
     )
@@ -531,6 +542,7 @@
         (pltpu.VMEM((cols, rows), f32),),
     )
     share = call(share_kernel, (change, window), "vv", shape((2 * modes + 1, extent, extent), bf16))
+    upper = call(upper_kernel, (offsets, sums), "sv", shape((2, cols, rows), f32))
     object_new, sent = call(
         object_kernel,
         (object_here, upper, received, inverse),

time: 29.4 us -> 29.3 us (level)
  waiting for transfers between devices: 8.74 us -> 7.85 us
  Pallas kernels: 9.45 us -> 10.3 us
    ppermute x1, waiting for transfers between devices: 2.56 us -> 1.66 us  [body(): received = lax.ppermute(lower, 'tile', swap_pairs(2, 1))]
    pallas_call x10 -> x11, Pallas kernels: 9.45 us -> 10.3 us  [call(): pl.pallas_call(kernel, out_shape=outputs, in_specs=[pl.BlockSpec(memory_s...]
  transfers between devices with their start and end apart: 10 -> 10, of which waited for: 5 -> 5; matrix products, arithmetic and copies ran while one was open for 0% -> 0% of each run, Pallas kernels for 13% -> 16%
where the time goes in v6:
time: 29.3 us; the launch traced here: 29.1 us
  Pallas kernels  10.3 us (35%)
  starting transfers between devices  10.3 us (35%)
  waiting for transfers between devices  7.85 us (27%)
  between operations  0.72 us (2%)
    pallas_call x11, Pallas kernels, call(): pl.pallas_call(kernel, out_shape=outputs, in_specs=[pl.BlockSpec(memory_s...  10.3 us
    ppermute x3, waiting for transfers between devices, body(): pieces[dz, 0] = lax.ppermute(sent, 'energy', swap_pairs(zs, dz))  5.02 us
    ppermute x3, starting transfers between devices, body(): pieces[dz, 0] = lax.ppermute(sent, 'energy', swap_pairs(zs, dz))  4.62 us
    ppermute x1, starting transfers between devices, body(): below = above = lax.ppermute(message, 'tile', swap_pairs(2, 1))  3.03 us
    ppermute x1, starting transfers between devices, body(): received = lax.ppermute(lower, 'tile', swap_pairs(2, 1))  1.89 us
    ppermute x1, waiting for transfers between devices, body(): received = lax.ppermute(lower, 'tile', swap_pairs(2, 1))  1.66 us
    ppermute x1, waiting for transfers between devices, body(): below = above = lax.ppermute(message, 'tile', swap_pairs(2, 1))  1.08 us
  transfers between devices with their start and end apart: 10, of which 5 were waited for; matrix products, arithmetic and copies ran while one was open for 0% of the time, Pallas kernels for 16%

profile of v6, /device:TPU:0, one launch (start us, length us, event | category | flops | bytes accessed | tf_op | source)
XLA Modules:
  0.0 29.1 jit_solution(7883586825484932804)
XLA Ops:
  0.6 1.0 %shard_map.105 = (bf16[392,128]{1,0:T(8,128)(2,1)S(1)}, f32[2,192,128]{2,1,0:T(8,128)S(1)}) custom-call(s32[2,8]{1,0:T(2,128)} %bitcast.4, f32[2,1,192,128]{3,2,1,0:T(8,128)} %bitcast.3), custom_call_target="tpu_custom_call" | custom-call | tf_op jit(solution)/shard_map/pallas_call | solution.py:444
  1.6 3.0 %collective-permute-start = (bf16[392,128]{1,0:T(8,128)(2,1)S(1)}, bf16[392,128]{1,0:T(8,128)(2,1)S(1)}, u32[]{:S(2)}, u32[]{:S(2)}) collective-permute-start(bf16[392,128]{1,0:T(8,128)(2,1)S(1)} %get-tuple-element.24.own_ref), channel_id=1, source_target_pairs={{0,2},{2,0},{1,3},{3,1},{4,6},{6,4},{5,7},{7,5},{8,10},{10,8},{9,1... | collective-permute-start | bytes 301064 | tf_op jit(solution)/shard_map/ppermute | solution.py:476
  4.7 1.8 %shard_map.104 = (s32[2,8]{1,0:T(2,128)S(1)}, bf16[256,256]{1,0:T(8,128)(2,1)S(1)}, bf16[256,256]{1,0:T(8,128)(2,1)S(1)}, f32[2,3,128,128]{3,2,1,0:T(8,128)S(1)}...) custom-call(s32[2,8]{1,0:T(2,128)} %bitcast.5, ...), custom_call_target="tpu_custom_call" | custom-call | tf_op jit(solution)/shard_map/pallas_call | solution.py:444
  6.4 1.1 %collective-permute-done.below_ref.above_ref = bf16[392,128]{1,0:T(8,128)(2,1)S(1)} collective-permute-done((bf16[392,128]{1,0:T(8,128)(2,1)S(1)}, bf16[392,128]{1,0:T(8,128)(2,1)S(1)}, u32[]{:S(2)}, u32[]{:S(2)}) %collective-permute-start) | collective-permute-done | bytes 100384 | tf_op jit(solution)/shard_map/ppermute | solution.py:476
  7.5 3.5 %shard_map.106 = (f32[8,2,128,128]{3,2,1,0:T(8,128)S(1)}, bf16[2,192,128]{2,1,0:T(8,128)(2,1)S(1)}, f32[8,3,2,128,128]{4,3,2,1,0:T(8,128)S(1)}, f32[8,2,128,128]{3,2,1,0:T(8,128)S(1)}) custom-call(s32[2,8]{1,0:T(2,128)S(1)} %get-tuple-element.23.offsets_ref, bf16[392,128]{1,0:T(8,128)(2,1)S(1)} %get-tuple-element.24.own_ref, ...), custom_call_target="tpu_custom_call" | custom-call | tf_op jit(solution)/shard_map/pallas_call | solution.py:444
  11.0 1.9 %collective-permute-start.2 = (bf16[2,192,128]{2,1,0:T(8,128)(2,1)S(1)}, bf16[2,192,128]{2,1,0:T(8,128)(2,1)S(1)}, u32[]{:S(2)}, u32[]{:S(2)}) collective-permute-start(bf16[2,192,128]{2,1,0:T(8,128)(2,1)S(1)} %get-tuple-element.35), channel_id=1, source_target_pairs={{0,2},{2,0},{1,3},{3,1},{4,6},{6,4},{5,7},{7,5},{8,10},{10,8},{9,1... | collective-permute-start | bytes 294920 | tf_op jit(solution)/shard_map/ppermute | solution.py:534
  12.9 0.7 %shard_map.107.own_ref = bf16[7,128,128]{2,1,0:T(8,128)(2,1)S(1)} custom-call(f32[8,3,2,128,128]{4,3,2,1,0:T(8,128)S(1)} %get-tuple-element.28.change_ref, f32[8,2,128,128]{3,2,1,0:T(8,128)S(1)} %get-tuple-element.29.window_ref), custom_call_target="tpu_custom_call" | custom-call | tf_op jit(solution)/shard_map/pallas_call | solution.py:444
  13.6 0.3 collective-permute-start.1
  13.9 0.9 %shard_map.109.upper_ref = f32[2,192,128]{2,1,0:T(8,128)S(1)} custom-call(s32[2,8]{1,0:T(2,128)S(1)} %get-tuple-element.23.offsets_ref, f32[8,2,128,128]{3,2,1,0:T(8,128)S(1)} %get-tuple-element.34.sums_ref), custom_call_target="tpu_custom_call" | custom-call | tf_op jit(solution)/shard_map/pallas_call | solution.py:444
  14.8 0.3 %shard_map.110.inverse_ref = f32[192,128]{1,0:T(8,128)S(1)} custom-call(bf16[392,128]{1,0:T(8,128)(2,1)S(1)} %collective-permute-done.below_ref.above_ref, f32[128,128]{1,0:T(8,128)S(1)} %get-tuple-element.36.power_ref, f32[192,128]{1,0:T(8,128)S(1)} %get-tuple-element.37.weight_ref), custom_call_target="tpu_custom_call" | custom-call | tf_op jit(solution)/shard_map/pallas_call | solution.py:444
  15.1 1.7 %collective-permute-done.2.received_ref = bf16[2,192,128]{2,1,0:T(8,128)(2,1)S(1)} collective-permute-done((bf16[2,192,128]{2,1,0:T(8,128)(2,1)S(1)}, bf16[2,192,128]{2,1,0:T(8,128)(2,1)S(1)}, u32[]{:S(2)}, u32[]{:S(2)}) %collective-permute-start.2) | collective-permute-done | bytes 98336 | tf_op jit(solution)/shard_map/ppermute | solution.py:534
  16.8 0.1 shard_map.111
  16.8 4.0 %collective-permute-start.4 = (bf16[2,192,128]{2,1,0:T(8,128)(2,1)S(1)}, bf16[2,192,128]{2,1,0:T(8,128)(2,1)S(1)}, u32[]{:S(2)}, u32[]{:S(2)}) collective-permute-start(bf16[2,192,128]{2,1,0:T(8,128)(2,1)S(1)} %get-tuple-element.38.refs_0_), channel_id=1, source_target_pairs={{0,12},{4,8},{8,4},{12,0},{1,13},{5,9},{9,5},{13,1},{2,14},{6,10},... | collective-permute-start | bytes 294920 | tf_op jit(solution)/shard_map/ppermute | solution.py:554
  20.8 0.6 %collective-permute-start.8 = (bf16[2,192,128]{2,1,0:T(8,128)(2,1)S(1)}, bf16[2,192,128]{2,1,0:T(8,128)(2,1)S(1)}, u32[]{:S(2)}, u32[]{:S(2)}) collective-permute-start(bf16[2,192,128]{2,1,0:T(8,128)(2,1)S(1)} %get-tuple-element.38.refs_0_), channel_id=1, source_target_pairs={{0,8},{4,12},{8,0},{12,4},{1,9},{5,13},{9,1},{13,5},{2,10},{6,14},... | collective-permute-start | bytes 294920 | tf_op jit(solution)/shard_map/ppermute | solution.py:554
  21.4 2.4 %collective-permute-done.4.refs_2_ = bf16[2,192,128]{2,1,0:T(8,128)(2,1)S(1)} collective-permute-done((bf16[2,192,128]{2,1,0:T(8,128)(2,1)S(1)}, bf16[2,192,128]{2,1,0:T(8,128)(2,1)S(1)}, u32[]{:S(2)}, u32[]{:S(2)}) %collective-permute-start.4) | collective-permute-done | bytes 98336 | tf_op jit(solution)/shard_map/ppermute | solution.py:554
  23.9 0.0 collective-permute-start.5
  23.9 2.6 %collective-permute-done.6.refs_2_ = bf16[2,192,128]{2,1,0:T(8,128)(2,1)S(1)} collective-permute-done((bf16[2,192,128]{2,1,0:T(8,128)(2,1)S(1)}, bf16[2,192,128]{2,1,0:T(8,128)(2,1)S(1)}, u32[]{:S(2)}, u32[]{:S(2)}) %collective-permute-start.6) | collective-permute-done | bytes 98336 | tf_op jit(solution)/shard_map/ppermute | solution.py:554
  26.5 0.0 collective-permute-start.7
  26.5 0.5 %collective-permute-start.9 = (bf16[2,192,128]{2,1,0:T(8,128)(2,1)S(1)}, bf16[2,192,128]{2,1,0:T(8,128)(2,1)S(1)}, u32[]{:S(2)}, u32[]{:S(2)}) collective-permute-start(bf16[2,192,128]{2,1,0:T(8,128)(2,1)S(1)} %collective-permute-done.8.refs_4_), channel_id=1, source_target_pairs={{0,1},{1,0},{2,3},{3,2},{4,5},{5,4},{6,7},{7,6},{8,9},{9,8},{10,11... | collective-permute-start | bytes 294920 | tf_op jit(solution)/shard_map/ppermute | solution.py:557
  27.0 0.3 %shard_map.108.probe_ref = f32[2,3,1,128,128]{4,3,2,1,0:T(8,128)S(1)} custom-call(f32[2,3,128,128]{3,2,1,0:T(8,128)S(1)} %get-tuple-element.22.probe_ref, bf16[7,128,128]{2,1,0:T(8,128)(2,1)S(1)} %shard_map.107.own_ref, bf16[7,128,128]{2,1,0:T(8,128)(2,1)S(1)} %collective-permute-done.1.received_ref), custom_call_target="tpu_custom_call" | custom-call | tf_op jit(solution)/shard_map/pallas_call | solution.py:444
  27.3 0.4 %shard_map.112.refs_0_ = f32[8,2,192,128]{3,2,1,0:T(8,128)S(1)} custom-call(f32[8,8,8,128]{3,2,1,0:T(8,128)S(1)} %get-tuple-element.30.table_ref, bf16[2,192,128]{2,1,0:T(8,128)(2,1)S(1)} %get-tuple-element.38.refs_0_, bf16[2,192,128]{2,1,0:T(8,128)(2,1)S(1)} %collective-permute-done.3.refs_1_, bf16[2,192,128]{2,1,0:T(8,128)(2,1)S(1)} %collective-permute-done.4.refs_2_, ...), custom_call_target="tpu_custom_call" | custom-call | tf_op jit(solution)/shard_map/pallas_call | solution.py:444
  27.7 0.1 collective-permute-done.7.refs_3_
  27.8 0.4 %shard_map.113.mixed_ref = f32[9,2,192,128]{3,2,1,0:T(8,128)S(1)} custom-call(f32[8,8,8,128]{3,2,1,0:T(8,128)S(1)} %get-tuple-element.30.table_ref, f32[8,2,192,128]{3,2,1,0:T(8,128)S(1)} %shard_map.112.refs_0_, f32[2,192,128]{2,1,0:T(8,128)S(1)} %get-tuple-element.39.refs_1_, bf16[2,192,128]{2,1,0:T(8,128)(2,1)S(1)} %collective-permute-done.6.refs_2_, ...), custom_call_target="tpu_custom_call" | custom-call | tf_op jit(solution)/shard_map/pallas_call | solution.py:444
  28.2 1.0 %shard_map.114 = (f32[2,1,192,128]{3,2,1,0:T(8,128)}, f32[2,3,1,128,128]{4,3,2,1,0:T(8,128)}) custom-call(f32[2,3,1,128,128]{4,3,2,1,0:T(8,128)S(1)} %shard_map.108.probe_ref, f32[8,8,8,128]{3,2,1,0:T(8,128)S(1)} %get-tuple-element.30.table_ref, f32[8,8,128]{2,1,0:T(8,128)S(1)} %get-tuple-element.31.last_ref, f32[8,8,128]{2,1,0:T(8,128)S(1)} %get-tuple-element.32.late_ref, ...), custom_call_target="tpu_custom_call" | custom-call | tf_op jit(solution)/shard_map/pallas_call | solution.py:444
  (7 shorter events, 0.0 us)
Async XLA Ops:
  1.6 5.9 %collective-permute-start = (bf16[392,128]{1,0:T(8,128)(2,1)S(1)}, bf16[392,128]{1,0:T(8,128)(2,1)S(1)}, u32[]{:S(2)}, u32[]{:S(2)}) collective-permute-start(bf16[392,128]{1,0:T(8,128)(2,1)S(1)} %get-tuple-element.24.own_ref), channel_id=1, source_target_pairs={{0,2},{2,0},{1,3},{3,1},{4,6},{6,4},{5,7},{7,5},{8,10},{10,8},{9,1... | collective-permute-start | bytes 301064 | tf_op jit(solution)/shard_map/ppermute | solution.py:476
  11.0 5.7 %collective-permute-start.2 = (bf16[2,192,128]{2,1,0:T(8,128)(2,1)S(1)}, bf16[2,192,128]{2,1,0:T(8,128)(2,1)S(1)}, u32[]{:S(2)}, u32[]{:S(2)}) collective-permute-start(bf16[2,192,128]{2,1,0:T(8,128)(2,1)S(1)} %get-tuple-element.35), channel_id=1, source_target_pairs={{0,2},{2,0},{1,3},{3,1},{4,6},{6,4},{5,7},{7,5},{8,10},{10,8},{9,1... | collective-permute-start | bytes 294920 | tf_op jit(solution)/shard_map/ppermute | solution.py:534
  13.6 13.4 %collective-permute-start.1 = (bf16[7,128,128]{2,1,0:T(8,128)(2,1)S(1)}, bf16[7,128,128]{2,1,0:T(8,128)(2,1)S(1)}, u32[]{:S(2)}, u32[]{:S(2)}) collective-permute-start(bf16[7,128,128]{2,1,0:T(8,128)(2,1)S(1)} %shard_map.107.own_ref), channel_id=1, source_target_pairs={{0,2},{2,0},{1,3},{3,1},{4,6},{6,4},{5,7},{7,5},{8,10},{10,8},{9,1... | collective-permute-start | bytes 688136 | tf_op jit(solution)/shard_map/ppermute | solution.py:573
  16.8 7.1 %collective-permute-start.4 = (bf16[2,192,128]{2,1,0:T(8,128)(2,1)S(1)}, bf16[2,192,128]{2,1,0:T(8,128)(2,1)S(1)}, u32[]{:S(2)}, u32[]{:S(2)}) collective-permute-start(bf16[2,192,128]{2,1,0:T(8,128)(2,1)S(1)} %get-tuple-element.38.refs_0_), channel_id=1, source_target_pairs={{0,12},{4,8},{8,4},{12,0},{1,13},{5,9},{9,5},{13,1},{2,14},{6,10},... | collective-permute-start | bytes 294920 | tf_op jit(solution)/shard_map/ppermute | solution.py:554
  20.8 5.7 %collective-permute-start.6 = (bf16[2,192,128]{2,1,0:T(8,128)(2,1)S(1)}, bf16[2,192,128]{2,1,0:T(8,128)(2,1)S(1)}, u32[]{:S(2)}, u32[]{:S(2)}) collective-permute-start(bf16[2,192,128]{2,1,0:T(8,128)(2,1)S(1)} %get-tuple-element.38.refs_0_), channel_id=1, source_target_pairs={{0,4},{4,0},{8,12},{12,8},{1,5},{5,1},{9,13},{13,9},{2,6},{6,2},{1... | collective-permute-start | bytes 294920 | tf_op jit(solution)/shard_map/ppermute | solution.py:554
  20.8 5.7 %collective-permute-start.8 = (bf16[2,192,128]{2,1,0:T(8,128)(2,1)S(1)}, bf16[2,192,128]{2,1,0:T(8,128)(2,1)S(1)}, u32[]{:S(2)}, u32[]{:S(2)}) collective-permute-start(bf16[2,192,128]{2,1,0:T(8,128)(2,1)S(1)} %get-tuple-element.38.refs_0_), channel_id=1, source_target_pairs={{0,8},{4,12},{8,0},{12,4},{1,9},{5,13},{9,1},{13,5},{2,10},{6,14},... | collective-permute-start | bytes 294920 | tf_op jit(solution)/shard_map/ppermute | solution.py:554
  21.4 5.8 %collective-permute-start.3 = (bf16[2,192,128]{2,1,0:T(8,128)(2,1)S(1)}, bf16[2,192,128]{2,1,0:T(8,128)(2,1)S(1)}, u32[]{:S(2)}, u32[]{:S(2)}) collective-permute-start(bf16[2,192,128]{2,1,0:T(8,128)(2,1)S(1)} %get-tuple-element.38.refs_0_), channel_id=1, source_target_pairs={{0,1},{1,0},{2,3},{3,2},{4,5},{5,4},{6,7},{7,6},{8,9},{9,8},{10,11... | collective-permute-start | bytes 294920 | tf_op jit(solution)/shard_map/ppermute | solution.py:557
  23.9 3.4 %collective-permute-start.5 = (bf16[2,192,128]{2,1,0:T(8,128)(2,1)S(1)}, bf16[2,192,128]{2,1,0:T(8,128)(2,1)S(1)}, u32[]{:S(2)}, u32[]{:S(2)}) collective-permute-start(bf16[2,192,128]{2,1,0:T(8,128)(2,1)S(1)} %collective-permute-done.4.refs_2_), channel_id=1, source_target_pairs={{0,1},{1,0},{2,3},{3,2},{4,5},{5,4},{6,7},{7,6},{8,9},{9,8},{10,11... | collective-permute-start | bytes 294920 | tf_op jit(solution)/shard_map/ppermute | solution.py:557
  26.5 1.3 %collective-permute-start.7 = (bf16[2,192,128]{2,1,0:T(8,128)(2,1)S(1)}, bf16[2,192,128]{2,1,0:T(8,128)(2,1)S(1)}, u32[]{:S(2)}, u32[]{:S(2)}) collective-permute-start(bf16[2,192,128]{2,1,0:T(8,128)(2,1)S(1)} %collective-permute-done.6.refs_2_), channel_id=1, source_target_pairs={{0,1},{1,0},{2,3},{3,2},{4,5},{5,4},{6,7},{7,6},{8,9},{9,8},{10,11... | collective-permute-start | bytes 294920 | tf_op jit(solution)/shard_map/ppermute | solution.py:557
  26.5 1.7 %collective-permute-start.9 = (bf16[2,192,128]{2,1,0:T(8,128)(2,1)S(1)}, bf16[2,192,128]{2,1,0:T(8,128)(2,1)S(1)}, u32[]{:S(2)}, u32[]{:S(2)}) collective-permute-start(bf16[2,192,128]{2,1,0:T(8,128)(2,1)S(1)} %collective-permute-done.8.refs_4_), channel_id=1, source_target_pairs={{0,1},{1,0},{2,3},{3,2},{4,5},{5,4},{6,7},{7,6},{8,9},{9,8},{10,11... | collective-permute-start | bytes 294920 | tf_op jit(solution)/shard_map/ppermute | solution.py:557
